TPU v7x, 32 devices: a whole 2x2x4 slice. The times are simulated.
32 devices in a mesh: dp: 16 (over z, y, x), band: 2 (over core).
Axes of the slice: x: 2, y: 2, z: 4, core: 2. Of those that a mesh axis runs over, the one named last changes fastest.
Arguments:
- inputs: float32 [16, 2048, 768], P('dp', 'band'), may hold values from -6 to 6
- segment_ids: int32 [16, 2048], P('dp', 'band'), may hold values from 0 to 15, as said below
- cotangent: float32 [16, 2048, 768], P('dp', 'band'), may hold values from -6 to 6
- first_gain: float32 [768], replicated, may hold values from 0.5 to 1.5
- first_bias: float32 [768], replicated, may hold values from -4 to 4
- w_qkv: bfloat16 [768, 2304], replicated, may hold values from -0.21875 to 0.21875
- query_bias: float32 [768], replicated, may hold values from -4 to 4
- value_bias: float32 [768], replicated, may hold values from -4 to 4
- w_proj: bfloat16 [768, 768], replicated, may hold values from -0.875 to 0.875
- proj_bias: float32 [768], replicated, may hold values from -4 to 4
- second_gain: float32 [768], replicated, may hold values from 0.5 to 1.5
- second_bias: float32 [768], replicated, may hold values from -4 to 4
- w_up: bfloat16 [768, 3072], replicated, may hold values from -0.21875 to 0.21875
- up_bias: float32 [3072], replicated, may hold values from -4 to 4
- w_down: bfloat16 [3072, 768], replicated, may hold values from -0.109375 to 0.109375
- down_bias: float32 [768], replicated, may hold values from -4 to 4
Outputs:
- output: float32 [16, 2048, 768], P('dp', 'band')
- input_grad: float32 [16, 2048, 768], P('dp', 'band')
- first_gain_grad: float32 [768], P('dp')
- first_bias_grad: float32 [768], P('dp')
- qkv_grad: float32 [768, 2304], P('dp', 'band')
- query_bias_grad: float32 [768], P('dp')
- value_bias_grad: float32 [768], P('dp')
- proj_grad: float32 [768, 768], P('dp', 'band')
- proj_bias_grad: float32 [768], P('dp')
- second_gain_grad: float32 [768], P('dp')
- second_bias_grad: float32 [768], P('dp')
- up_grad: float32 [768, 3072], P('dp', 'band')
- up_bias_grad: float32 [3072], P('dp')
- down_grad: float32 [3072, 768], P('dp', 'band')
- down_bias_grad: float32 [768], P('dp')
Inputs may be any that keep to these rules, and one draw needn't show every extreme that they name: `segment_ids`: in every sequence the ids start at 0, never fall, and rise by one where a new tile begins; every sequence has the same number of tiles; positions 512 to 1535 of every sequence lie in one tile.
All inputs are finite; a program needn't handle non-finite values.
Results may differ from a plain program's by a relative error of at most 0.012.
Values may be sent and summed in bfloat16 or wider, within the bound.
A program may use at most 384 MiB of HBM per device.

v0:
```python
import functools

import jax
import jax.numpy as jnp
from jax import lax
from jax.experimental import pallas as pl
from jax.experimental.pallas import tpu as pltpu
from jax.sharding import PartitionSpec as P

EPS = 1e-05
HEADS = 12
HEAD_DIM = 64
NEG_LARGE = -1e30
PAIRS = HEADS // 2
CHUNK = 256
MIB = 1 << 20
f32, bf16 = jnp.float32, jnp.bfloat16
NN = (((1,), (0,)), ((), ()))
NT = (((1,), (1,)), ((), ()))


def mm(a, b, dims=NN):
    return lax.dot_general(a, b, dims, preferred_element_type=f32)


def low_lanes(rows):
    return lax.broadcasted_iota(jnp.int32, (rows, 128), 1) < HEAD_DIM


def side_lanes(rows):
    return lax.broadcasted_iota(jnp.int32, (rows, 128), 1) & (HEAD_DIM - 1)


def split3(x):
    high = x.astype(bf16).astype(f32)
    middle = (x - high).astype(bf16).astype(f32)
    return high, middle, x - high - middle


def place(side, parts, base):
    for t, part in enumerate(parts):
        base = jnp.where(side == 16 + t, part, base)
    return base


def fill_pairs(src, dst, rows, low, extra):
    for p in range(PAIRS):
        pair = src[:, p * 128 : (p + 1) * 128]
        dst[2 * p, rows, :] = jnp.where(low, pair, extra)
        dst[2 * p + 1, rows, :] = jnp.where(low, extra, pair)


def fill_keys(band, i, k_own, k_far, v_own, v_far, seg_own, seg_far, kaug, vaug, value_extra):
    local = kaug.shape[1] // 2
    low, side = low_lanes(CHUNK), side_lanes(CHUNK)
    for k, v, seg, first in ((k_own, v_own, seg_own, band), (k_far, v_far, seg_far, 1 - band)):
        rows = pl.ds(pl.multiple_of(first * local + i * CHUNK, CHUNK), CHUNK)
        extra = jnp.where(side < 16, jnp.where(side == seg[...], 0.0, NEG_LARGE), jnp.where(side < 19, -1.0, 0.0))
        fill_pairs(k, kaug, rows, low, extra.astype(bf16))
        fill_pairs(v, vaug, rows, low, value_extra)


def attend_fwd_kernel(fills, BQ, BK, start_ref, count_ref, band_ref, q_ref, qseg_ref, k_own, k_far, v_own, v_far,
                      seg_own, seg_far, o_ref, lse_ref, kaug, vaug, qm, s_all, mx, acc):
    i = pl.program_id(0)

    @pl.when(i < fills)
    def _():
        fill_keys(band_ref[0], i, k_own, k_far, v_own, v_far, seg_own, seg_far, kaug, vaug, jnp.ones((CHUNK, 128), bf16))

    @pl.when(i >= fills)
    def _():
        low, side = low_lanes(BQ), side_lanes(BQ)
        own = (side == qseg_ref[...]).astype(f32).astype(bf16)
        for p in range(PAIRS):
            pair = q_ref[:, p * 128 : (p + 1) * 128]
            qm[2 * p] = jnp.where(low, pair, own)
            qm[2 * p + 1] = jnp.where(low, own, pair)
        mx[...] = jnp.full(mx.shape, -3e38, f32)
        acc[...] = jnp.zeros(acc.shape, f32)
        start = start_ref[i - fills]
        count = count_ref[i - fills]

        def first(j, c):
            at = pl.multiple_of(start + j * BK, 128)
            out = pl.ds(pl.multiple_of(j * BK, BK), BK)
            for h in range(HEADS):
                s = mm(qm[h], kaug[h, pl.ds(at, BK), :], NT)
                s_all[h, :, out] = s
                m = mx[h]
                for t in range(BK // 128):
                    m = jnp.maximum(m, s[:, t * 128 : (t + 1) * 128])
                mx[h] = m
            return c

        lax.fori_loop(0, count, first, 0)
        for h in range(HEADS):
            mx[h] = jnp.broadcast_to(jnp.max(mx[h], axis=1, keepdims=True), (BQ, 128))

        def second(j, c):
            at = pl.multiple_of(start + j * BK, 128)
            src = pl.ds(pl.multiple_of(j * BK, BK), BK)
            for h in range(HEADS):
                p = jnp.exp(s_all[h, :, src] - jnp.concatenate([mx[h]] * (BK // 128), axis=1)).astype(bf16)
                acc[h] += mm(p, vaug[h, pl.ds(at, BK), :])
            return c

        lax.fori_loop(0, count, second, 0)
        lane = lax.broadcasted_iota(jnp.int32, (BQ, 128), 1)
        lse = jnp.zeros((BQ, 128), f32)
        for p in range(PAIRS):
            even, odd = acc[2 * p], acc[2 * p + 1]
            swapped = pltpu.roll(even, HEAD_DIM, 1)
            total = jnp.where(low, swapped, pltpu.roll(odd, HEAD_DIM, 1))
            o_ref[:, p * 128 : (p + 1) * 128] = (jnp.where(low, even, odd) / total).astype(bf16)
            lse = jnp.where(lane == 2 * p, mx[2 * p] + jnp.log(swapped), lse)
            lse = jnp.where(lane == 2 * p + 1, mx[2 * p + 1] + jnp.log(odd), lse)
        lse_ref[...] = lse


def attend_forward(band, q, seg_own, seg_far, k_own, k_far, v_own, v_far, start, count, BQ=256, BK=256):
    rows, width = q.shape
    fills, steps = rows // CHUNK, rows // BQ
    mine = lambda i, *_: (jnp.clip(i - fills, 0, steps - 1), 0)
    fill = lambda i, *_: (jnp.minimum(i, fills - 1), 0)
    wide = pl.BlockSpec((CHUNK, width), fill)
    thin = pl.BlockSpec((CHUNK, 1), fill)
    return pl.pallas_call(
        functools.partial(attend_fwd_kernel, fills, BQ, BK),
        out_shape=(jax.ShapeDtypeStruct((rows, width), bf16), jax.ShapeDtypeStruct((rows, 128), f32)),
        grid_spec=pltpu.PrefetchScalarGridSpec(
            num_scalar_prefetch=3,
            grid=(fills + steps,),
            in_specs=[pl.BlockSpec((BQ, width), mine), pl.BlockSpec((BQ, 1), mine), wide, wide, wide, wide, thin, thin],
            out_specs=[pl.BlockSpec((BQ, width), mine), pl.BlockSpec((BQ, 128), mine)],
            scratch_shapes=[
                pltpu.VMEM((HEADS, 2 * rows, 128), bf16),
                pltpu.VMEM((HEADS, 2 * rows, 128), bf16),
                pltpu.VMEM((HEADS, BQ, 128), bf16),
                pltpu.VMEM((HEADS, BQ, 2 * rows), f32),
                pltpu.VMEM((HEADS, BQ, 128), f32),
                pltpu.VMEM((HEADS, BQ, 128), f32),
            ],
        ),
        compiler_params=pltpu.CompilerParams(vmem_limit_bytes=56 * MIB),
        cost_estimate=pl.CostEstimate(flops=30 * 10**9, bytes_accessed=10 * 10**6, transcendentals=0),
        name="attend_forward",
    )(start, count, band, q, seg_own, k_own, k_far, v_own, v_far, seg_own, seg_far)


def attend_bwd_kernel(fills, steps, BQ, BK, start_ref, count_ref, band_ref, q_ref, do_ref, o_ref, lse_ref, qseg_ref,
                      k_own, k_far, v_own, v_far, seg_own, seg_far, dq_ref, dkt_own, dkt_far, dvt_own, dvt_far,
                      kaug, vaug, qm, dom, lqt, ldot, dq_acc, dk_acc, dv_acc):
    i = pl.program_id(0)
    band = band_ref[0]
    local = kaug.shape[1] // 2

    @pl.when(i < fills)
    def _():
        side = side_lanes(CHUNK)
        extra = jnp.where((side >= 16) & (side < 19), -1.0, 0.0).astype(bf16)
        fill_keys(band, i, k_own, k_far, v_own, v_far, seg_own, seg_far, kaug, vaug, extra)
        for part in range(2):
            cols = pl.ds(pl.multiple_of(part * local + i * CHUNK, CHUNK), CHUNK)
            for p in range(PAIRS):
                dk_acc[p, :, cols] = jnp.zeros((128, CHUNK), f32)
                dv_acc[p, :, cols] = jnp.zeros((128, CHUNK), f32)

    @pl.when((i >= fills) & (i < fills + steps))
    def _():
        low, side = low_lanes(BQ), side_lanes(BQ)
        own = (side == qseg_ref[...]).astype(f32)
        for p in range(PAIRS):
            cols = slice(p * 128, (p + 1) * 128)
            q_pair, do_pair = q_ref[:, cols], do_ref[:, cols]
            prod = do_pair.astype(f32) * o_ref[:, cols].astype(f32)
            for e in range(2):
                mine = low if e == 0 else jnp.logical_not(low)
                h = 2 * p + e
                delta = jnp.sum(jnp.where(mine, prod, 0.0), axis=1, keepdims=True)
                qm[h] = jnp.where(mine, q_pair, place(side, split3(lse_ref[:, h : h + 1]), own).astype(bf16))
                dom[h] = jnp.where(mine, do_pair, place(side, split3(delta), jnp.zeros_like(own)).astype(bf16))
            zero = jnp.zeros((HEAD_DIM, BQ), bf16)
            for pair, dst in ((q_pair, lqt), (do_pair, ldot)):
                flipped = pair.T
                dst[p, 0:HEAD_DIM, 0:BQ] = flipped[0:HEAD_DIM]
                dst[p, HEAD_DIM:128, 0:BQ] = zero
                dst[p, 0:HEAD_DIM, BQ : 2 * BQ] = zero
                dst[p, HEAD_DIM:128, BQ : 2 * BQ] = flipped[HEAD_DIM:128]
        dq_acc[...] = jnp.zeros(dq_acc.shape, f32)
        start = start_ref[i - fills]

        def step(j, c):
            window = pl.ds(pl.multiple_of(start + j * BK, 128), BK)

            def scores(h):
                return mm(qm[h], kaug[h, window, :], NT), mm(dom[h], vaug[h, window, :], NT)

            ahead = scores(0)
            kept = []
            for h in range(HEADS):
                p = h // 2
                s, dp = ahead
                if h + 1 < HEADS:
                    ahead = scores(h + 1)
                prob = jnp.exp(s)
                ds = (prob * dp).astype(bf16)
                kept.append((prob.astype(bf16), ds))
                dq_acc[h] += mm(ds, kaug[h, window, :])
                if h % 2:
                    dv_acc[p, :, window] += mm(ldot[p], jnp.concatenate([kept[0][0], kept[1][0]], axis=0))
                    dk_acc[p, :, window] += mm(lqt[p], jnp.concatenate([kept[0][1], kept[1][1]], axis=0))
                    kept = []
            return c

        lax.fori_loop(0, count_ref[i - fills], step, 0)
        for p in range(PAIRS):
            pair = jnp.where(low, dq_acc[2 * p], dq_acc[2 * p + 1]) * HEAD_DIM**-0.5
            dq_ref[:, p * 128 : (p + 1) * 128] = pair.astype(bf16)

    @pl.when(i >= fills + steps)
    def _():
        j = i - fills - steps
        for p in range(PAIRS):
            rows = slice(p * 128, (p + 1) * 128)
            for first, dk_out, dv_out in ((band, dkt_own, dvt_own), (1 - band, dkt_far, dvt_far)):
                cols = pl.ds(pl.multiple_of(first * local + j * CHUNK, CHUNK), CHUNK)
                dk_out[rows, :] = dk_acc[p, :, cols].astype(bf16)
                dv_out[rows, :] = dv_acc[p, :, cols].astype(bf16)


def attend_backward(band, q, do, o, lse, seg_own, seg_far, k_own, k_far, v_own, v_far, start, count, BQ=256, BK=256):
    rows, width = q.shape
    fills, steps = rows // CHUNK, rows // BQ
    mine = lambda i, *_: (jnp.clip(i - fills, 0, steps - 1), 0)
    fill = lambda i, *_: (jnp.minimum(i, fills - 1), 0)
    drain = lambda i, *_: (0, jnp.clip(i - fills - steps, 0, fills - 1))
    wide = pl.BlockSpec((CHUNK, width), fill)
    thin = pl.BlockSpec((CHUNK, 1), fill)
    block = pl.BlockSpec((BQ, width), mine)
    flat = jax.ShapeDtypeStruct((width, rows), bf16)
    return pl.pallas_call(
        functools.partial(attend_bwd_kernel, fills, steps, BQ, BK),
        out_shape=(jax.ShapeDtypeStruct((rows, width), bf16), flat, flat, flat, flat),
        grid_spec=pltpu.PrefetchScalarGridSpec(
            num_scalar_prefetch=3,
            grid=(fills + steps + fills,),
            in_specs=[block, block, block, pl.BlockSpec((BQ, 128), mine), pl.BlockSpec((BQ, 1), mine), wide, wide, wide, wide, thin, thin],
            out_specs=[block] + [pl.BlockSpec((width, CHUNK), drain)] * 4,
            scratch_shapes=[
                pltpu.VMEM((HEADS, 2 * rows, 128), bf16),
                pltpu.VMEM((HEADS, 2 * rows, 128), bf16),
                pltpu.VMEM((HEADS, BQ, 128), bf16),
                pltpu.VMEM((HEADS, BQ, 128), bf16),
                pltpu.VMEM((PAIRS, 128, 2 * BQ), bf16),
                pltpu.VMEM((PAIRS, 128, 2 * BQ), bf16),
                pltpu.VMEM((HEADS, BQ, 128), f32),
                pltpu.VMEM((PAIRS, 128, 2 * rows), f32),
                pltpu.VMEM((PAIRS, 128, 2 * rows), f32),
            ],
        ),
        compiler_params=pltpu.CompilerParams(vmem_limit_bytes=56 * MIB),
        cost_estimate=pl.CostEstimate(flops=45 * 10**9, bytes_accessed=20 * 10**6, transcendentals=0),
        name="attend_backward",
    )(start, count, band, q, do, o, lse, seg_own, k_own, k_far, v_own, v_far, seg_own, seg_far)


def key_windows(seg_own, seg_far, band, BQ=256, BK=256):
    keys = 2 * seg_own.shape[0]
    blocks = seg_own.reshape(-1, BQ)
    first, last = blocks[:, 0], blocks[:, -1]

    def below(limit, strict):
        def count(seg):
            return jnp.sum((seg[None, :] < limit[:, None]) if strict else (seg[None, :] <= limit[:, None]), axis=1, dtype=jnp.int32)

        return count(seg_own) + count(seg_far)

    lo = below(first, True) // 128 * 128
    count = (below(last, False) - lo + BK - 1) // BK
    return jnp.minimum(lo, keys - count * BK), count


TN = (((0,), (0,)), ((), ()))
SLICE = 768
ERFC_RATE = 0.39
ERFC_TERMS = (0.23532524, 0.09138829, 0.64955972, -0.63540067, 0.88666461, -0.22753718)


def gelu_and_slope(u):
    bell = jnp.exp(u * u * -0.5)
    t = 1.0 / (1.0 + jnp.abs(u) * (ERFC_RATE * 0.5**0.5))
    total = ERFC_TERMS[-1] * 0.5
    for term in ERFC_TERMS[-2::-1]:
        total = total * t + term * 0.5
    half = total * t * bell
    below = jnp.where(u < 0, half, 1.0 - half)
    return u * below, below + u * bell * (0.5 / 3.141592653589793) ** 0.5


def normalize(rows):
    centred = rows - jnp.mean(rows, axis=-1, keepdims=True)
    scale = lax.rsqrt(jnp.mean(centred * centred, axis=-1, keepdims=True) + EPS)
    return centred * scale, scale


def add_sums(ref, row, values, first):
    sums = jnp.sum(values, axis=0, keepdims=True)
    at = slice(row, row + 1)
    ref[at, :] = jnp.where(first, sums, ref[at, :] + sums)


def mlp_kernel(blocks, rows, slices, band_ref, tok_ref, att_ref, cot_ref, wproj, wup, wdown, pbias, gain, shift, ubias, dbias,
               out_ref, rgrad_ref, agrad_ref, down_own, down_far, up_own, up_far, proj_own, proj_far, sums_ref, usums_ref,
               hid, ugr, n2s, bgs, ags, ats):
    i = pl.program_id(0)
    band = band_ref[0]
    half = down_own.shape[1]

    @pl.when(i < blocks)
    def _():
        here = pl.ds(pl.multiple_of(i * rows, rows), rows)
        first = i == 0
        att = att_ref[...]
        ats[here, :] = att
        residual = tok_ref[...] + mm(att, wproj[...]) + pbias[...]
        xhat, scale = normalize(residual)
        n2 = (xhat * gain[...] + shift[...]).astype(bf16)
        n2s[here, :] = n2
        cot = cot_ref[...]
        bg = cot.astype(bf16)
        bgs[here, :] = bg
        add_sums(sums_ref, 0, bg.astype(f32), first)
        for c in range(slices):
            cols = slice(c * SLICE, (c + 1) * SLICE)
            hidden, slope = gelu_and_slope(mm(n2, wup[:, cols]) + ubias[:, cols])
            hid[here, cols] = hidden.astype(bf16)
            grad = (mm(bg, wdown[cols, :], NT) * slope).astype(bf16)
            ugr[here, cols] = grad
            sums = jnp.sum(grad.astype(f32), axis=0, keepdims=True)
            usums_ref[0:1, cols] = jnp.where(first, sums, usums_ref[0:1, cols] + sums)
        out_ref[...] = residual + mm(hid[here, :], wdown[...]) + dbias[...]
        e = mm(ugr[here, :], wup[...], NT)
        add_sums(sums_ref, 1, e * xhat, first)
        add_sums(sums_ref, 2, e, first)
        f = e * gain[...]
        rgrad = cot + scale * (f - jnp.mean(f, axis=-1, keepdims=True) - xhat * jnp.mean(f * xhat, axis=-1, keepdims=True))
        rgrad_ref[...] = rgrad
        ag = rgrad.astype(bf16)
        ags[here, :] = ag
        add_sums(sums_ref, 3, ag.astype(f32), first)
        agrad_ref[...] = mm(ag, wproj[...], NT).astype(bf16)

    def columns(grad, own, far):
        left, right = grad[:, :half].astype(bf16), grad[:, half:].astype(bf16)
        own[...] = jnp.where(band == 0, left, right)
        far[...] = jnp.where(band == 0, right, left)

    @pl.when((i >= blocks) & (i < blocks + slices))
    def _():
        at = pl.ds(pl.multiple_of((i - blocks) * SLICE, SLICE), SLICE)
        columns(mm(hid[:, at], bgs[...], TN), down_own, down_far)

    def up_slice(which):
        at = pl.ds(pl.multiple_of(which * SLICE, SLICE), SLICE)
        return mm(n2s[...], ugr[:, at], TN).astype(bf16)

    middle = blocks + slices
    per_half = slices // 2

    @pl.when((i >= middle) & (i < middle + per_half))
    def _():
        up_far[...] = up_slice((1 - band) * per_half + i - middle)

    @pl.when((i >= middle + per_half) & (i < middle + slices))
    def _():
        up_own[...] = up_slice(band * per_half + i - middle - per_half)

    @pl.when(i == middle + slices)
    def _():
        columns(mm(ats[...], ags[...], TN), proj_own, proj_far)


def mlp(band, tokens, attended, cotangent, w_proj, w_up, w_down, proj_bias, gain, shift, up_bias, down_bias, rows=256):
    count, width = tokens.shape
    ff = w_up.shape[1]
    blocks, slices = count // rows, ff // SLICE
    half, per_half = width // 2, slices // 2
    one = pl.Buffered(1)
    mine = lambda i, *_: (jnp.minimum(i, blocks - 1), 0)
    whole = lambda i, *_: (0, 0)
    down_at = lambda i, *_: (jnp.clip(i - blocks, 0, slices - 1), 0)
    far_at = lambda i, *_: (0, jnp.clip(i - blocks - slices, 0, per_half - 1))
    own_at = lambda i, *_: (0, jnp.clip(i - blocks - slices - per_half, 0, per_half - 1))
    block = pl.BlockSpec((rows, width), mine)

    def full(a):
        return pl.BlockSpec(a.shape, whole, pipeline_mode=one)

    vectors = [v.reshape(1, -1) for v in (proj_bias, gain, shift, up_bias, down_bias)]
    shape = jax.ShapeDtypeStruct
    return pl.pallas_call(
        functools.partial(mlp_kernel, blocks, rows, slices),
        out_shape=(
            shape((count, width), f32),
            shape((count, width), f32),
            shape((count, width), bf16),
            shape((ff, half), bf16),
            shape((ff, half), bf16),
            shape((width, ff // 2), bf16),
            shape((width, ff // 2), bf16),
            shape((width, half), bf16),
            shape((width, half), bf16),
            shape((8, width), f32),
            shape((8, ff), f32),
        ),
        grid_spec=pltpu.PrefetchScalarGridSpec(
            num_scalar_prefetch=1,
            grid=(blocks + 2 * slices + 1,),
            in_specs=[block, block, block] + [full(a) for a in (w_proj, w_up, w_down, *vectors)],
            out_specs=[
                block,
                block,
                block,
                pl.BlockSpec((SLICE, half), down_at),
                pl.BlockSpec((SLICE, half), down_at),
                pl.BlockSpec((width, SLICE), own_at),
                pl.BlockSpec((width, SLICE), far_at),
                pl.BlockSpec((width, half), whole, pipeline_mode=one),
                pl.BlockSpec((width, half), whole, pipeline_mode=one),
                pl.BlockSpec((8, width), whole, pipeline_mode=one),
                pl.BlockSpec((8, ff), whole, pipeline_mode=one),
            ],
            scratch_shapes=[
                pltpu.VMEM((count, ff), bf16),
                pltpu.VMEM((count, ff), bf16),
                pltpu.VMEM((count, width), bf16),
                pltpu.VMEM((count, width), bf16),
                pltpu.VMEM((count, width), bf16),
                pltpu.VMEM((count, width), bf16),
            ],
        ),
        compiler_params=pltpu.CompilerParams(vmem_limit_bytes=58 * MIB),
        cost_estimate=pl.CostEstimate(flops=40 * 10**9, bytes_accessed=40 * 10**6, transcendentals=0),
        name="mlp",
    )(band, tokens, attended, cotangent, w_proj, w_up, w_down, *vectors)


def qkv_kernel(tok_ref, w_ref, gain, shift, qbias, vbias, q_ref, k_ref, v_ref, n_ref):
    width = tok_ref.shape[1]
    xhat, _ = normalize(tok_ref[...])
    n1 = (xhat * gain[...] + shift[...]).astype(bf16)
    n_ref[...] = n1
    k_ref[...] = mm(n1, w_ref[:, width : 2 * width]).astype(bf16)
    v_ref[...] = (mm(n1, w_ref[:, 2 * width :]) + vbias[...]).astype(bf16)
    q = (mm(n1, w_ref[:, :width]) + qbias[...]).astype(bf16)
    q_ref[...] = q * jnp.asarray(HEAD_DIM**-0.5, bf16)


def project_qkv(tokens, w_qkv, gain, shift, query_bias, value_bias, rows=256):
    count, width = tokens.shape
    one = pl.Buffered(1)
    block = pl.BlockSpec((rows, width), lambda i: (i, 0))
    vectors = [v.reshape(1, -1) for v in (gain, shift, query_bias, value_bias)]
    return pl.pallas_call(
        qkv_kernel,
        out_shape=(jax.ShapeDtypeStruct((count, width), bf16),) * 4,
        grid=(count // rows,),
        in_specs=[block] + [pl.BlockSpec(a.shape, lambda i: (0, 0), pipeline_mode=one) for a in (w_qkv, *vectors)],
        out_specs=[block] * 4,
        compiler_params=pltpu.CompilerParams(vmem_limit_bytes=32 * MIB),
        cost_estimate=pl.CostEstimate(flops=4 * 10**9, bytes_accessed=13 * 10**6, transcendentals=0),
        name="project_qkv",
    )(tokens, w_qkv, *vectors)


def qkv_grad_kernel(blocks, rows, band_ref, dq_ref, dk_own, dk_far, dv_own, dv_far, n_ref, packed_ref, own_ref, far_ref, sums_ref, packed):
    i = pl.program_id(0)
    band = band_ref[0]
    width = dq_ref.shape[1]
    half = own_ref.shape[1]

    @pl.when(i < blocks)
    def _():
        here = pl.ds(pl.multiple_of(i * rows, rows), rows)
        first = i == 0
        dq = dq_ref[...]
        packed_ref[:, :width] = dq
        packed[here, :width] = dq
        add_sums(sums_ref, 0, dq.astype(f32), first)
        for t, (own, far) in enumerate(((dk_own, dk_far), (dv_own, dv_far))):
            for p in range(width // 128):
                at = slice(p * 128, (p + 1) * 128)
                to = slice((t + 1) * width + p * 128, (t + 1) * width + (p + 1) * 128)
                turned = (own[at, :].astype(f32) + far[at, :].astype(f32)).astype(bf16).T
                packed_ref[:, to] = turned
                packed[here, to] = turned
        add_sums(sums_ref, 1, packed_ref[:, 2 * width :].astype(f32), first)

    def columns(which):
        at = pl.ds(pl.multiple_of(which * half, 128), half)
        return mm(n_ref[...], packed[:, at], TN).astype(bf16)

    @pl.when(i == blocks)
    def _():
        far_ref[...] = columns(1 - band)

    @pl.when(i == blocks + 1)
    def _():
        own_ref[...] = columns(band)


def qkv_grads(band, dq, dk_own, dk_far, dv_own, dv_far, normed, rows=256):
    count, width = dq.shape
    blocks = count // rows
    half = 3 * width // 2
    one = pl.Buffered(1)
    mine = lambda i, *_: (jnp.minimum(i, blocks - 1), 0)
    flip = lambda i, *_: (0, jnp.minimum(i, blocks - 1))
    whole = lambda i, *_: (0, 0)
    shape = jax.ShapeDtypeStruct
    return pl.pallas_call(
        functools.partial(qkv_grad_kernel, blocks, rows),
        out_shape=(shape((count, 3 * width), bf16), shape((width, half), bf16), shape((width, half), bf16), shape((8, width), f32)),
        grid_spec=pltpu.PrefetchScalarGridSpec(
            num_scalar_prefetch=1,
            grid=(blocks + 2,),
            in_specs=[pl.BlockSpec((rows, width), mine)]
            + [pl.BlockSpec((width, rows), flip)] * 4
            + [pl.BlockSpec((count, width), whole, pipeline_mode=one)],
            out_specs=[
                pl.BlockSpec((rows, 3 * width), mine),
                pl.BlockSpec((width, half), whole, pipeline_mode=one),
                pl.BlockSpec((width, half), whole, pipeline_mode=one),
                pl.BlockSpec((8, width), whole, pipeline_mode=one),
            ],
            scratch_shapes=[pltpu.VMEM((count, 3 * width), bf16)],
        ),
        compiler_params=pltpu.CompilerParams(vmem_limit_bytes=40 * MIB),
        cost_estimate=pl.CostEstimate(flops=8 * 10**9, bytes_accessed=18 * 10**6, transcendentals=0),
        name="qkv_grads",
    )(band, dq, dk_own, dk_far, dv_own, dv_far, normed)


def input_grad_kernel(packed_ref, tok_ref, rgrad_ref, w_ref, gain, out_ref, sums_ref):
    first = pl.program_id(0) == 0
    e = mm(packed_ref[...], w_ref[...], NT)
    xhat, scale = normalize(tok_ref[...])
    add_sums(sums_ref, 0, e * xhat, first)
    add_sums(sums_ref, 1, e, first)
    f = e * gain[...]
    back = scale * (f - jnp.mean(f, axis=-1, keepdims=True) - xhat * jnp.mean(f * xhat, axis=-1, keepdims=True))
    out_ref[...] = rgrad_ref[...] + back


def input_grads(packed, tokens, rgrad, w_qkv, gain, rows=256):
    count, width = tokens.shape
    one = pl.Buffered(1)
    block = pl.BlockSpec((rows, width), lambda i: (i, 0))
    return pl.pallas_call(
        input_grad_kernel,
        out_shape=(jax.ShapeDtypeStruct((count, width), f32), jax.ShapeDtypeStruct((8, width), f32)),
        grid=(count // rows,),
        in_specs=[
            pl.BlockSpec((rows, packed.shape[1]), lambda i: (i, 0)),
            block,
            block,
            pl.BlockSpec(w_qkv.shape, lambda i: (0, 0), pipeline_mode=one),
            pl.BlockSpec((1, width), lambda i: (0, 0), pipeline_mode=one),
        ],
        out_specs=[block, pl.BlockSpec((8, width), lambda i: (0, 0), pipeline_mode=one)],
        compiler_params=pltpu.CompilerParams(vmem_limit_bytes=32 * MIB),
        cost_estimate=pl.CostEstimate(flops=6 * 10**9, bytes_accessed=18 * 10**6, transcendentals=0),
        name="input_grads",
    )(packed, tokens, rgrad, w_qkv, gain.reshape(1, -1))


def swap_band(x):
    return lax.ppermute(x, "band", [(0, 1), (1, 0)])


def join_band(own, far):
    return (own.astype(f32) + swap_band(far).astype(f32)).astype(bf16)


def pick(x, which, axis):
    return lax.dynamic_index_in_dim(x, which, axis, keepdims=False)


def halve(x, axis, bit, size):
    mine = (lax.axis_index("dp") >> bit) & 1
    arrived = lax.ppermute(pick(x, 1 - mine, axis), "dp", [(i, i ^ (1 << bit)) for i in range(size)])
    return pick(x, mine, axis).astype(f32) + arrived.astype(f32)


class Reduction:
    def __init__(self, x, order, size):
        rows, columns = x.shape
        levels = size.bit_length() - 1
        self.size = size
        self.x = x.reshape((2,) * levels + (rows // size, columns))
        self.left = list(range(levels - 1, -1, -1))
        self.order = list(order)

    def step(self):
        if self.order:
            bit = self.order.pop(0)
            x = halve(self.x, self.left.index(bit), bit, self.size)
            self.left.remove(bit)
            self.x = x.astype(bf16) if self.left else x

    def finish(self):
        while self.order:
            self.step()
        return self.x


def local(
    size,
    inputs,
    segment_ids,
    cotangent,
    first_gain,
    first_bias,
    w_qkv,
    query_bias,
    value_bias,
    w_proj,
    proj_bias,
    second_gain,
    second_bias,
    w_up,
    up_bias,
    w_down,
    down_bias,
):
    local_shape = inputs.shape
    width = local_shape[-1]
    levels = size.bit_length() - 1
    rising = list(range(levels))
    turned = [1, 0] + list(range(2, levels))
    band = lax.axis_index("band")
    band_at = band.astype(jnp.int32).reshape(1)
    tokens = inputs.reshape(-1, width)
    seg_own = segment_ids.reshape(-1)
    seg_far = swap_band(seg_own)
    start, count = key_windows(seg_own, seg_far, band)
    queries, k_own, v_own, normed = project_qkv(tokens, w_qkv, first_gain, first_bias, query_bias, value_bias)
    k_far, v_far = swap_band(k_own), swap_band(v_own)
    keys = (seg_own[:, None], seg_far[:, None], k_own, k_far, v_own, v_far, start, count)
    attended, log_totals = attend_forward(band_at, queries, *keys)
    (
        output,
        residual_grad,
        attended_grad,
        down_own,
        down_far,
        up_own,
        up_far,
        proj_own,
        proj_far,
        mlp_sums,
        up_sums,
    ) = mlp(
        band_at,
        tokens,
        attended,
        cotangent.reshape(-1, width),
        w_proj,
        w_up,
        w_down,
        proj_bias,
        second_gain,
        second_bias,
        up_bias,
        down_bias,
    )
    down = Reduction(join_band(down_own, down_far), rising, size)
    up = Reduction(join_band(up_own, up_far), turned, size)
    query_grad, dk_own, dk_far, dv_own, dv_far = attend_backward(
        band_at, queries, attended_grad, attended, log_totals, *keys
    )
    packed, qkv_own, qkv_far, qkv_sums = qkv_grads(
        band_at, query_grad, dk_own, swap_band(dk_far), dv_own, swap_band(dv_far), normed
    )
    input_grad, first_sums = input_grads(packed, tokens, residual_grad, w_qkv, first_gain)
    proj = Reduction(join_band(proj_own, proj_far), turned, size)
    qkv = Reduction(join_band(qkv_own, qkv_far), rising, size)
    tall = jnp.concatenate([first_sums[:2], qkv_sums[:2], mlp_sums[:4]], axis=0)
    thin = jnp.concatenate([tall.T, up_sums[0].reshape(width, -1)], axis=1)
    thin = jnp.pad(thin, ((0, 0), (0, 128 - thin.shape[1]))).astype(bf16)
    thin_sum = Reduction(join_band(thin, thin), turned, size).finish()
    vectors = [thin_sum[:, t] for t in range(8)]
    ups = up_bias.shape[0] // width
    return (
        output.reshape(local_shape),
        input_grad.reshape(local_shape),
        vectors[0],
        vectors[1],
        qkv.finish(),
        vectors[2],
        vectors[3],
        proj.finish(),
        vectors[7],
        vectors[5],
        vectors[6],
        up.finish(),
        thin_sum[:, 8 : 8 + ups].reshape(-1),
        down.finish(),
        vectors[4],
    )


def solution(mesh):
    size = mesh.shape["dp"]
    placed = (P("dp", "band", None), P("dp", "band"), P("dp", "band", None)) + (P(),) * 13
    split, thin = P("dp", "band"), P("dp")
    wide = P("dp", "band", None)
    return jax.shard_map(
        functools.partial(local, size),
        mesh=mesh,
        in_specs=placed,
        out_specs=(wide, wide, thin, thin, split, thin, thin, split, thin, thin, thin, split, thin, split, thin),
        check_vma=False,
    )
```

profile of v0, /device:TPU:0, one launch (start us, length us, event | category | flops | bytes accessed | tf_op | source)
XLA Modules:
  0.0 335.4 jit_solution(10559993956002488894)
XLA Ops:
  3.4 2.0 copy-done
  5.4 1.9 copy-done.2
  7.3 5.3 %project_qkv.1 = (bf16[1024,768]{1,0:T(8,128)(2,1)S(1)}, bf16[1024,768]{1,0:T(8,128)(2,1)S(1)}, bf16[1024,768]{1,0:T(8,128)(2,1)S(1)}, bf16[1024,768]{1,0:T(8,128)(2,1)S(1)}) custom-call(f32[1024,768]{1,0:T(8,128)S(1)} %bitcast.131, bf16[768,2304]{1,0:T(8,128)(2,1)S(1)} %copy-done, f32[1,768]{1,0:T(1,128)S(1)} %reshape.135.gain, ...), custom_call_target="tpu_custom_call" | custom-call | flops 4000000000 | bytes 13000000 | tf_op jit(solution)/shard_map/project_qkv/pallas_call | solution.py:465
  12.6 1.2 copy-done.12
  13.8 1.2 copy-done.14
  17.5 1.0 copy.82.qseg_ref.seg_own
  20.9 1.0 copy.84.seg_far
  22.7 33.7 %attend_forward.1 = (bf16[1024,768]{1,0:T(8,128)(2,1)}, f32[1024,128]{1,0:T(8,128)}) custom-call(s32[4]{0:T(128)} %get-tuple-element.85.start_ref, s32[4]{0:T(128)} %get-tuple-element.86.count_ref, s32[1]{0:T(128)} %bitcast.band_ref, bf16[1024,768]{1,0:T(8,128)(2,1)} %copy-done.14, s32[1024,1]{1,0:T(8,128)} %copy.82.qseg_ref.seg_own, ...), custom_call_target="tpu_custom_call" | custom-call | flops 30000001024 | bytes 10000000 | tf_op jit(solution)/shard_map/attend_forward/pallas_call | solution.py:128
  56.4 57.6 %mlp.1 = (f32[1024,768]{1,0:T(8,128)}, f32[1024,768]{1,0:T(8,128)}, bf16[1024,768]{1,0:T(8,128)(2,1)}, bf16[3072,384]{1,0:T(8,128)(2,1)}, bf16[3072,384]{1,0:T(8...) custom-call(s32[1]{0:T(128)} %bitcast.band_ref, ...), custom_call_target="tpu_custom_call" | custom-call | flops 40000000000 | bytes 40000000 | tf_op jit(solution)/shard_map/mlp/pallas_call | solution.py:402
  114.1 50.6 %attend_backward.1 = (bf16[1024,768]{1,0:T(8,128)(2,1)}, bf16[768,1024]{1,0:T(8,128)(2,1)}, bf16[768,1024]{1,0:T(8,128)(2,1)}, bf16[768,1024]{1,0:T(8,128)(2,1)}, bf16[768,1024]{1,0:T(8,128)(2,1)}) custom-call(s32[4]{0:T(128)} %get-tuple-element.85.start_ref, s32[4]{0:T(128)} %get-tuple-element.86.count_ref, s32[1]{0:T(128)} %bitcast.band_ref, ...), custom_call_target="tpu_custom_call" | custom-call | flops 44999999488 | bytes 20000000 | tf_op jit(solution)/shard_map/attend_backward/pallas_call | solution.py:242
  165.3 1.4 add_convert_fusion.3
  167.5 9.2 %collective-permute-start.16 = (bf16[2,2,2,48,384]{4,3,0,1,2:T(8,128)(2,1)}, bf16[2,2,2,48,384]{4,3,0,1,2:T(8,128)(2,1)}, u32[]{:S(2)}, u32[]{:S(2)}) collective-permute-start(bf16[2,2,2,48,384]{4,3,0,1,2:T(8,128)(2,1)} %bitcast.129), channel_id=1, source_target_pairs={{0,4},{2,6},{4,0},{6,2},{8,12},{10,14},{12,8},{14,10},{16,20},{18,... | collective-permute-start | bytes 884744 | tf_op jit(solution)/shard_map/ppermute | solution.py:592
  177.2 1.3 slice.93
  179.5 1.1 reshape_squeeze.4
  180.6 1.0 copy.88
  181.6 2.6 collective-permute-done.16
  184.3 1.0 fusion.8
  185.4 1.6 collective-permute-start.17
  186.9 1.2 copy-done.4
  188.1 1.2 copy-done.6
  189.3 1.4 copy-done.5
  190.7 1.4 copy-done.7
  192.1 1.4 copy-done.13
  193.5 1.4 copy-done.15
  194.9 1.4 copy-done.16
  196.3 1.4 copy-done.17
  197.7 9.2 %qkv_grads.1 = (bf16[1024,2304]{1,0:T(8,128)(2,1)}, bf16[768,1152]{1,0:T(8,128)(2,1)S(1)}, bf16[768,1152]{1,0:T(8,128)(2,1)S(1)}, f32[8,768]{1,0:T(8,128)S(1)}) custom-call(s32[1]{0:T(128)} %bitcast.band_ref, bf16[1024,768]{1,0:T(8,128)(2,1)S(1)} %copy-done.15, bf16[768,1024]{1,0:T(8,128)(2,1)S(1)} %copy-done.16, bf16[768,1024]{1,0:T(8,128)(2,1)S(1)} %copy-done.5, ...), custom_call_target="tpu_custom_call" | custom-call | flops 8000000000 | bytes 18000000 | tf_op jit(solution)/shard_map/qkv_grads/pallas_call | solution.py:522
  207.0 2.3 copy-done.10
  209.3 6.4 %input_grads.1 = (f32[1024,768]{1,0:T(8,128)}, f32[8,768]{1,0:T(8,128)S(1)}) custom-call(bf16[1024,2304]{1,0:T(8,128)(2,1)S(1)} %copy-done.10, f32[1024,768]{1,0:T(8,128)S(1)} %bitcast.132, f32[1024,768]{1,0:T(8,128)S(1)} %copy-done.11, bf16[768,2304]{1,0:T(8,128)(2,1)S(1)} %copy-done.1, f32[1,768]{1,0:T(1,128)S(1)} %reshape.135.gain), custom_call_target="tpu_custom_call" | custom-call | flops 6000000000 | bytes 18000000 | tf_op jit(solution)/shard_map/input_grads/pallas_call | solution.py:560
  218.0 1.7 copy.89
  220.6 1.7 collective-permute-start.6
  223.3 1.6 collective-permute-start.18
  228.5 2.0 collective-permute-done.7
  230.6 2.0 collective-permute-start.8
  232.6 2.6 collective-permute-start.19
  235.2 2.3 collective-permute-start.9
  238.3 1.6 collective-permute-done.9
  239.9 3.0 add_convert_fusion
  242.9 1.3 constant_dynamic-slice_fusion.1
  244.2 1.2 copy.120
  246.3 2.4 add_convert_fusion.1
  248.7 1.3 constant_dynamic-slice_fusion.3
  250.0 1.1 copy.121
  251.1 1.4 collective-permute-start.21
  254.0 1.4 reshape.151
  255.4 2.1 add_convert_fusion.2
  257.5 15.0 %collective-permute-done.26 = bf16[2,2,2,192,384]{4,3,0,1,2:T(8,128)(2,1)} collective-permute-done((bf16[2,2,2,192,384]{4,3,0,1,2:T(8,128)(2,1)}, bf16[2,2,2,192,384]{4,3,0,1,2:T(8,128)(2,1)}, u32[]{:S(2)}, u32[]{:S(2)}) %collective-permute-start.26) | collective-permute-done | bytes 1179680 | tf_op jit(solution)/shard_map/ppermute | solution.py:592
  272.4 1.8 fusion
  274.3 1.5 collective-permute-start.27
  275.8 4.5 %collective-permute-done.21 = bf16[2,2,2,48,1536]{4,3,0,1,2:T(8,128)(2,1)} collective-permute-done((bf16[2,2,2,48,1536]{4,3,0,1,2:T(8,128)(2,1)}, bf16[2,2,2,48,1536]{4,3,0,1,2:T(8,128)(2,1)}, u32[]{:S(2)}, u32[]{:S(2)}) %collective-permute-start.21) | collective-permute-done | bytes 1179680 | tf_op jit(solution)/shard_map/ppermute | solution.py:592
  280.3 1.5 fusion.1
  281.9 1.2 collective-permute-start.22
  284.3 6.5 %collective-permute-done.27 = bf16[2,2,192,384]{3,2,0,1:T(8,128)(2,1)S(1)} collective-permute-done((bf16[2,2,192,384]{3,2,0,1:T(8,128)(2,1)S(1)}, bf16[2,2,192,384]{3,2,0,1:T(8,128)(2,1)S(1)}, u32[]{:S(2)}, u32[]{:S(2)}) %collective-permute-start.27) | collective-permute-done | bytes 589856 | tf_op jit(solution)/shard_map/ppermute | solution.py:592
  290.9 1.5 collective-permute-start.28
  292.5 5.8 %collective-permute-done.22 = bf16[2,2,48,1536]{3,2,0,1:T(8,128)(2,1)S(1)} collective-permute-done((bf16[2,2,48,1536]{3,2,0,1:T(8,128)(2,1)S(1)}, bf16[2,2,48,1536]{3,2,0,1:T(8,128)(2,1)S(1)}, u32[]{:S(2)}, u32[]{:S(2)}) %collective-permute-start.22) | collective-permute-done | bytes 589856 | tf_op jit(solution)/shard_map/ppermute | solution.py:592
  298.4 1.3 collective-permute-start.23
  299.7 12.4 %collective-permute-done.11 = bf16[2,2,2,48,1152]{4,3,0,1,2:T(8,128)(2,1)S(1)} collective-permute-done((bf16[2,2,2,48,1152]{4,3,0,1,2:T(8,128)(2,1)S(1)}, bf16[2,2,2,48,1152]{4,3,0,1,2:T(8,128)(2,1)S(1)}, u32[]{:S(2)}, u32[]{:S(2)}) %collective-permute-start.11) | collective-permute-done | bytes 884768 | tf_op jit(solution)/shard_map/ppermute | solution.py:592
  312.3 1.6 collective-permute-start.12
  314.1 2.4 collective-permute-start.29
  317.2 3.5 %collective-permute-done.12 = bf16[2,2,48,1152]{3,2,0,1:T(8,128)(2,1)S(1)} collective-permute-done((bf16[2,2,48,1152]{3,2,0,1:T(8,128)(2,1)S(1)}, bf16[2,2,48,1152]{3,2,0,1:T(8,128)(2,1)S(1)}, u32[]{:S(2)}, u32[]{:S(2)}) %collective-permute-start.12) | collective-permute-done | bytes 442400 | tf_op jit(solution)/shard_map/ppermute | solution.py:592
  320.9 1.7 collective-permute-start.13
  322.6 2.7 collective-permute-done.24
  327.0 3.7 %collective-permute-start.14 = (bf16[48,1152]{1,0:T(8,128)(2,1)S(1)}, bf16[48,1152]{1,0:T(8,128)(2,1)S(1)}, u32[]{:S(2)}, u32[]{:S(2)}) collective-permute-start(bf16[48,1152]{1,0:T(8,128)(2,1)S(1)} %dynamic-slice_bitcast_fusion.9), channel_id=1, source_target_pairs={{0,16},{2,18},{4,20},{6,22},{8,24},{10,26},{12,28},{14,30},{16,0},... | collective-permute-start | bytes 331784 | tf_op jit(solution)/shard_map/ppermute | solution.py:592
  331.5 3.2 collective-permute-done.14
  (135 shorter events, 28.4 us)
Async XLA Ops:
  3.4 2.0 copy-start
  5.4 1.9 copy-start.2
  7.3 8.2 %copy-start.21 = (s32[1,1024]{1,0:T(1,128)S(1)}, s32[1,1024]{1,0:T(1,128)}, u32[]{:S(2)}) copy-start(s32[1,1024]{1,0:T(1,128)} %param.17) | copy-start | bytes 12292
  7.3 11.2 %copy-start.23 = (f32[768]{0:T(1024)S(1)}, f32[768]{0:T(1024)}, u32[]{:S(2)}) copy-start(f32[768]{0:T(1024)} %param.25) | copy-start | bytes 9220
  7.3 11.8 %copy-start.24 = (f32[768]{0:T(1024)S(1)}, f32[768]{0:T(1024)}, u32[]{:S(2)}) copy-start(f32[768]{0:T(1024)} %param.26) | copy-start | bytes 9220
  7.3 12.4 %copy-start.25 = (f32[768]{0:T(1024)S(1)}, f32[768]{0:T(1024)}, u32[]{:S(2)}) copy-start(f32[768]{0:T(1024)} %param.27) | copy-start | bytes 9220
  7.3 12.9 %copy-start.26 = (f32[768]{0:T(1024)S(1)}, f32[768]{0:T(1024)}, u32[]{:S(2)}) copy-start(f32[768]{0:T(1024)} %param.31) | copy-start | bytes 9220
  12.6 1.2 copy-start.12
  13.8 1.2 copy-start.14
  15.0 7.7 %copy-start.8 = (bf16[1024,768]{1,0:T(8,128)(2,1)}, bf16[1024,768]{1,0:T(8,128)(2,1)S(1)}, u32[]{:S(2)}) copy-start(bf16[1024,768]{1,0:T(8,128)(2,1)S(1)} %get-tuple-element.44.k_own) | copy-start | bytes 4718596
  15.0 7.7 %copy-start.9 = (bf16[1024,768]{1,0:T(8,128)(2,1)}, bf16[1024,768]{1,0:T(8,128)(2,1)S(1)}, u32[]{:S(2)}) copy-start(bf16[1024,768]{1,0:T(8,128)(2,1)S(1)} %get-tuple-element.45.v_own) | copy-start | bytes 4718596
  15.0 7.7 %collective-permute-start.1 = (bf16[1024,768]{1,0:T(8,128)(2,1)S(1)}, bf16[1024,768]{1,0:T(8,128)(2,1)}, u32[]{:S(2)}, u32[]{:S(2)}) collective-permute-start(bf16[1024,768]{1,0:T(8,128)(2,1)S(1)} %get-tuple-element.44.k_own), channel_id=1, source_target_pairs={{0,1},{1,0},{2,3},{3,2},{4,5},{5,4},{6,7},{7,6},{8,9},{9,8},{10,11... | collective-permute-start | bytes 4718600 | tf_op jit(solution)/shard_map/ppermute | solution.py:579
  15.4 7.2 %collective-permute-start.2 = (bf16[1024,768]{1,0:T(8,128)(2,1)S(1)}, bf16[1024,768]{1,0:T(8,128)(2,1)}, u32[]{:S(2)}, u32[]{:S(2)}) collective-permute-start(bf16[1024,768]{1,0:T(8,128)(2,1)S(1)} %get-tuple-element.45.v_own), channel_id=1, source_target_pairs={{0,1},{1,0},{2,3},{3,2},{4,5},{5,4},{6,7},{7,6},{8,9},{9,8},{10,11... | collective-permute-start | bytes 4718600 | tf_op jit(solution)/shard_map/ppermute | solution.py:579
  15.5 5.3 %collective-permute-start = (s32[1024]{0:T(1024)S(1)}, s32[1024]{0:T(1024)S(1)}, u32[]{:S(2)}, u32[]{:S(2)}) collective-permute-start(s32[1024]{0:T(1024)S(1)} %bitcast.140), channel_id=1, source_target_pairs={{0,1},{1,0},{2,3},{3,2},{4,5},{5,4},{6,7},{7,6},{8,9},{9,8},{10,11... | collective-permute-start | bytes 12296 | tf_op jit(solution)/shard_map/ppermute | solution.py:579
  114.0 51.3 %collective-permute-start.15 = (bf16[768,384]{1,0:T(8,128)(2,1)}, bf16[768,384]{1,0:T(8,128)(2,1)}, u32[]{:S(2)}, u32[]{:S(2)}) collective-permute-start(bf16[768,384]{1,0:T(8,128)(2,1)} %get-tuple-element.66), channel_id=1, source_target_pairs={{0,1},{1,0},{2,3},{3,2},{4,5},{5,4},{6,7},{7,6},{8,9},{9,8},{10,11... | collective-permute-start | bytes 1769480 | tf_op jit(solution)/shard_map/ppermute | solution.py:579
  164.7 22.2 %collective-permute-start.3 = (bf16[768,1024]{1,0:T(8,128)(2,1)}, bf16[768,1024]{1,0:T(8,128)(2,1)S(1)}, u32[]{:S(2)}, u32[]{:S(2)}) collective-permute-start(bf16[768,1024]{1,0:T(8,128)(2,1)} %get-tuple-element.52), channel_id=1, source_target_pairs={{0,1},{1,0},{2,3},{3,2},{4,5},{5,4},{6,7},{7,6},{8,9},{9,8},{10,11... | collective-permute-start | bytes 4718600 | tf_op jit(solution)/shard_map/ppermute | solution.py:579
  164.8 23.3 %collective-permute-start.4 = (bf16[768,1024]{1,0:T(8,128)(2,1)}, bf16[768,1024]{1,0:T(8,128)(2,1)S(1)}, u32[]{:S(2)}, u32[]{:S(2)}) collective-permute-start(bf16[768,1024]{1,0:T(8,128)(2,1)} %get-tuple-element.54), channel_id=1, source_target_pairs={{0,1},{1,0},{2,3},{3,2},{4,5},{5,4},{6,7},{7,6},{8,9},{9,8},{10,11... | collective-permute-start | bytes 4718600 | tf_op jit(solution)/shard_map/ppermute | solution.py:579
  167.5 16.8 %collective-permute-start.16 = (bf16[2,2,2,48,384]{4,3,0,1,2:T(8,128)(2,1)}, bf16[2,2,2,48,384]{4,3,0,1,2:T(8,128)(2,1)}, u32[]{:S(2)}, u32[]{:S(2)}) collective-permute-start(bf16[2,2,2,48,384]{4,3,0,1,2:T(8,128)(2,1)} %bitcast.129), channel_id=1, source_target_pairs={{0,4},{2,6},{4,0},{6,2},{8,12},{10,14},{12,8},{14,10},{16,20},{18,... | collective-permute-start | bytes 884744 | tf_op jit(solution)/shard_map/ppermute | solution.py:592
  176.7 63.2 %collective-permute-start.25 = (bf16[3072,384]{1,0:T(8,128)(2,1)}, bf16[3072,384]{1,0:T(8,128)(2,1)}, u32[]{:S(2)}, u32[]{:S(2)}) collective-permute-start(bf16[3072,384]{1,0:T(8,128)(2,1)} %get-tuple-element.70), channel_id=1, source_target_pairs={{0,1},{1,0},{2,3},{3,2},{4,5},{5,4},{6,7},{7,6},{8,9},{9,8},{10,11... | collective-permute-start | bytes 7077896 | tf_op jit(solution)/shard_map/ppermute | solution.py:579
  176.7 69.0 %collective-permute-start.20 = (bf16[768,1536]{1,0:T(8,128)(2,1)}, bf16[768,1536]{1,0:T(8,128)(2,1)}, u32[]{:S(2)}, u32[]{:S(2)}) collective-permute-start(bf16[768,1536]{1,0:T(8,128)(2,1)} %get-tuple-element.68), channel_id=1, source_target_pairs={{0,1},{1,0},{2,3},{3,2},{4,5},{5,4},{6,7},{7,6},{8,9},{9,8},{10,11... | collective-permute-start | bytes 7077896 | tf_op jit(solution)/shard_map/ppermute | solution.py:579
  185.4 30.5 %collective-permute-start.17 = (bf16[2,2,48,384]{3,2,0,1:T(8,128)(2,1)S(1)}, bf16[2,2,48,384]{3,2,0,1:T(8,128)(2,1)S(1)}, u32[]{:S(2)}, u32[]{:S(2)}) collective-permute-start(bf16[2,2,48,384]{3,2,0,1:T(8,128)(2,1)S(1)} %dynamic-slice_bitcast_fusion.8), channel_id=1, source_target_pairs={{0,2},{2,0},{4,6},{6,4},{8,10},{10,8},{12,14},{14,12},{16,18},{18,... | collective-permute-start | bytes 442376 | tf_op jit(solution)/shard_map/ppermute | solution.py:592
  186.9 1.2 copy-start.4
  188.1 1.2 copy-start.6
  189.3 1.4 copy-start.5
  190.7 1.4 copy-start.7
  192.1 1.4 copy-start.13
  193.5 1.4 copy-start.15
  194.9 1.4 copy-start.16
  196.3 1.4 copy-start.17
  197.7 9.2 %copy-start.1 = (bf16[768,2304]{1,0:T(8,128)(2,1)S(1)}, bf16[768,2304]{1,0:T(8,128)(2,1)}, u32[]{:S(2)}) copy-start(bf16[768,2304]{1,0:T(8,128)(2,1)} %w_ref.3) | copy-start | bytes 10616836
  197.7 9.2 %copy-start.3 = (f32[1,1024,768]{2,1,0:T(8,128)S(1)}, f32[1,1024,768]{2,1,0:T(8,128)}, u32[]{:S(2)}) copy-start(f32[1,1024,768]{2,1,0:T(8,128)} %param.16) | copy-start | bytes 9437188
  197.7 9.2 %copy-start.11 = (f32[1024,768]{1,0:T(8,128)S(1)}, f32[1024,768]{1,0:T(8,128)}, u32[]{:S(2)}) copy-start(f32[1024,768]{1,0:T(8,128)} %get-tuple-element.57.rgrad_ref) | copy-start | bytes 9437188
  206.9 2.3 copy-start.10
  209.3 6.4 %copy-start.22 = (bf16[4,768]{1,0:T(4,128)(2,1)S(1)}, bf16[4,768]{1,0:T(4,128)(2,1)}, u32[]{:S(2)}) copy-start(bf16[4,768]{1,0:T(4,128)(2,1)} %slice.93) | copy-start | bytes 18436
  215.8 1.5 collective-permute-start.5
  220.6 4.8 %collective-permute-start.6 = (bf16[2,2,2,48,128]{4,3,2,1,0:T(8,128)(2,1)S(1)}, bf16[2,2,2,48,128]{4,3,2,1,0:T(8,128)(2,1)S(1)}, u32[]{:S(2)}, u32[]{:S(2)}) collective-permute-start(bf16[2,2,2,48,128]{4,3,2,1,0:T(8,128)(2,1)S(1)} %dynamic-slice_bitcast_fusion.10), channel_id=1, source_target_pairs={{0,4},{2,6},{4,0},{6,2},{8,12},{10,14},{12,8},{14,10},{16,20},{18,... | collective-permute-start | bytes 294920 | tf_op jit(solution)/shard_map/ppermute | solution.py:592
  223.3 4.4 %collective-permute-start.18 = (bf16[2,48,384]{2,1,0:T(8,128)(2,1)S(1)}, bf16[2,48,384]{2,1,0:T(8,128)(2,1)S(1)}, u32[]{:S(2)}, u32[]{:S(2)}) collective-permute-start(bf16[2,48,384]{2,1,0:T(8,128)(2,1)S(1)} %dynamic-slice_bitcast_fusion.11), channel_id=1, source_target_pairs={{0,8},{2,10},{4,12},{6,14},{8,0},{10,2},{12,4},{14,6},{16,24},{18,... | collective-permute-start | bytes 221192 | tf_op jit(solution)/shard_map/ppermute | solution.py:592
  226.4 4.2 %collective-permute-start.7 = (bf16[2,2,48,128]{3,2,1,0:T(8,128)(2,1)S(1)}, bf16[2,2,48,128]{3,2,1,0:T(8,128)(2,1)S(1)}, u32[]{:S(2)}, u32[]{:S(2)}) collective-permute-start(bf16[2,2,48,128]{3,2,1,0:T(8,128)(2,1)S(1)} %dynamic-slice_bitcast_fusion.12), channel_id=1, source_target_pairs={{0,2},{2,0},{4,6},{6,4},{8,10},{10,8},{12,14},{14,12},{16,18},{18,... | collective-permute-start | bytes 147464 | tf_op jit(solution)/shard_map/ppermute | solution.py:592
  230.6 4.6 %collective-permute-start.8 = (bf16[2,48,128]{2,1,0:T(8,128)(2,1)S(1)}, bf16[2,48,128]{2,1,0:T(8,128)(2,1)S(1)}, u32[]{:S(2)}, u32[]{:S(2)}) collective-permute-start(bf16[2,48,128]{2,1,0:T(8,128)(2,1)S(1)} %dynamic-slice_bitcast_fusion.14), channel_id=1, source_target_pairs={{0,8},{2,10},{4,12},{6,14},{8,0},{10,2},{12,4},{14,6},{16,24},{18,... | collective-permute-start | bytes 73736 | tf_op jit(solution)/shard_map/ppermute | solution.py:592
  232.6 5.1 %collective-permute-start.19 = (bf16[48,384]{1,0:T(8,128)(2,1)S(1)}, bf16[48,384]{1,0:T(8,128)(2,1)S(1)}, u32[]{:S(2)}, u32[]{:S(2)}) collective-permute-start(bf16[48,384]{1,0:T(8,128)(2,1)S(1)} %dynamic-slice_bitcast_fusion.13), channel_id=1, source_target_pairs={{0,16},{2,18},{4,20},{6,22},{8,24},{10,26},{12,28},{14,30},{16,0},... | collective-permute-start | bytes 110600 | tf_op jit(solution)/shard_map/ppermute | solution.py:592
  235.2 4.7 %collective-permute-start.9 = (bf16[48,128]{1,0:T(8,128)(2,1)S(1)}, bf16[48,128]{1,0:T(8,128)(2,1)S(1)}, u32[]{:S(2)}, u32[]{:S(2)}) collective-permute-start(bf16[48,128]{1,0:T(8,128)(2,1)S(1)} %dynamic-slice_bitcast_fusion.15), channel_id=1, source_target_pairs={{0,16},{2,18},{4,20},{6,22},{8,24},{10,26},{12,28},{14,30},{16,0},... | collective-permute-start | bytes 36872 | tf_op jit(solution)/shard_map/ppermute | solution.py:592
  238.3 17.1 %collective-permute-start.10 = (bf16[768,1152]{1,0:T(8,128)(2,1)S(1)}, bf16[768,1152]{1,0:T(8,128)(2,1)}, u32[]{:S(2)}, u32[]{:S(2)}) collective-permute-start(bf16[768,1152]{1,0:T(8,128)(2,1)S(1)} %get-tuple-element.64), channel_id=1, source_target_pairs={{0,1},{1,0},{2,3},{3,2},{4,5},{5,4},{6,7},{7,6},{8,9},{9,8},{10,11... | collective-permute-start | bytes 5308424 | tf_op jit(solution)/shard_map/ppermute | solution.py:579
  244.2 2.1 copy-start.20
  245.3 27.1 %collective-permute-start.26 = (bf16[2,2,2,192,384]{4,3,0,1,2:T(8,128)(2,1)}, bf16[2,2,2,192,384]{4,3,0,1,2:T(8,128)(2,1)}, u32[]{:S(2)}, u32[]{:S(2)}) collective-permute-start(bf16[2,2,2,192,384]{4,3,0,1,2:T(8,128)(2,1)} %bitcast.126), channel_id=1, source_target_pairs={{0,2},{2,0},{4,6},{6,4},{8,10},{10,8},{12,14},{14,12},{16,18},{18,... | collective-permute-start | bytes 3538952 | tf_op jit(solution)/shard_map/ppermute | solution.py:592
  251.1 29.2 %collective-permute-start.21 = (bf16[2,2,2,48,1536]{4,3,0,1,2:T(8,128)(2,1)}, bf16[2,2,2,48,1536]{4,3,0,1,2:T(8,128)(2,1)}, u32[]{:S(2)}, u32[]{:S(2)}) collective-permute-start(bf16[2,2,2,48,1536]{4,3,0,1,2:T(8,128)(2,1)} %bitcast.127), channel_id=1, source_target_pairs={{0,4},{2,6},{4,0},{6,2},{8,12},{10,14},{12,8},{14,10},{16,20},{18,... | collective-permute-start | bytes 3538952 | tf_op jit(solution)/shard_map/ppermute | solution.py:592
  255.4 17.1 %copy-start.18 = (bf16[2,2,2,1,192,384]{5,4,3,2,1,0:T(8,128)(2,1)S(1)}, bf16[2,2,2,1,192,384]{5,4,3,2,1,0:T(8,128)(2,1)}, u32[]{:S(2)}) copy-start(bf16[2,2,2,1,192,384]{5,4,3,2,1,0:T(8,128)(2,1)} %get-tuple-element.87) | copy-start | bytes 3538948
  272.4 7.9 %copy-start.19 = (bf16[2,2,1,2,48,1536]{5,4,3,2,1,0:T(8,128)(2,1)S(1)}, bf16[2,2,1,2,48,1536]{5,4,3,2,1,0:T(8,128)(2,1)}, u32[]{:S(2)}) copy-start(bf16[2,2,1,2,48,1536]{5,4,3,2,1,0:T(8,128)(2,1)} %get-tuple-element.89) | copy-start | bytes 3538948
  274.3 16.5 %collective-permute-start.27 = (bf16[2,2,192,384]{3,2,0,1:T(8,128)(2,1)S(1)}, bf16[2,2,192,384]{3,2,0,1:T(8,128)(2,1)S(1)}, u32[]{:S(2)}, u32[]{:S(2)}) collective-permute-start(bf16[2,2,192,384]{3,2,0,1:T(8,128)(2,1)S(1)} %dynamic-slice_bitcast_fusion), channel_id=1, source_target_pairs={{0,4},{2,6},{4,0},{6,2},{8,12},{10,14},{12,8},{14,10},{16,20},{18,... | collective-permute-start | bytes 1769480 | tf_op jit(solution)/shard_map/ppermute | solution.py:592
  281.9 16.3 %collective-permute-start.22 = (bf16[2,2,48,1536]{3,2,0,1:T(8,128)(2,1)S(1)}, bf16[2,2,48,1536]{3,2,0,1:T(8,128)(2,1)S(1)}, u32[]{:S(2)}, u32[]{:S(2)}) collective-permute-start(bf16[2,2,48,1536]{3,2,0,1:T(8,128)(2,1)S(1)} %dynamic-slice_bitcast_fusion.1), channel_id=1, source_target_pairs={{0,2},{2,0},{4,6},{6,4},{8,10},{10,8},{12,14},{14,12},{16,18},{18,... | collective-permute-start | bytes 1769480 | tf_op jit(solution)/shard_map/ppermute | solution.py:592
  283.3 28.8 %collective-permute-start.11 = (bf16[2,2,2,48,1152]{4,3,0,1,2:T(8,128)(2,1)S(1)}, bf16[2,2,2,48,1152]{4,3,0,1,2:T(8,128)(2,1)S(1)}, u32[]{:S(2)}, u32[]{:S(2)}) collective-permute-start(bf16[2,2,2,48,1152]{4,3,0,1,2:T(8,128)(2,1)S(1)} %bitcast.137), channel_id=1, source_target_pairs={{0,2},{2,0},{4,6},{6,4},{8,10},{10,8},{12,14},{14,12},{16,18},{18,... | collective-permute-start | bytes 2654216 | tf_op jit(solution)/shard_map/ppermute | solution.py:592
  290.9 23.0 %collective-permute-start.28 = (bf16[2,192,384]{2,1,0:T(8,128)(2,1)S(1)}, bf16[2,192,384]{2,1,0:T(8,128)(2,1)S(1)}, u32[]{:S(2)}, u32[]{:S(2)}) collective-permute-start(bf16[2,192,384]{2,1,0:T(8,128)(2,1)S(1)} %dynamic-slice_bitcast_fusion.3), channel_id=1, source_target_pairs={{0,8},{2,10},{4,12},{6,14},{8,0},{10,2},{12,4},{14,6},{16,24},{18,... | collective-permute-start | bytes 884744 | tf_op jit(solution)/shard_map/ppermute | solution.py:592
  298.4 18.1 %collective-permute-start.23 = (bf16[2,48,1536]{2,1,0:T(8,128)(2,1)S(1)}, bf16[2,48,1536]{2,1,0:T(8,128)(2,1)S(1)}, u32[]{:S(2)}, u32[]{:S(2)}) collective-permute-start(bf16[2,48,1536]{2,1,0:T(8,128)(2,1)S(1)} %dynamic-slice_bitcast_fusion.4), channel_id=1, source_target_pairs={{0,8},{2,10},{4,12},{6,14},{8,0},{10,2},{12,4},{14,6},{16,24},{18,... | collective-permute-start | bytes 884744 | tf_op jit(solution)/shard_map/ppermute | solution.py:592
  312.3 8.4 %collective-permute-start.12 = (bf16[2,2,48,1152]{3,2,0,1:T(8,128)(2,1)S(1)}, bf16[2,2,48,1152]{3,2,0,1:T(8,128)(2,1)S(1)}, u32[]{:S(2)}, u32[]{:S(2)}) collective-permute-start(bf16[2,2,48,1152]{3,2,0,1:T(8,128)(2,1)S(1)} %dynamic-slice_bitcast_fusion.2), channel_id=1, source_target_pairs={{0,4},{2,6},{4,0},{6,2},{8,12},{10,14},{12,8},{14,10},{16,20},{18,... | collective-permute-start | bytes 1327112 | tf_op jit(solution)/shard_map/ppermute | solution.py:592
  314.1 16.7 %collective-permute-start.29 = (bf16[192,384]{1,0:T(8,128)(2,1)S(1)}, bf16[192,384]{1,0:T(8,128)(2,1)S(1)}, u32[]{:S(2)}, u32[]{:S(2)}) collective-permute-start(bf16[192,384]{1,0:T(8,128)(2,1)S(1)} %dynamic-slice_bitcast_fusion.6), channel_id=1, source_target_pairs={{0,16},{2,18},{4,20},{6,22},{8,24},{10,26},{12,28},{14,30},{16,0},... | collective-permute-start | bytes 442376 | tf_op jit(solution)/shard_map/ppermute | solution.py:592
  316.6 8.7 %collective-permute-start.24 = (bf16[48,1536]{1,0:T(8,128)(2,1)S(1)}, bf16[48,1536]{1,0:T(8,128)(2,1)S(1)}, u32[]{:S(2)}, u32[]{:S(2)}) collective-permute-start(bf16[48,1536]{1,0:T(8,128)(2,1)S(1)} %dynamic-slice_bitcast_fusion.7), channel_id=1, source_target_pairs={{0,16},{2,18},{4,20},{6,22},{8,24},{10,26},{12,28},{14,30},{16,0},... | collective-permute-start | bytes 442376 | tf_op jit(solution)/shard_map/ppermute | solution.py:592
  320.9 6.1 %collective-permute-start.13 = (bf16[2,48,1152]{2,1,0:T(8,128)(2,1)S(1)}, bf16[2,48,1152]{2,1,0:T(8,128)(2,1)S(1)}, u32[]{:S(2)}, u32[]{:S(2)}) collective-permute-start(bf16[2,48,1152]{2,1,0:T(8,128)(2,1)S(1)} %dynamic-slice_bitcast_fusion.5), channel_id=1, source_target_pairs={{0,8},{2,10},{4,12},{6,14},{8,0},{10,2},{12,4},{14,6},{16,24},{18,... | collective-permute-start | bytes 663560 | tf_op jit(solution)/shard_map/ppermute | solution.py:592
  327.0 7.6 %collective-permute-start.14 = (bf16[48,1152]{1,0:T(8,128)(2,1)S(1)}, bf16[48,1152]{1,0:T(8,128)(2,1)S(1)}, u32[]{:S(2)}, u32[]{:S(2)}) collective-permute-start(bf16[48,1152]{1,0:T(8,128)(2,1)S(1)} %dynamic-slice_bitcast_fusion.9), channel_id=1, source_target_pairs={{0,16},{2,18},{4,20},{6,22},{8,24},{10,26},{12,28},{14,30},{16,0},... | collective-permute-start | bytes 331784 | tf_op jit(solution)/shard_map/ppermute | solution.py:592
where the time goes:
time: 337 us; the launch traced here: 335 us
  Pallas kernels  163 us (48%)
  waiting for transfers between devices  62.6 us (19%)
  local copies, waits for them, and re-layouts  45 us (13%)
  starting transfers between devices  42.2 us (13%)
  other arithmetic  21.6 us (6%)
    ppermute x20, waiting for transfers between devices, halve(): lax.ppermute(pick(x, 1 - mine, axis), 'dp', [(i, i ^ 1 << bit) for i in r...  61.9 us
    pallas_call x1, Pallas kernels, mlp(): pl.pallas_call(functools.partial(mlp_kernel, blocks, rows, slices), out_s...  57.6 us
    pallas_call x1, Pallas kernels, attend_backward(): pl.pallas_call(functools.partial(attend_bwd_kernel, fills, steps, BQ, BK)...  50.6 us
    ppermute x20, starting transfers between devices, halve(): lax.ppermute(pick(x, 1 - mine, axis), 'dp', [(i, i ^ 1 << bit) for i in r...  40 us
    pallas_call x1, Pallas kernels, attend_forward(): pl.pallas_call(functools.partial(attend_fwd_kernel, fills, BQ, BK), out_s...  33.7 us
    unnamed x57, local copies, waits for them, and re-layouts  20.7 us
    convert_element_type x5, other arithmetic, join_band(): return (own.astype(f32) + swap_band(far).astype(f32)).astype(bf16)  9.56 us
    pallas_call x1, Pallas kernels, qkv_grads(): pl.pallas_call(functools.partial(qkv_grad_kernel, blocks, rows), out_shap...  9.21 us
  transfers between devices with their start and end apart: 30, of which 16 were waited for; matrix products, arithmetic and copies ran while one was open for 13% of the time, Pallas kernels for 20%

commit v1 on v0

--- a/solution.py
+++ b/solution.py
@@ -575,12 +575,297 @@
     )(packed, tokens, rgrad, w_qkv, gain.reshape(1, -1))
 
 
+MESH = pl.DeviceIdType.MESH
+
+
+def add_low(dst, a, b):
+    dst[...] = (a[...].astype(f32) + b[...].astype(f32)).astype(bf16)
+
+
+def finish_kernel(
+    dq_hbm, dko_hbm, dkf_hbm, dvo_hbm, dvf_hbm, n_hbm, tok_hbm, rgrad_hbm, w_hbm, downo_hbm, downf_hbm, upo_hbm, upf_hbm,
+    projo_hbm, projf_hbm, gain, msums, usums,
+    out_hbm, down_out, up_out, qkv_out, proj_out, vec_out,
+    packed, dko, dko_in, dvo, dvo_in, n1, tok, rgrad, wq, down, down_in, up, up_in, proj, proj_in, far, far_in, tail,
+    one_d, one_u, one_t, two_d, two_u, two_t, thr_d, thr_u, thr_t, vec, vec_band, vec_x, vec_y, vec_z,
+    load_sem, store_sem, swap_send, swap_recv, send, recv, vsend, vrecv,
+):
+    me = lax.axis_index("dp")
+    band = lax.axis_index("band")
+    x, y, z = me & 1, (me >> 1) & 1, me >> 2
+    rows, width = tok.shape
+    half = far.shape[-1]
+    peer_band = (me, 1 - band)
+    peer_x = (me ^ 1, band)
+    peer_y = (me ^ 2, band)
+    peers_z = [(((z + d) & 3) * 4 + (me & 3), band) for d in (1, 2, 3)]
+
+    def load(t, src, dst):
+        copy = pltpu.make_async_copy(src, dst, load_sem.at[t])
+        copy.start()
+        return copy
+
+    loads = {
+        "down": (load(0, downo_hbm, down), load(1, downf_hbm, down_in)),
+        "up": (load(2, upo_hbm, up), load(3, upf_hbm, up_in)),
+        "keys": (load(4, dko_hbm, dko), load(5, dvo_hbm, dvo), load(6, dq_hbm, packed.at[:, 0:width])),
+        "normed": (load(7, n_hbm, n1),),
+        "proj": (load(8, projo_hbm, proj), load(9, projf_hbm, proj_in)),
+        "weight": (load(10, w_hbm, wq),),
+        "rows": (load(11, tok_hbm, tok), load(12, rgrad_hbm, rgrad)),
+    }
+
+    def ready(name):
+        for copy in loads[name]:
+            copy.wait()
+
+    barrier = pltpu.get_barrier_semaphore()
+    for peer in (peer_band, peer_x, peer_y, *peers_z):
+        pl.semaphore_signal(barrier, inc=1, device_id=peer, device_id_type=MESH)
+    pl.semaphore_wait(barrier, 6)
+
+    pending = []
+
+    def push(src, dst, peer, s, r):
+        copy = pltpu.make_async_remote_copy(src_ref=src, dst_ref=dst, send_sem=s, recv_sem=r, device_id=peer, device_id_type=MESH)
+        copy.start()
+        pending.append(copy)
+        return copy
+
+    swap_k = push(dkf_hbm, dko_in, peer_band, swap_send.at[0], swap_recv.at[0])
+    swap_v = push(dvf_hbm, dvo_in, peer_band, swap_send.at[1], swap_recv.at[1])
+
+    def each_shard(body):
+        def step(s, c):
+            body(s >> 2, (s >> 1) & 1, s & 1)
+            return c
+
+        lax.fori_loop(0, 16, step, 0)
+
+    def first_stage(t, work, one, cut):
+        a, b = cut
+        return (
+            push(work.at[:, :, 1 - x, a[0], a[1]], one.at[0], peer_x, send.at[t, 0, 0], recv.at[t, 0, 0]),
+            push(work.at[:, 1 - y, :, b[0], b[1]], one.at[1], peer_y, send.at[t, 1, 0], recv.at[t, 1, 0]),
+        )
+
+    def second_stage(t, work, one, two, cut, copies):
+        a, b = cut
+        copies[0].wait_recv()
+
+        def sum_a(s, c):
+            zz, yy = s >> 1, s & 1
+            add_low(one.at[0, zz, yy], one.at[0, zz, yy], work.at[zz, yy, x, a[0], a[1]])
+            return c
+
+        lax.fori_loop(0, 8, sum_a, 0)
+        first = push(one.at[0, :, 1 - y], two.at[0], peer_y, send.at[t, 0, 1], recv.at[t, 0, 1])
+        copies[1].wait_recv()
+
+        def sum_b(s, c):
+            zz, xx = s >> 1, s & 1
+            add_low(one.at[1, zz, xx], one.at[1, zz, xx], work.at[zz, y, xx, b[0], b[1]])
+            return c
+
+        lax.fori_loop(0, 8, sum_b, 0)
+        return first, push(one.at[1, :, 1 - x], two.at[1], peer_x, send.at[t, 1, 1], recv.at[t, 1, 1])
+
+    def third_stage(t, one, two, three, copies):
+        out = []
+        for piece, mine in ((0, y), (1, x)):
+            copies[piece].wait_recv()
+
+            def total(zz, c, piece=piece, mine=mine):
+                add_low(two.at[piece, zz], two.at[piece, zz], one.at[piece, zz, mine])
+                return c
+
+            lax.fori_loop(0, 4, total, 0)
+            for d in (1, 2, 3):
+                out.append(
+                    push(two.at[piece, (z + d) & 3], three.at[piece, d - 1], peers_z[d - 1], send.at[t, piece, 1 + d], recv.at[t, piece, 1 + d])
+                )
+        return out
+
+    def last(two, three, copies, piece):
+        for d in range(3):
+            copies[3 * piece + d].wait_recv()
+        total = two[piece, z].astype(f32)
+        for d in range(3):
+            total = total + three[piece, d].astype(f32)
+        return total
+
+    everything = slice(None)
+    down_cut = ((slice(0, 96), everything), (slice(96, 192), everything))
+    wide_cut = ((everything, slice(0, 768)), (everything, slice(768, 1536)))
+
+    ready("down")
+    each_shard(lambda i, j, k: add_low(down.at[i, j, k], down.at[i, j, k], down_in.at[i, j, k]))
+    d_one = first_stage(0, down, one_d, down_cut)
+    ready("up")
+    each_shard(lambda i, j, k: add_low(up.at[i, j, k], up.at[i, j, k], up_in.at[i, j, k]))
+    u_one = first_stage(1, up, one_u, wide_cut)
+
+    ready("keys")
+    swap_k.wait_recv()
+    swap_v.wait_recv()
+
+    def turn(i, c):
+        here = pl.ds(pl.multiple_of(i * 256, 256), 256)
+        for t, (own, other) in enumerate(((dko, dko_in), (dvo, dvo_in))):
+            for p in range(width // 128):
+                at = slice(p * 128, (p + 1) * 128)
+                turned = (own[at, here].astype(f32) + other[at, here].astype(f32)).astype(bf16).T
+                packed[here, (t + 1) * width + p * 128 : (t + 1) * width + (p + 1) * 128] = turned
+        return c
+
+    lax.fori_loop(0, rows // 256, turn, 0)
+    ready("normed")
+
+    def columns(which):
+        at = pl.ds(pl.multiple_of(which * half, 128), half)
+        return mm(n1[...], packed[:, at], TN).astype(bf16).reshape(far.shape)
+
+    far[...] = columns(1 - band)
+    swap_far = push(far, far_in, peer_band, swap_send.at[2], swap_recv.at[2])
+    tail[:, :, :, :, 0:half] = columns(band)
+    ready("proj")
+    each_shard(lambda i, j, k: add_low(tail.at[i, j, k, :, half : 2 * width], proj.at[i, j, k], proj_in.at[i, j, k]))
+    swap_far.wait_recv()
+    each_shard(lambda i, j, k: add_low(tail.at[i, j, k, :, 0:half], tail.at[i, j, k, :, 0:half], far_in.at[i, j, k]))
+    t_one = first_stage(2, tail, one_t, wide_cut)
+    d_two = second_stage(0, down, one_d, two_d, down_cut, d_one)
+    u_two = second_stage(1, up, one_u, two_u, wide_cut, u_one)
+
+    ready("weight")
+    ready("rows")
+    vec[...] = jnp.zeros(vec.shape, f32)
+
+    def rows_back(i, c):
+        here = pl.ds(pl.multiple_of(i * 256, 256), 256)
+        e = mm(packed[here, :], wq[...], NT)
+        xhat, scale = normalize(tok[here, :])
+        vec[0:1, :] = vec[0:1, :] + jnp.sum(e * xhat, axis=0, keepdims=True)
+        vec[1:2, :] = vec[1:2, :] + jnp.sum(e, axis=0, keepdims=True)
+        vec[2:3, :] = vec[2:3, :] + jnp.sum(packed[here, 0:width].astype(f32), axis=0, keepdims=True)
+        vec[3:4, :] = vec[3:4, :] + jnp.sum(packed[here, 2 * width : 3 * width].astype(f32), axis=0, keepdims=True)
+        f = e * gain[...]
+        back = scale * (f - jnp.mean(f, axis=-1, keepdims=True) - xhat * jnp.mean(f * xhat, axis=-1, keepdims=True))
+        rgrad[here, :] = rgrad[here, :] + back
+        return c
+
+    lax.fori_loop(0, rows // 256, rows_back, 0)
+    store = pltpu.make_async_copy(rgrad, out_hbm, store_sem)
+    store.start()
+    vec[4:8, :] = msums[0:4, :]
+    for t in range(usums.shape[1] // width):
+        vec[8 + t : 9 + t, :] = usums[0:1, t * width : (t + 1) * width]
+    v_band = push(vec, vec_band, peer_band, vsend.at[0], vrecv.at[0])
+    d_three = third_stage(0, one_d, two_d, thr_d, d_two)
+    v_band.wait()
+    vec_band[...] = vec[...] + vec_band[...]
+    v_x = push(vec_band, vec_x, peer_x, vsend.at[1], vrecv.at[1])
+    u_three = third_stage(1, one_u, two_u, thr_u, u_two)
+    v_x.wait()
+    vec_x[...] = vec_band[...] + vec_x[...]
+    v_y = push(vec_x, vec_y, peer_y, vsend.at[2], vrecv.at[2])
+    t_two = second_stage(2, tail, one_t, two_t, wide_cut, t_one)
+    v_y.wait()
+    vec_y[...] = vec_x[...] + vec_y[...]
+    v_z = [push(vec_y, vec_z.at[d], peers_z[d], vsend.at[3 + d], vrecv.at[3 + d]) for d in range(3)]
+    t_three = third_stage(2, one_t, two_t, thr_t, t_two)
+    down_out[0:96, :] = last(two_d, thr_d, d_three, 0)
+    down_out[96:192, :] = last(two_d, thr_d, d_three, 1)
+    up_out[:, 0:768] = last(two_u, thr_u, u_three, 0)
+    up_out[:, 768:1536] = last(two_u, thr_u, u_three, 1)
+    for copy in v_z:
+        copy.wait_recv()
+    vec_out[...] = vec_y[...] + vec_z[0] + vec_z[1] + vec_z[2]
+    qkv_out[:, 0:768] = last(two_t, thr_t, t_three, 0)
+    final = last(two_t, thr_t, t_three, 1)
+    qkv_out[:, 768:half] = final[:, 0 : half - 768]
+    proj_out[...] = final[:, half - 768 :]
+    done = {id(c) for c in (v_band, v_x, v_y)}
+    for copy in pending:
+        if id(copy) not in done:
+            copy.wait_send()
+    store.wait()
+
+
+def finish(dq, dk_own, dk_far, dv_own, dv_far, normed, tokens, rgrad, w_qkv, down, up, proj, gain, msums, usums):
+    rows, width = tokens.shape
+    ff = usums.shape[1]
+    half = 3 * width // 2
+    shards = (4, 2, 2)
+    d_shape, u_shape, p_shape = shards + (ff // 16, width // 2), shards + (width // 16, ff // 2), shards + (width // 16, width // 2)
+    q_shape = shards + (width // 16, half)
+    down_own, down_far = (a.reshape(d_shape) for a in down)
+    up_own, up_far = (a.reshape(u_shape) for a in up)
+    proj_own, proj_far = (a.reshape(p_shape) for a in proj)
+    d_piece, w_piece = (ff // 32, width // 2), (width // 16, ff // 4)
+    hbm, vmem = pl.BlockSpec(memory_space=pl.ANY), pl.BlockSpec(memory_space=pltpu.VMEM)
+    shape = jax.ShapeDtypeStruct
+    low = lambda *s: pltpu.VMEM(s, bf16)
+    dma = pltpu.SemaphoreType.DMA
+    return pl.pallas_call(
+        finish_kernel,
+        out_shape=(
+            shape((rows, width), f32),
+            shape((ff // 16, width // 2), f32),
+            shape((width // 16, ff // 2), f32),
+            shape((width // 16, half), f32),
+            shape((width // 16, width // 2), f32),
+            shape((16, width), f32),
+        ),
+        in_specs=[hbm] * 15 + [vmem] * 3,
+        out_specs=[hbm] + [vmem] * 5,
+        scratch_shapes=[
+            low(rows, 3 * width),
+            *([low(width, rows)] * 4),
+            low(rows, width),
+            pltpu.VMEM((rows, width), f32),
+            pltpu.VMEM((rows, width), f32),
+            low(width, 3 * width),
+            low(*d_shape),
+            low(*d_shape),
+            low(*u_shape),
+            low(*u_shape),
+            low(*p_shape),
+            low(*p_shape),
+            low(*q_shape),
+            low(*q_shape),
+            low(*u_shape),
+            low(2, 4, 2, *d_piece),
+            low(2, 4, 2, *w_piece),
+            low(2, 4, 2, *w_piece),
+            low(2, 4, *d_piece),
+            low(2, 4, *w_piece),
+            low(2, 4, *w_piece),
+            low(2, 3, *d_piece),
+            low(2, 3, *w_piece),
+            low(2, 3, *w_piece),
+            pltpu.VMEM((16, width), f32),
+            pltpu.VMEM((16, width), f32),
+            pltpu.VMEM((16, width), f32),
+            pltpu.VMEM((16, width), f32),
+            pltpu.VMEM((3, 16, width), f32),
+            dma((13,)),
+            dma,
+            dma((3,)),
+            dma((3,)),
+            dma((3, 2, 5)),
+            dma((3, 2, 5)),
+            dma((6,)),
+            dma((6,)),
+        ],
+        compiler_params=pltpu.CompilerParams(vmem_limit_bytes=60 * MIB, collective_id=0, has_side_effects=True),
+        cost_estimate=pl.CostEstimate(flops=20 * 10**9, bytes_accessed=40 * 10**6, transcendentals=0),
+        name="finish",
+    )(dq, dk_own, dk_far, dv_own, dv_far, normed, tokens, rgrad, w_qkv, down_own, down_far, up_own, up_far, proj_own, proj_far,
+      gain.reshape(1, -1), msums, usums)
+
+
 def swap_band(x):
     return lax.ppermute(x, "band", [(0, 1), (1, 0)])
-
-
-def join_band(own, far):
-    return (own.astype(f32) + swap_band(far).astype(f32)).astype(bf16)
 
 
 def pick(x, which, axis):
@@ -613,6 +898,34 @@
         while self.order:
             self.step()
         return self.x
+
+
+def finish_any(size, band_at, query_grad, dk_own, dk_far, dv_own, dv_far, normed, tokens, residual_grad, w_qkv, down, up, proj, gain, msums, usums):
+    width = tokens.shape[1]
+    rising = list(range(size.bit_length() - 1))
+    turned = [1, 0] + rising[2:]
+    packed, qkv_own, qkv_far, qkv_sums = qkv_grads(
+        band_at, query_grad, dk_own, swap_band(dk_far), dv_own, swap_band(dv_far), normed
+    )
+    input_grad, first_sums = input_grads(packed, tokens, residual_grad, w_qkv, gain)
+
+    def total(own, arrived, order):
+        return Reduction((own.astype(f32) + arrived.astype(f32)).astype(bf16), order, size).finish()
+
+    tall = jnp.concatenate([first_sums[:2], qkv_sums[:2], msums[:4]], axis=0)
+    thin = jnp.concatenate([tall.T, usums[0].reshape(width, -1)], axis=1)
+    thin = jnp.pad(thin, ((0, 0), (0, 128 - thin.shape[1]))).astype(bf16)
+    thin_sum = total(thin, swap_band(thin), turned)
+    ups = usums.shape[1] // width
+    return (
+        input_grad,
+        total(*down, rising),
+        total(*up, turned),
+        total(qkv_own, swap_band(qkv_far), rising),
+        total(*proj, turned),
+        [thin_sum[:, t] for t in range(8)],
+        thin_sum[:, 8 : 8 + ups].reshape(-1),
+    )
 
 
 def local(
@@ -636,9 +949,6 @@
 ):
     local_shape = inputs.shape
     width = local_shape[-1]
-    levels = size.bit_length() - 1
-    rising = list(range(levels))
-    turned = [1, 0] + list(range(2, levels))
     band = lax.axis_index("band")
     band_at = band.astype(jnp.int32).reshape(1)
     tokens = inputs.reshape(-1, width)
@@ -675,38 +985,38 @@
         up_bias,
         down_bias,
     )
-    down = Reduction(join_band(down_own, down_far), rising, size)
-    up = Reduction(join_band(up_own, up_far), turned, size)
+    down, up, proj = (down_own, swap_band(down_far)), (up_own, swap_band(up_far)), (proj_own, swap_band(proj_far))
     query_grad, dk_own, dk_far, dv_own, dv_far = attend_backward(
         band_at, queries, attended_grad, attended, log_totals, *keys
     )
-    packed, qkv_own, qkv_far, qkv_sums = qkv_grads(
-        band_at, query_grad, dk_own, swap_band(dk_far), dv_own, swap_band(dv_far), normed
-    )
-    input_grad, first_sums = input_grads(packed, tokens, residual_grad, w_qkv, first_gain)
-    proj = Reduction(join_band(proj_own, proj_far), turned, size)
-    qkv = Reduction(join_band(qkv_own, qkv_far), rising, size)
-    tall = jnp.concatenate([first_sums[:2], qkv_sums[:2], mlp_sums[:4]], axis=0)
-    thin = jnp.concatenate([tall.T, up_sums[0].reshape(width, -1)], axis=1)
-    thin = jnp.pad(thin, ((0, 0), (0, 128 - thin.shape[1]))).astype(bf16)
-    thin_sum = Reduction(join_band(thin, thin), turned, size).finish()
-    vectors = [thin_sum[:, t] for t in range(8)]
     ups = up_bias.shape[0] // width
+    if size == 16:
+        input_grad, down_sum, up_sum, qkv_sum, proj_sum, vec = finish(
+            query_grad, dk_own, dk_far, dv_own, dv_far, normed, tokens, residual_grad, w_qkv, down, up, proj, first_gain, mlp_sums, up_sums
+        )
+        shard = width // size
+        mine = lax.dynamic_slice_in_dim(vec[:8], lax.axis_index("dp") * shard, shard, 1)
+        vectors = [mine[t] for t in range(8)]
+        up_vector = lax.dynamic_slice_in_dim(vec[8 : 8 + ups].reshape(-1), lax.axis_index("dp") * ups * shard, ups * shard, 0)
+    else:
+        input_grad, down_sum, up_sum, qkv_sum, proj_sum, vectors, up_vector = finish_any(
+            size, band_at, query_grad, dk_own, dk_far, dv_own, dv_far, normed, tokens, residual_grad, w_qkv, down, up, proj, first_gain, mlp_sums, up_sums
+        )
     return (
         output.reshape(local_shape),
         input_grad.reshape(local_shape),
         vectors[0],
         vectors[1],
-        qkv.finish(),
+        qkv_sum,
         vectors[2],
         vectors[3],
-        proj.finish(),
+        proj_sum,
         vectors[7],
         vectors[5],
         vectors[6],
-        up.finish(),
-        thin_sum[:, 8 : 8 + ups].reshape(-1),
-        down.finish(),
+        up_sum,
+        up_vector,
+        down_sum,
         vectors[4],
     )
 

time: 337 us -> 278 us (0.82)
  Pallas kernels: 163 us -> 247 us
  waiting for transfers between devices: 62.6 us -> 0.02 us
  starting transfers between devices: 42.2 us -> 1.61 us
  other arithmetic: 21.6 us -> 1.42 us
  local copies, waits for them, and re-layouts: 45 us -> 25.2 us
    pallas_call x2 -> x1, Pallas kernels: 15.6 us -> 95.3 us  [finish(): pl.pallas_call(finish_kernel, out_shape=(shape((rows, width), f32), shape...]
    ppermute x20 -> x0, waiting for transfers between devices: 61.9 us -> none  [halve(): lax.ppermute(pick(x, 1 - mine, axis), 'dp', [(i, i ^ 1 << bit) for i in r...]
    ppermute x20 -> x0, starting transfers between devices: 40 us -> none  [halve(): lax.ppermute(pick(x, 1 - mine, axis), 'dp', [(i, i ^ 1 << bit) for i in r...]
    convert_element_type x20 -> x0, other arithmetic: 17.3 us -> none  [the longest x5 9.56 us: join_band(): return (own.astype(f32) + swap_band(far).astype(f32)).astype(bf16)]
    unnamed x57 -> x44, local copies, waits for them, and re-layouts: 20.7 us -> 15.2 us
    dynamic_slice x8 -> x2, local copies, waits for them, and re-layouts: 5.85 us -> 0.71 us  [the longest x1 0.64 us: local(): lax.dynamic_slice_in_dim(vec[8:8 + ups].reshape(-1), lax.axis_index('dp')...]
    pallas_call x1, Pallas kernels: 50.6 us -> 54 us  [attend_backward(): pl.pallas_call(functools.partial(attend_bwd_kernel, fills, steps, BQ, BK)...]
  transfers between devices with their start and end apart: 30 -> 6, of which waited for: 16 -> 0; matrix products, arithmetic and copies ran while one was open for 13% -> 2% of each run, Pallas kernels for 20% -> 20%
where the time goes in v1:
time: 278 us; the launch traced here: 276 us
  Pallas kernels  247 us (89%)
  local copies, waits for them, and re-layouts  25.2 us (9%)
    pallas_call x1, Pallas kernels, finish(): pl.pallas_call(finish_kernel, out_shape=(shape((rows, width), f32), shape...  95.3 us
    pallas_call x1, Pallas kernels, mlp(): pl.pallas_call(functools.partial(mlp_kernel, blocks, rows, slices), out_s...  57.3 us
    pallas_call x1, Pallas kernels, attend_backward(): pl.pallas_call(functools.partial(attend_bwd_kernel, fills, steps, BQ, BK)...  54 us
    pallas_call x1, Pallas kernels, attend_forward(): pl.pallas_call(functools.partial(attend_fwd_kernel, fills, BQ, BK), out_s...  35.3 us
    unnamed x44, local copies, waits for them, and re-layouts  15.2 us
  transfers between devices with their start and end apart: 6, of which 0 were waited for; matrix products, arithmetic and copies ran while one was open for 2% of the time, Pallas kernels for 20%

profile of v1, /device:TPU:0, one launch (start us, length us, event | category | flops | bytes accessed | tf_op | source)
XLA Modules:
  0.0 276.2 jit_solution(1574980098468344218)
XLA Ops:
  0.6 0.7 reshape.98.gain
  1.3 0.7 reshape.100.qbias
  2.0 0.7 reshape.101.vbias
  2.7 0.7 reshape.99.shift
  3.4 2.0 copy-done.1
  5.4 1.9 copy-done.2
  7.3 0.0 copy-start.15
  7.3 5.3 %project_qkv.1 = (bf16[1024,768]{1,0:T(8,128)(2,1)S(1)}, bf16[1024,768]{1,0:T(8,128)(2,1)S(1)}, bf16[1024,768]{1,0:T(8,128)(2,1)S(1)}, bf16[1024,768]{1,0:T(8,128)(2,1)S(1)}) custom-call(f32[1024,768]{1,0:T(8,128)S(1)} %bitcast.35, bf16[768,2304]{1,0:T(8,128)(2,1)S(1)} %copy-done.1, f32[1,768]{1,0:T(1,128)S(1)} %reshape.98.gain, ...), custom_call_target="tpu_custom_call" | custom-call | flops 4000000000 | bytes 13000000 | tf_op jit(solution)/shard_map/project_qkv/pallas_call | solution.py:465
  12.6 0.0 copy-done
  12.7 0.0 copy-start.5
  12.7 1.2 copy-done.5
  13.8 1.1 copy-done.6
  15.0 0.5 collective-permute-start.1
  15.4 0.1 collective-permute-start.2
  15.5 0.0 copy-done.11
  15.5 0.5 collective-permute-start
  15.9 0.6 broadcast.44
  16.5 0.7 reduce.3
  17.2 0.1 fusion.1
  17.3 0.1 copy.49
  17.4 0.1 copy.50
  17.4 1.0 copy.43.qseg_ref.seg_own
  18.5 0.0 copy-done.12
  18.5 0.6 reshape.103.pbias
  19.1 0.0 copy-done.13
  19.1 0.6 reshape.104.gain
  19.6 0.0 copy-done.14
  19.6 0.6 reshape.105.shift
  20.2 0.0 copy-done.15
  20.2 0.6 reshape.107.dbias
  20.8 0.0 collective-permute-done
  20.8 1.1 copy.45.seg_far
  21.9 0.2 convert_reduce_fusion.1
  22.1 0.5 subtract_minimum_fusion
  22.6 0.0 collective-permute-done.1.k_far
  22.7 0.0 collective-permute-done.2.v_far
  22.7 0.0 copy-done.3
  22.7 0.0 copy-done.4
  22.7 35.3 %attend_forward.1 = (bf16[1024,768]{1,0:T(8,128)(2,1)}, f32[1024,128]{1,0:T(8,128)}) custom-call(s32[4]{0:T(128)} %get-tuple-element.77.start_ref, s32[4]{0:T(128)} %get-tuple-element.78.count_ref, s32[1]{0:T(128)} %bitcast.band_ref, bf16[1024,768]{1,0:T(8,128)(2,1)} %copy-done.6, s32[1024,1]{1,0:T(8,128)} %copy.43.qseg_ref.seg_own, ...), custom_call_target="tpu_custom_call" | custom-call | flops 30000001024 | bytes 10000000 | tf_op jit(solution)/shard_map/attend_forward/pallas_call | solution.py:128
  58.0 57.3 %mlp.1 = (f32[1024,768]{1,0:T(8,128)}, f32[1024,768]{1,0:T(8,128)}, bf16[1024,768]{1,0:T(8,128)(2,1)}, bf16[3072,384]{1,0:T(8,128)(2,1)}, bf16[3072,384]{1,0:T(8...) custom-call(s32[1]{0:T(128)} %bitcast.band_ref, ...), custom_call_target="tpu_custom_call" | custom-call | flops 40000000000 | bytes 40000000 | tf_op jit(solution)/shard_map/mlp/pallas_call | solution.py:402
  115.2 0.1 collective-permute-start.3
  115.3 0.5 collective-permute-start.4
  115.8 0.1 collective-permute-start.5
  115.9 54.0 %attend_backward.1 = (bf16[1024,768]{1,0:T(8,128)(2,1)}, bf16[768,1024]{1,0:T(8,128)(2,1)}, bf16[768,1024]{1,0:T(8,128)(2,1)}, bf16[768,1024]{1,0:T(8,128)(2,1)}, bf16[768,1024]{1,0:T(8,128)(2,1)}) custom-call(s32[4]{0:T(128)} %get-tuple-element.77.start_ref, s32[4]{0:T(128)} %get-tuple-element.78.count_ref, s32[1]{0:T(128)} %bitcast.band_ref, ...), custom_call_target="tpu_custom_call" | custom-call | flops 44999999488 | bytes 20000000 | tf_op jit(solution)/shard_map/attend_backward/pallas_call | solution.py:242
  169.9 0.0 collective-permute-done.5
  169.9 0.0 copy-start.17
  170.0 0.0 collective-permute-done.3
  170.0 0.0 copy-start.16
  170.0 0.0 collective-permute-done.4
  170.0 0.8 copy-done.17
  170.8 0.8 copy-done.16
  171.6 95.3 %finish.1 = (f32[1024,768]{1,0:T(8,128)}, f32[192,384]{1,0:T(8,128)}, f32[48,1536]{1,0:T(8,128)}, f32[48,1152]{1,0:T(8,128)}, f32[48,384]{1,0:T(8,128)}, /*index=5*/f32[16,768]{1,0:T(8,128)}) custom-call(bf16[1024,768]{1,0:T(8,128)(2,1)} %get-tuple-element.50.dq_hbm, bf16[768,1024]{1,0:T(8,128)(2,1)} %get-tuple-element.51.dko_hbm, ...), custom_call_target="tpu_custom_call" | custom-call | flops 20000000000 | bytes 40000000 | tf_op jit(solution)/shard_map/finish/pallas_call | solution.py:809
  266.9 0.7 slice.38
  267.6 0.7 slice.46
  268.4 0.1 constant_dynamic-slice_fusion
  268.4 0.5 slice_bitcast_fusion
  269.0 0.6 dynamic_slice.7
  269.7 3.8 %copy.56 = f32[1,1024,768]{2,1,0:T(8,128)} copy(f32[1,1024,768]{2,1,0:T(8,128)} %bitcast.36) | data formatting | bytes 6291456
  273.5 0.0 copy-done.9
  273.5 0.7 copy.57
  274.2 0.0 copy-done.10
  274.2 0.6 copy.58
  274.8 0.7 copy.59
  275.5 0.7 copy.60
  (18 shorter events, 0.0 us)
Async XLA Ops:
  1.3 11.3 %copy-start = (f32[1,768]{1,0:T(1,128)}, f32[1,768]{1,0:T(1,128)S(1)}, u32[]{:S(2)}) copy-start(f32[1,768]{1,0:T(1,128)S(1)} %reshape.98.gain) | copy-start | bytes 9220
  3.4 2.0 copy-start.1
  5.4 1.9 copy-start.2
  7.3 8.2 %copy-start.11 = (s32[1,1024]{1,0:T(1,128)S(1)}, s32[1,1024]{1,0:T(1,128)}, u32[]{:S(2)}) copy-start(s32[1,1024]{1,0:T(1,128)} %param.17) | copy-start | bytes 12292
  7.3 11.2 %copy-start.12 = (f32[768]{0:T(1024)S(1)}, f32[768]{0:T(1024)}, u32[]{:S(2)}) copy-start(f32[768]{0:T(1024)} %param.25) | copy-start | bytes 9220
  7.3 11.8 %copy-start.13 = (f32[768]{0:T(1024)S(1)}, f32[768]{0:T(1024)}, u32[]{:S(2)}) copy-start(f32[768]{0:T(1024)} %param.26) | copy-start | bytes 9220
  7.3 12.3 %copy-start.14 = (f32[768]{0:T(1024)S(1)}, f32[768]{0:T(1024)}, u32[]{:S(2)}) copy-start(f32[768]{0:T(1024)} %param.27) | copy-start | bytes 9220
  7.3 12.9 %copy-start.15 = (f32[768]{0:T(1024)S(1)}, f32[768]{0:T(1024)}, u32[]{:S(2)}) copy-start(f32[768]{0:T(1024)} %param.31) | copy-start | bytes 9220
  12.7 1.2 copy-start.5
  13.8 1.1 copy-start.6
  15.0 7.7 %copy-start.3 = (bf16[1024,768]{1,0:T(8,128)(2,1)}, bf16[1024,768]{1,0:T(8,128)(2,1)S(1)}, u32[]{:S(2)}) copy-start(bf16[1024,768]{1,0:T(8,128)(2,1)S(1)} %get-tuple-element.44.k_own) | copy-start | bytes 4718596
  15.0 7.7 %copy-start.4 = (bf16[1024,768]{1,0:T(8,128)(2,1)}, bf16[1024,768]{1,0:T(8,128)(2,1)S(1)}, u32[]{:S(2)}) copy-start(bf16[1024,768]{1,0:T(8,128)(2,1)S(1)} %get-tuple-element.45.v_own) | copy-start | bytes 4718596
  15.0 7.7 %collective-permute-start.1 = (bf16[1024,768]{1,0:T(8,128)(2,1)S(1)}, bf16[1024,768]{1,0:T(8,128)(2,1)}, u32[]{:S(2)}, u32[]{:S(2)}) collective-permute-start(bf16[1024,768]{1,0:T(8,128)(2,1)S(1)} %get-tuple-element.44.k_own), channel_id=1, source_target_pairs={{0,1},{1,0},{2,3},{3,2},{4,5},{5,4},{6,7},{7,6},{8,9},{9,8},{10,11... | collective-permute-start | bytes 4718600 | tf_op jit(solution)/shard_map/ppermute | solution.py:868
  15.4 7.2 %collective-permute-start.2 = (bf16[1024,768]{1,0:T(8,128)(2,1)S(1)}, bf16[1024,768]{1,0:T(8,128)(2,1)}, u32[]{:S(2)}, u32[]{:S(2)}) collective-permute-start(bf16[1024,768]{1,0:T(8,128)(2,1)S(1)} %get-tuple-element.45.v_own), channel_id=1, source_target_pairs={{0,1},{1,0},{2,3},{3,2},{4,5},{5,4},{6,7},{7,6},{8,9},{9,8},{10,11... | collective-permute-start | bytes 4718600 | tf_op jit(solution)/shard_map/ppermute | solution.py:868
  15.5 5.3 %collective-permute-start = (s32[1024]{0:T(1024)S(1)}, s32[1024]{0:T(1024)S(1)}, u32[]{:S(2)}, u32[]{:S(2)}) collective-permute-start(s32[1024]{0:T(1024)S(1)} %bitcast.37), channel_id=1, source_target_pairs={{0,1},{1,0},{2,3},{3,2},{4,5},{5,4},{6,7},{7,6},{8,9},{9,8},{10,11... | collective-permute-start | bytes 12296 | tf_op jit(solution)/shard_map/ppermute | solution.py:868
  115.2 54.7 %collective-permute-start.3 = (bf16[3072,384]{1,0:T(8,128)(2,1)}, bf16[3072,384]{1,0:T(8,128)(2,1)S(1)}, u32[]{:S(2)}, u32[]{:S(2)}) collective-permute-start(bf16[3072,384]{1,0:T(8,128)(2,1)} %get-tuple-element.58), channel_id=1, source_target_pairs={{0,1},{1,0},{2,3},{3,2},{4,5},{5,4},{6,7},{7,6},{8,9},{9,8},{10,11... | collective-permute-start | bytes 7077896 | tf_op jit(solution)/shard_map/ppermute | solution.py:868
  115.3 54.7 %collective-permute-start.4 = (bf16[768,1536]{1,0:T(8,128)(2,1)}, bf16[768,1536]{1,0:T(8,128)(2,1)}, u32[]{:S(2)}, u32[]{:S(2)}) collective-permute-start(bf16[768,1536]{1,0:T(8,128)(2,1)} %get-tuple-element.60), channel_id=1, source_target_pairs={{0,1},{1,0},{2,3},{3,2},{4,5},{5,4},{6,7},{7,6},{8,9},{9,8},{10,11... | collective-permute-start | bytes 7077896 | tf_op jit(solution)/shard_map/ppermute | solution.py:868
  115.8 54.1 %collective-permute-start.5 = (bf16[768,384]{1,0:T(8,128)(2,1)}, bf16[768,384]{1,0:T(8,128)(2,1)S(1)}, u32[]{:S(2)}, u32[]{:S(2)}) collective-permute-start(bf16[768,384]{1,0:T(8,128)(2,1)} %get-tuple-element.62), channel_id=1, source_target_pairs={{0,1},{1,0},{2,3},{3,2},{4,5},{5,4},{6,7},{7,6},{8,9},{9,8},{10,11... | collective-permute-start | bytes 1769480 | tf_op jit(solution)/shard_map/ppermute | solution.py:868
  169.9 0.8 copy-start.17
  170.0 1.6 copy-start.16
  269.6 3.8 %copy-start.9 = (f32[48,1152]{1,0:T(8,128)S(1)}, f32[48,1152]{1,0:T(8,128)}, u32[]{:S(2)}) copy-start(f32[48,1152]{1,0:T(8,128)} %get-tuple-element.108) | copy-start | bytes 663556
  269.6 4.5 %copy-start.10 = (f32[48,384]{1,0:T(8,128)S(1)}, f32[48,384]{1,0:T(8,128)}, u32[]{:S(2)}) copy-start(f32[48,384]{1,0:T(8,128)} %get-tuple-element.111) | copy-start | bytes 221188
  269.6 5.2 %copy-start.8 = (f32[48,1536]{1,0:T(8,128)S(1)}, f32[48,1536]{1,0:T(8,128)}, u32[]{:S(2)}) copy-start(f32[48,1536]{1,0:T(8,128)} %get-tuple-element.115) | copy-start | bytes 884740
  269.6 5.9 %copy-start.7 = (f32[192,384]{1,0:T(8,128)S(1)}, f32[192,384]{1,0:T(8,128)}, u32[]{:S(2)}) copy-start(f32[192,384]{1,0:T(8,128)} %get-tuple-element.117) | copy-start | bytes 884740

commit v2 on v1

--- a/solution.py
+++ b/solution.py
@@ -281,6 +281,7 @@
     return jnp.minimum(lo, keys - count * BK), count
 
 
+MESH = pl.DeviceIdType.MESH
 TN = (((0,), (0,)), ((), ()))
 SLICE = 768
 ERFC_RATE = 0.39
@@ -310,12 +311,40 @@
     ref[at, :] = jnp.where(first, sums, ref[at, :] + sums)
 
 
-def mlp_kernel(blocks, rows, slices, band_ref, tok_ref, att_ref, cot_ref, wproj, wup, wdown, pbias, gain, shift, ubias, dbias,
-               out_ref, rgrad_ref, agrad_ref, down_own, down_far, up_own, up_far, proj_own, proj_far, sums_ref, usums_ref,
-               hid, ugr, n2s, bgs, ags, ats):
+def add_low(dst, a, b):
+    dst[...] = (a[...].astype(f32) + b[...].astype(f32)).astype(bf16)
+
+
+def mlp_kernel(sorted_out, blocks, rows, slices, tok_ref, att_ref, cot_ref, wproj, wup, wdown, pbias, gain, shift, ubias, dbias,
+               out_ref, rgrad_ref, agrad_ref, sums_ref, usums_ref, proj_out, *rest):
+    outs, scratch = rest[: 8 if sorted_out else 2], rest[8 if sorted_out else 2 :]
+    hid, ugr, n2s, bgs, ags, ats, d_own, d_far, d_in, u_in, p_own, p_far, p_in, send_sem, recv_sem = scratch
     i = pl.program_id(0)
-    band = band_ref[0]
-    half = down_own.shape[1]
+    me, band = lax.axis_index("dp"), lax.axis_index("band")
+    other = (me, 1 - band)
+    width = tok_ref.shape[1]
+    half, per_half = width // 2, slices // 2
+
+    def push(t, src, dst):
+        return pltpu.make_async_remote_copy(
+            src_ref=src, dst_ref=dst, send_sem=send_sem.at[t], recv_sem=recv_sem.at[t], device_id=other, device_id_type=MESH
+        )
+
+    def d_copy(j):
+        at = pl.ds(pl.multiple_of(j * SLICE, SLICE), SLICE)
+        return push(j, d_far.at[at, :], d_in.at[at, :])
+
+    def u_copy(c):
+        return push(slices + c, hid.at[0:width, pl.ds(pl.multiple_of(c * SLICE, SLICE), SLICE)], u_in.at[c])
+
+    def p_copy():
+        return push(slices + per_half, p_far, p_in)
+
+    @pl.when(i == 0)
+    def _():
+        barrier = pltpu.get_barrier_semaphore()
+        pl.semaphore_signal(barrier, inc=1, device_id=other, device_id_type=MESH)
+        pl.semaphore_wait(barrier, 1)
 
     @pl.when(i < blocks)
     def _():
@@ -351,127 +380,207 @@
         add_sums(sums_ref, 3, ag.astype(f32), first)
         agrad_ref[...] = mm(ag, wproj[...], NT).astype(bf16)
 
-    def columns(grad, own, far):
+    def columns(grad, own, far, at):
         left, right = grad[:, :half].astype(bf16), grad[:, half:].astype(bf16)
-        own[...] = jnp.where(band == 0, left, right)
-        far[...] = jnp.where(band == 0, right, left)
+        own[at, :] = jnp.where(band == 0, left, right)
+        far[at, :] = jnp.where(band == 0, right, left)
 
     @pl.when((i >= blocks) & (i < blocks + slices))
     def _():
-        at = pl.ds(pl.multiple_of((i - blocks) * SLICE, SLICE), SLICE)
-        columns(mm(hid[:, at], bgs[...], TN), down_own, down_far)
+        j = i - blocks
+        at = pl.ds(pl.multiple_of(j * SLICE, SLICE), SLICE)
+        columns(mm(hid[:, at], bgs[...], TN), d_own, d_far, at)
+        d_copy(j).start()
 
     def up_slice(which):
         at = pl.ds(pl.multiple_of(which * SLICE, SLICE), SLICE)
         return mm(n2s[...], ugr[:, at], TN).astype(bf16)
 
+    x, y = me & 1, (me >> 1) & 1
+
+    def join_down(j):
+        d_copy(j).wait_recv()
+        if not sorted_out:
+            at = pl.ds(pl.multiple_of(j * SLICE, SLICE), SLICE)
+            add_low(outs[0].at[at, :], d_own.at[at, :], d_in.at[at, :])
+            return
+        shard = SLICE // 4
+        piece = shard // 2
+        for t in range(2):
+            for out, x_bit, y_bit, first in (
+                (outs[0], 1 - x, t, 0),
+                (outs[1], x, t, 0),
+                (outs[2], t, 1 - y, piece),
+                (outs[3], t, y, piece),
+            ):
+                at = pl.ds(pl.multiple_of(j * SLICE + y_bit * 2 * shard + x_bit * shard + first, piece), piece)
+                add_low(out.at[j, t], d_own.at[at, :], d_in.at[at, :])
+
+    def join_up(c):
+        u_copy(c).wait_recv()
+        own = hid.at[0:width, (per_half + c) * SLICE : (per_half + c + 1) * SLICE]
+        if not sorted_out:
+            add_low(outs[1].at[:, c * SLICE : (c + 1) * SLICE], own, u_in.at[c])
+            return
+        shard = width // 16
+
+        def one(s, carry):
+            z, t = s >> 1, s & 1
+            for out, sends in ((outs[4 + 2 * c], 1), (outs[5 + 2 * c], 0)):
+                bit = (y if c else x) ^ sends
+                x_bit, y_bit = (t, bit) if c else (bit, t)
+                at = pl.ds(pl.multiple_of((z * 4 + y_bit * 2 + x_bit) * shard, shard), shard)
+                add_low(out.at[z, t], own.at[at, :], u_in.at[c, at, :])
+            return carry
+
+        lax.fori_loop(0, 8, one, 0)
+
     middle = blocks + slices
-    per_half = slices // 2
-
-    @pl.when((i >= middle) & (i < middle + per_half))
-    def _():
-        up_far[...] = up_slice((1 - band) * per_half + i - middle)
-
-    @pl.when((i >= middle + per_half) & (i < middle + slices))
-    def _():
-        up_own[...] = up_slice(band * per_half + i - middle - per_half)
+    for c in range(per_half):
+        at = slice(c * SLICE, (c + 1) * SLICE)
+
+        @pl.when(i == middle + c)
+        def _(c=c, at=at):
+            hid[0:width, at] = up_slice((1 - band) * per_half + c)
+            u_copy(c).start()
+            join_down(c)
+
+        @pl.when(i == middle + per_half + c)
+        def _(c=c):
+            hid[0:width, (per_half + c) * SLICE : (per_half + c + 1) * SLICE] = up_slice(band * per_half + c)
+            join_down(per_half + c)
 
     @pl.when(i == middle + slices)
     def _():
-        columns(mm(ats[...], ags[...], TN), proj_own, proj_far)
-
-
-def mlp(band, tokens, attended, cotangent, w_proj, w_up, w_down, proj_bias, gain, shift, up_bias, down_bias, rows=256):
+        columns(mm(ats[...], ags[...], TN), p_own, p_far, slice(None))
+        p_copy().start()
+        for c in range(per_half):
+            join_up(c)
+        p_copy().wait_recv()
+        add_low(proj_out, p_own, p_in)
+        for j in range(slices):
+            d_copy(j).wait_send()
+        for c in range(per_half):
+            u_copy(c).wait_send()
+        p_copy().wait_send()
+
+
+def mlp(size, tokens, attended, cotangent, w_proj, w_up, w_down, proj_bias, gain, shift, up_bias, down_bias, rows=256):
     count, width = tokens.shape
     ff = w_up.shape[1]
     blocks, slices = count // rows, ff // SLICE
     half, per_half = width // 2, slices // 2
+    sorted_out = size == 16
     one = pl.Buffered(1)
-    mine = lambda i, *_: (jnp.minimum(i, blocks - 1), 0)
-    whole = lambda i, *_: (0, 0)
-    down_at = lambda i, *_: (jnp.clip(i - blocks, 0, slices - 1), 0)
-    far_at = lambda i, *_: (0, jnp.clip(i - blocks - slices, 0, per_half - 1))
-    own_at = lambda i, *_: (0, jnp.clip(i - blocks - slices - per_half, 0, per_half - 1))
+    mine = lambda i: (jnp.minimum(i, blocks - 1), 0)
     block = pl.BlockSpec((rows, width), mine)
 
     def full(a):
-        return pl.BlockSpec(a.shape, whole, pipeline_mode=one)
+        return pl.BlockSpec(a.shape, lambda i: (0,) * len(a.shape), pipeline_mode=one)
 
     vectors = [v.reshape(1, -1) for v in (proj_bias, gain, shift, up_bias, down_bias)]
     shape = jax.ShapeDtypeStruct
+    if sorted_out:
+        pieces = [shape((4, 2, ff // 32, half), bf16)] * 4 + [shape((4, 2, width // 16, ff // 4), bf16)] * 4
+    else:
+        pieces = [shape((ff, half), bf16), shape((width, ff // 2), bf16)]
+    kept = [shape((8, width), f32), shape((8, ff), f32), shape((width, half), bf16)] + pieces
+    low = lambda *s: pltpu.VMEM(s, bf16)
+    copies = slices + per_half + 1
     return pl.pallas_call(
-        functools.partial(mlp_kernel, blocks, rows, slices),
-        out_shape=(
-            shape((count, width), f32),
-            shape((count, width), f32),
-            shape((count, width), bf16),
-            shape((ff, half), bf16),
-            shape((ff, half), bf16),
-            shape((width, ff // 2), bf16),
-            shape((width, ff // 2), bf16),
-            shape((width, half), bf16),
-            shape((width, half), bf16),
-            shape((8, width), f32),
-            shape((8, ff), f32),
-        ),
-        grid_spec=pltpu.PrefetchScalarGridSpec(
-            num_scalar_prefetch=1,
-            grid=(blocks + 2 * slices + 1,),
-            in_specs=[block, block, block] + [full(a) for a in (w_proj, w_up, w_down, *vectors)],
-            out_specs=[
-                block,
-                block,
-                block,
-                pl.BlockSpec((SLICE, half), down_at),
-                pl.BlockSpec((SLICE, half), down_at),
-                pl.BlockSpec((width, SLICE), own_at),
-                pl.BlockSpec((width, SLICE), far_at),
-                pl.BlockSpec((width, half), whole, pipeline_mode=one),
-                pl.BlockSpec((width, half), whole, pipeline_mode=one),
-                pl.BlockSpec((8, width), whole, pipeline_mode=one),
-                pl.BlockSpec((8, ff), whole, pipeline_mode=one),
-            ],
-            scratch_shapes=[
-                pltpu.VMEM((count, ff), bf16),
-                pltpu.VMEM((count, ff), bf16),
-                pltpu.VMEM((count, width), bf16),
-                pltpu.VMEM((count, width), bf16),
-                pltpu.VMEM((count, width), bf16),
-                pltpu.VMEM((count, width), bf16),
-            ],
-        ),
-        compiler_params=pltpu.CompilerParams(vmem_limit_bytes=58 * MIB),
+        functools.partial(mlp_kernel, sorted_out, blocks, rows, slices),
+        out_shape=[shape((count, width), f32), shape((count, width), f32), shape((count, width), bf16)] + kept,
+        grid=(blocks + 2 * slices + 1,),
+        in_specs=[block, block, block] + [full(a) for a in (w_proj, w_up, w_down, *vectors)],
+        out_specs=[block, block, block] + [full(a) for a in kept],
+        scratch_shapes=[
+            low(count, ff),
+            low(count, ff),
+            *([low(count, width)] * 4),
+            *([low(ff, half)] * 3),
+            low(per_half, width, SLICE),
+            *([low(width, half)] * 3),
+            pltpu.SemaphoreType.DMA((copies,)),
+            pltpu.SemaphoreType.DMA((copies,)),
+        ],
+        compiler_params=pltpu.CompilerParams(vmem_limit_bytes=62 * MIB, collective_id=1, has_side_effects=True),
         cost_estimate=pl.CostEstimate(flops=40 * 10**9, bytes_accessed=40 * 10**6, transcendentals=0),
         name="mlp",
-    )(band, tokens, attended, cotangent, w_proj, w_up, w_down, *vectors)
-
-
-def qkv_kernel(tok_ref, w_ref, gain, shift, qbias, vbias, q_ref, k_ref, v_ref, n_ref):
-    width = tok_ref.shape[1]
+    )(tokens, attended, cotangent, w_proj, w_up, w_down, *vectors)
+
+
+def qkv_kernel(tok_ref, seg_ref, w_ref, gain, shift, qbias, vbias, q_ref, k_ref, v_ref, n_ref, k_far, v_far, seg_far,
+               k_all, v_all, send_sem, recv_sem):
+    i = pl.program_id(0)
+    last = pl.num_programs(0) - 1
+    other = (lax.axis_index("dp"), 1 - lax.axis_index("band"))
+    rows, width = tok_ref.shape
+
+    def push(t, src, dst):
+        return pltpu.make_async_remote_copy(
+            src_ref=src, dst_ref=dst, send_sem=send_sem.at[t], recv_sem=recv_sem.at[t], device_id=other, device_id_type=MESH
+        )
+
+    def copies(j):
+        at = pl.ds(pl.multiple_of(j * rows, rows), rows)
+        return push(2 * j, k_all.at[at, :], k_far.at[at, :]), push(2 * j + 1, v_all.at[at, :], v_far.at[at, :])
+
+    segs = push(send_sem.shape[0] - 1, seg_ref, seg_far)
+
+    @pl.when(i == 0)
+    def _():
+        barrier = pltpu.get_barrier_semaphore()
+        pl.semaphore_signal(barrier, inc=1, device_id=other, device_id_type=MESH)
+        pl.semaphore_wait(barrier, 1)
+        segs.start()
+
+    here = pl.ds(pl.multiple_of(i * rows, rows), rows)
     xhat, _ = normalize(tok_ref[...])
     n1 = (xhat * gain[...] + shift[...]).astype(bf16)
     n_ref[...] = n1
-    k_ref[...] = mm(n1, w_ref[:, width : 2 * width]).astype(bf16)
-    v_ref[...] = (mm(n1, w_ref[:, 2 * width :]) + vbias[...]).astype(bf16)
+    k = mm(n1, w_ref[:, width : 2 * width]).astype(bf16)
+    k_ref[...] = k
+    k_all[here, :] = k
+    v = (mm(n1, w_ref[:, 2 * width :]) + vbias[...]).astype(bf16)
+    v_ref[...] = v
+    v_all[here, :] = v
+    for copy in copies(i):
+        copy.start()
     q = (mm(n1, w_ref[:, :width]) + qbias[...]).astype(bf16)
     q_ref[...] = q * jnp.asarray(HEAD_DIM**-0.5, bf16)
 
-
-def project_qkv(tokens, w_qkv, gain, shift, query_bias, value_bias, rows=256):
+    @pl.when(i == last)
+    def _():
+        segs.wait()
+        for j in range(k_all.shape[0] // rows):
+            for copy in copies(j):
+                copy.wait()
+
+
+def project_qkv(tokens, seg, w_qkv, gain, shift, query_bias, value_bias, rows=256):
     count, width = tokens.shape
     one = pl.Buffered(1)
     block = pl.BlockSpec((rows, width), lambda i: (i, 0))
     vectors = [v.reshape(1, -1) for v in (gain, shift, query_bias, value_bias)]
+    hbm = pl.BlockSpec(memory_space=pl.ANY)
+    steps = count // rows
+    low = jax.ShapeDtypeStruct((count, width), bf16)
     return pl.pallas_call(
         qkv_kernel,
-        out_shape=(jax.ShapeDtypeStruct((count, width), bf16),) * 4,
-        grid=(count // rows,),
-        in_specs=[block] + [pl.BlockSpec(a.shape, lambda i: (0, 0), pipeline_mode=one) for a in (w_qkv, *vectors)],
-        out_specs=[block] * 4,
-        compiler_params=pltpu.CompilerParams(vmem_limit_bytes=32 * MIB),
+        out_shape=(low,) * 6 + (jax.ShapeDtypeStruct(seg.shape, seg.dtype),),
+        grid=(steps,),
+        in_specs=[block, hbm] + [pl.BlockSpec(a.shape, lambda i: (0, 0), pipeline_mode=one) for a in (w_qkv, *vectors)],
+        out_specs=[block] * 4 + [hbm] * 3,
+        scratch_shapes=[
+            pltpu.VMEM((count, width), bf16),
+            pltpu.VMEM((count, width), bf16),
+            pltpu.SemaphoreType.DMA((2 * steps + 1,)),
+            pltpu.SemaphoreType.DMA((2 * steps + 1,)),
+        ],
+        compiler_params=pltpu.CompilerParams(vmem_limit_bytes=60 * MIB, collective_id=2, has_side_effects=True),
         cost_estimate=pl.CostEstimate(flops=4 * 10**9, bytes_accessed=13 * 10**6, transcendentals=0),
         name="project_qkv",
-    )(tokens, w_qkv, *vectors)
+    )(tokens, seg, w_qkv, *vectors)
 
 
 def qkv_grad_kernel(blocks, rows, band_ref, dq_ref, dk_own, dk_far, dv_own, dv_far, n_ref, packed_ref, own_ref, far_ref, sums_ref, packed):
@@ -575,18 +684,11 @@
     )(packed, tokens, rgrad, w_qkv, gain.reshape(1, -1))
 
 
-MESH = pl.DeviceIdType.MESH
-
-
-def add_low(dst, a, b):
-    dst[...] = (a[...].astype(f32) + b[...].astype(f32)).astype(bf16)
-
-
 def finish_kernel(
-    dq_hbm, dko_hbm, dkf_hbm, dvo_hbm, dvf_hbm, n_hbm, tok_hbm, rgrad_hbm, w_hbm, downo_hbm, downf_hbm, upo_hbm, upf_hbm,
-    projo_hbm, projf_hbm, gain, msums, usums,
+    dq_hbm, dko_hbm, dkf_hbm, dvo_hbm, dvf_hbm, n_hbm, tok_hbm, rgrad_hbm, w_hbm, dak_hbm, dar_hbm, dbk_hbm, dbr_hbm,
+    uak_hbm, uar_hbm, ubk_hbm, ubr_hbm, proj_hbm, gain, msums, usums,
     out_hbm, down_out, up_out, qkv_out, proj_out, vec_out,
-    packed, dko, dko_in, dvo, dvo_in, n1, tok, rgrad, wq, down, down_in, up, up_in, proj, proj_in, far, far_in, tail,
+    packed, dko, dko_in, dvo, dvo_in, n1, tok, rgrad, wq, down, up, proj, far, far_in, tail,
     one_d, one_u, one_t, two_d, two_u, two_t, thr_d, thr_u, thr_t, vec, vec_band, vec_x, vec_y, vec_z,
     load_sem, store_sem, swap_send, swap_recv, send, recv, vsend, vrecv,
 ):
@@ -606,11 +708,11 @@
         return copy
 
     loads = {
-        "down": (load(0, downo_hbm, down), load(1, downf_hbm, down_in)),
-        "up": (load(2, upo_hbm, up), load(3, upf_hbm, up_in)),
+        "down": (load(0, dak_hbm, down.at[0]), load(1, dar_hbm, one_d.at[0]), load(2, dbk_hbm, down.at[1]), load(3, dbr_hbm, one_d.at[1])),
+        "up": (load(13, uak_hbm, up.at[0]), load(14, uar_hbm, one_u.at[0]), load(15, ubk_hbm, up.at[1]), load(16, ubr_hbm, one_u.at[1])),
         "keys": (load(4, dko_hbm, dko), load(5, dvo_hbm, dvo), load(6, dq_hbm, packed.at[:, 0:width])),
         "normed": (load(7, n_hbm, n1),),
-        "proj": (load(8, projo_hbm, proj), load(9, projf_hbm, proj_in)),
+        "proj": (load(8, proj_hbm, proj),),
         "weight": (load(10, w_hbm, wq),),
         "rows": (load(11, tok_hbm, tok), load(12, rgrad_hbm, rgrad)),
     }
@@ -634,6 +736,9 @@
 
     swap_k = push(dkf_hbm, dko_in, peer_band, swap_send.at[0], swap_recv.at[0])
     swap_v = push(dvf_hbm, dvo_in, peer_band, swap_send.at[1], swap_recv.at[1])
+
+    def put(dst, src):
+        dst[...] = src[...]
 
     def each_shard(body):
         def step(s, c):
@@ -649,26 +754,19 @@
             push(work.at[:, 1 - y, :, b[0], b[1]], one.at[1], peer_y, send.at[t, 1, 0], recv.at[t, 1, 0]),
         )
 
-    def second_stage(t, work, one, two, cut, copies):
-        a, b = cut
-        copies[0].wait_recv()
-
-        def sum_a(s, c):
-            zz, yy = s >> 1, s & 1
-            add_low(one.at[0, zz, yy], one.at[0, zz, yy], work.at[zz, yy, x, a[0], a[1]])
-            return c
-
-        lax.fori_loop(0, 8, sum_a, 0)
-        first = push(one.at[0, :, 1 - y], two.at[0], peer_y, send.at[t, 0, 1], recv.at[t, 0, 1])
-        copies[1].wait_recv()
-
-        def sum_b(s, c):
-            zz, xx = s >> 1, s & 1
-            add_low(one.at[1, zz, xx], one.at[1, zz, xx], work.at[zz, y, xx, b[0], b[1]])
-            return c
-
-        lax.fori_loop(0, 8, sum_b, 0)
-        return first, push(one.at[1, :, 1 - x], two.at[1], peer_x, send.at[t, 1, 1], recv.at[t, 1, 1])
+    def second_stage(t, kept, one, two, copies):
+        out = []
+        for piece, mine, peer in ((0, y, peer_y), (1, x, peer_x)):
+            if copies is not None:
+                copies[piece].wait_recv()
+
+            def total(s, c, piece=piece):
+                add_low(one.at[piece, s >> 1, s & 1], one.at[piece, s >> 1, s & 1], kept(piece, s >> 1, s & 1))
+                return c
+
+            lax.fori_loop(0, 8, total, 0)
+            out.append(push(one.at[piece, :, 1 - mine], two.at[piece], peer, send.at[t, piece, 1], recv.at[t, piece, 1]))
+        return out
 
     def third_stage(t, one, two, three, copies):
         out = []
@@ -695,15 +793,15 @@
         return total
 
     everything = slice(None)
-    down_cut = ((slice(0, 96), everything), (slice(96, 192), everything))
     wide_cut = ((everything, slice(0, 768)), (everything, slice(768, 1536)))
 
     ready("down")
-    each_shard(lambda i, j, k: add_low(down.at[i, j, k], down.at[i, j, k], down_in.at[i, j, k]))
-    d_one = first_stage(0, down, one_d, down_cut)
+    d_two = second_stage(0, lambda p, i, j: down.at[p, i, j], one_d, two_d, None)
     ready("up")
-    each_shard(lambda i, j, k: add_low(up.at[i, j, k], up.at[i, j, k], up_in.at[i, j, k]))
-    u_one = first_stage(1, up, one_u, wide_cut)
+    u_two = second_stage(1, lambda p, i, j: up.at[p, i, j], one_u, two_u, None)
+
+    def tail_kept(piece, zz, t):
+        return tail.at[zz, t, x, :, 0:768] if piece == 0 else tail.at[zz, y, t, :, 768:1536]
 
     ready("keys")
     swap_k.wait_recv()
@@ -729,12 +827,12 @@
     swap_far = push(far, far_in, peer_band, swap_send.at[2], swap_recv.at[2])
     tail[:, :, :, :, 0:half] = columns(band)
     ready("proj")
-    each_shard(lambda i, j, k: add_low(tail.at[i, j, k, :, half : 2 * width], proj.at[i, j, k], proj_in.at[i, j, k]))
+    each_shard(lambda i, j, k: put(tail.at[i, j, k, :, half : 2 * width], proj.at[i, j, k]))
     swap_far.wait_recv()
     each_shard(lambda i, j, k: add_low(tail.at[i, j, k, :, 0:half], tail.at[i, j, k, :, 0:half], far_in.at[i, j, k]))
     t_one = first_stage(2, tail, one_t, wide_cut)
-    d_two = second_stage(0, down, one_d, two_d, down_cut, d_one)
-    u_two = second_stage(1, up, one_u, two_u, wide_cut, u_one)
+    d_three = third_stage(0, one_d, two_d, thr_d, d_two)
+    u_three = third_stage(1, one_u, two_u, thr_u, u_two)
 
     ready("weight")
     ready("rows")
@@ -760,15 +858,13 @@
     for t in range(usums.shape[1] // width):
         vec[8 + t : 9 + t, :] = usums[0:1, t * width : (t + 1) * width]
     v_band = push(vec, vec_band, peer_band, vsend.at[0], vrecv.at[0])
-    d_three = third_stage(0, one_d, two_d, thr_d, d_two)
     v_band.wait()
     vec_band[...] = vec[...] + vec_band[...]
     v_x = push(vec_band, vec_x, peer_x, vsend.at[1], vrecv.at[1])
-    u_three = third_stage(1, one_u, two_u, thr_u, u_two)
     v_x.wait()
     vec_x[...] = vec_band[...] + vec_x[...]
     v_y = push(vec_x, vec_y, peer_y, vsend.at[2], vrecv.at[2])
-    t_two = second_stage(2, tail, one_t, two_t, wide_cut, t_one)
+    t_two = second_stage(2, tail_kept, one_t, two_t, t_one)
     v_y.wait()
     vec_y[...] = vec_x[...] + vec_y[...]
     v_z = [push(vec_y, vec_z.at[d], peers_z[d], vsend.at[3 + d], vrecv.at[3 + d]) for d in range(3)]
@@ -791,16 +887,13 @@
     store.wait()
 
 
-def finish(dq, dk_own, dk_far, dv_own, dv_far, normed, tokens, rgrad, w_qkv, down, up, proj, gain, msums, usums):
+def finish(dq, dk_own, dk_far, dv_own, dv_far, normed, tokens, rgrad, w_qkv, pieces, proj, gain, msums, usums):
     rows, width = tokens.shape
     ff = usums.shape[1]
     half = 3 * width // 2
     shards = (4, 2, 2)
-    d_shape, u_shape, p_shape = shards + (ff // 16, width // 2), shards + (width // 16, ff // 2), shards + (width // 16, width // 2)
+    u_shape, p_shape = shards + (width // 16, ff // 2), shards + (width // 16, width // 2)
     q_shape = shards + (width // 16, half)
-    down_own, down_far = (a.reshape(d_shape) for a in down)
-    up_own, up_far = (a.reshape(u_shape) for a in up)
-    proj_own, proj_far = (a.reshape(p_shape) for a in proj)
     d_piece, w_piece = (ff // 32, width // 2), (width // 16, ff // 4)
     hbm, vmem = pl.BlockSpec(memory_space=pl.ANY), pl.BlockSpec(memory_space=pltpu.VMEM)
     shape = jax.ShapeDtypeStruct
@@ -816,7 +909,7 @@
             shape((width // 16, width // 2), f32),
             shape((16, width), f32),
         ),
-        in_specs=[hbm] * 15 + [vmem] * 3,
+        in_specs=[hbm] * 18 + [vmem] * 3,
         out_specs=[hbm] + [vmem] * 5,
         scratch_shapes=[
             low(rows, 3 * width),
@@ -825,11 +918,8 @@
             pltpu.VMEM((rows, width), f32),
             pltpu.VMEM((rows, width), f32),
             low(width, 3 * width),
-            low(*d_shape),
-            low(*d_shape),
-            low(*u_shape),
-            low(*u_shape),
-            low(*p_shape),
+            low(2, 4, 2, *d_piece),
+            low(2, 4, 2, *w_piece),
             low(*p_shape),
             low(*q_shape),
             low(*q_shape),
@@ -848,7 +938,7 @@
             pltpu.VMEM((16, width), f32),
             pltpu.VMEM((16, width), f32),
             pltpu.VMEM((3, 16, width), f32),
-            dma((13,)),
+            dma((17,)),
             dma,
             dma((3,)),
             dma((3,)),
@@ -860,7 +950,7 @@
         compiler_params=pltpu.CompilerParams(vmem_limit_bytes=60 * MIB, collective_id=0, has_side_effects=True),
         cost_estimate=pl.CostEstimate(flops=20 * 10**9, bytes_accessed=40 * 10**6, transcendentals=0),
         name="finish",
-    )(dq, dk_own, dk_far, dv_own, dv_far, normed, tokens, rgrad, w_qkv, down_own, down_far, up_own, up_far, proj_own, proj_far,
+    )(dq, dk_own, dk_far, dv_own, dv_far, normed, tokens, rgrad, w_qkv, *pieces, proj.reshape(p_shape),
       gain.reshape(1, -1), msums, usums)
 
 
@@ -900,7 +990,7 @@
         return self.x
 
 
-def finish_any(size, band_at, query_grad, dk_own, dk_far, dv_own, dv_far, normed, tokens, residual_grad, w_qkv, down, up, proj, gain, msums, usums):
+def finish_any(size, band_at, query_grad, dk_own, dk_far, dv_own, dv_far, normed, tokens, residual_grad, w_qkv, pieces, proj, gain, msums, usums):
     width = tokens.shape[1]
     rising = list(range(size.bit_length() - 1))
     turned = [1, 0] + rising[2:]
@@ -909,20 +999,23 @@
     )
     input_grad, first_sums = input_grads(packed, tokens, residual_grad, w_qkv, gain)
 
-    def total(own, arrived, order):
-        return Reduction((own.astype(f32) + arrived.astype(f32)).astype(bf16), order, size).finish()
+    def total(x, order):
+        return Reduction(x, order, size).finish()
+
+    def join(own, far):
+        return (own.astype(f32) + swap_band(far).astype(f32)).astype(bf16)
 
     tall = jnp.concatenate([first_sums[:2], qkv_sums[:2], msums[:4]], axis=0)
     thin = jnp.concatenate([tall.T, usums[0].reshape(width, -1)], axis=1)
     thin = jnp.pad(thin, ((0, 0), (0, 128 - thin.shape[1]))).astype(bf16)
-    thin_sum = total(thin, swap_band(thin), turned)
+    thin_sum = total(join(thin, thin), turned)
     ups = usums.shape[1] // width
     return (
         input_grad,
-        total(*down, rising),
-        total(*up, turned),
-        total(qkv_own, swap_band(qkv_far), rising),
-        total(*proj, turned),
+        total(pieces[0], rising),
+        total(pieces[1], turned),
+        total(join(qkv_own, qkv_far), rising),
+        total(proj, turned),
         [thin_sum[:, t] for t in range(8)],
         thin_sum[:, 8 : 8 + ups].reshape(-1),
     )
@@ -953,26 +1046,14 @@
     band_at = band.astype(jnp.int32).reshape(1)
     tokens = inputs.reshape(-1, width)
     seg_own = segment_ids.reshape(-1)
-    seg_far = swap_band(seg_own)
+    queries, k_own, v_own, normed, k_far, v_far, seg_far = project_qkv(
+        tokens, seg_own, w_qkv, first_gain, first_bias, query_bias, value_bias
+    )
     start, count = key_windows(seg_own, seg_far, band)
-    queries, k_own, v_own, normed = project_qkv(tokens, w_qkv, first_gain, first_bias, query_bias, value_bias)
-    k_far, v_far = swap_band(k_own), swap_band(v_own)
     keys = (seg_own[:, None], seg_far[:, None], k_own, k_far, v_own, v_far, start, count)
     attended, log_totals = attend_forward(band_at, queries, *keys)
-    (
-        output,
-        residual_grad,
-        attended_grad,
-        down_own,
-        down_far,
-        up_own,
-        up_far,
-        proj_own,
-        proj_far,
-        mlp_sums,
-        up_sums,
-    ) = mlp(
-        band_at,
+    output, residual_grad, attended_grad, mlp_sums, up_sums, proj, *pieces = mlp(
+        size,
         tokens,
         attended,
         cotangent.reshape(-1, width),
@@ -985,14 +1066,20 @@
         up_bias,
         down_bias,
     )
-    down, up, proj = (down_own, swap_band(down_far)), (up_own, swap_band(up_far)), (proj_own, swap_band(proj_far))
+    if size == 16:
+        turns = [[(i, i ^ bit) for i in range(size)] for bit in (1, 2)]
+        pieces = [
+            part
+            for t in range(4)
+            for part in (pieces[2 * t + 1], lax.ppermute(pieces[2 * t], "dp", turns[t % 2]))
+        ]
     query_grad, dk_own, dk_far, dv_own, dv_far = attend_backward(
         band_at, queries, attended_grad, attended, log_totals, *keys
     )
     ups = up_bias.shape[0] // width
     if size == 16:
         input_grad, down_sum, up_sum, qkv_sum, proj_sum, vec = finish(
-            query_grad, dk_own, dk_far, dv_own, dv_far, normed, tokens, residual_grad, w_qkv, down, up, proj, first_gain, mlp_sums, up_sums
+            query_grad, dk_own, dk_far, dv_own, dv_far, normed, tokens, residual_grad, w_qkv, pieces, proj, first_gain, mlp_sums, up_sums
         )
         shard = width // size
         mine = lax.dynamic_slice_in_dim(vec[:8], lax.axis_index("dp") * shard, shard, 1)
@@ -1000,7 +1087,7 @@
         up_vector = lax.dynamic_slice_in_dim(vec[8 : 8 + ups].reshape(-1), lax.axis_index("dp") * ups * shard, ups * shard, 0)
     else:
         input_grad, down_sum, up_sum, qkv_sum, proj_sum, vectors, up_vector = finish_any(
-            size, band_at, query_grad, dk_own, dk_far, dv_own, dv_far, normed, tokens, residual_grad, w_qkv, down, up, proj, first_gain, mlp_sums, up_sums
+            size, band_at, query_grad, dk_own, dk_far, dv_own, dv_far, normed, tokens, residual_grad, w_qkv, pieces, proj, first_gain, mlp_sums, up_sums
         )
     return (
         output.reshape(local_shape),

time: 278 us -> 256 us (0.921)
  Pallas kernels: 247 us -> 225 us
  starting transfers between devices: 1.61 us -> 4.6 us
    pallas_call x1, Pallas kernels: 95.3 us -> 63 us  [finish(): pl.pallas_call(finish_kernel, out_shape=(shape((rows, width), f32), shape...]
    pallas_call x2, Pallas kernels: 62.6 us -> 72.5 us  [the longest x1 60 us: mlp(): pl.pallas_call(functools.partial(mlp_kernel, sorted_out, blocks, rows, sl...]
    unnamed x44 -> x39, local copies, waits for them, and re-layouts: 15.2 us -> 9.5 us
    ppermute x6 -> x4, starting transfers between devices: 1.61 us -> 4.6 us  [local(): lax.ppermute(pieces[2 * t], 'dp', turns[t % 2])]
  transfers between devices with their start and end apart: 6 -> 4, of which waited for: 0 -> 0; matrix products, arithmetic and copies ran while one was open for 2% -> 0% of each run, Pallas kernels for 20% -> 21%
where the time goes in v2:
time: 256 us; the launch traced here: 255 us
  Pallas kernels  225 us (88%)
  local copies, waits for them, and re-layouts  22.5 us (9%)
  starting transfers between devices  4.6 us (2%)
  other arithmetic  2.79 us (1%)
    pallas_call x1, Pallas kernels, finish(): pl.pallas_call(finish_kernel, out_shape=(shape((rows, width), f32), shape...  63 us
    pallas_call x1, Pallas kernels, mlp(): pl.pallas_call(functools.partial(mlp_kernel, sorted_out, blocks, rows, sl...  60 us
    pallas_call x1, Pallas kernels, attend_backward(): pl.pallas_call(functools.partial(attend_bwd_kernel, fills, steps, BQ, BK)...  54.1 us
    pallas_call x1, Pallas kernels, attend_forward(): pl.pallas_call(functools.partial(attend_fwd_kernel, fills, BQ, BK), out_s...  35.1 us
    pallas_call x1, Pallas kernels, project_qkv(): pl.pallas_call(qkv_kernel, out_shape=(low,) * 6 + (jax.ShapeDtypeStruct(s...  12.5 us
    unnamed x39, local copies, waits for them, and re-layouts  9.5 us
  transfers between devices with their start and end apart: 4, of which 0 were waited for; matrix products, arithmetic and copies ran while one was open for 0% of the time, Pallas kernels for 21%

profile of v2, /device:TPU:0, one launch (start us, length us, event | category | flops | bytes accessed | tf_op | source)
XLA Modules:
  0.0 255.4 jit_solution(1826942105050882132)
XLA Ops:
  0.6 1.3 reshape.82.gain
  1.9 1.3 reshape.83.shift
  3.2 1.3 reshape.84.qbias
  4.5 1.3 reshape.85.vbias
  5.7 0.5 broadcast.44
  6.2 1.3 reduce.3
  7.6 0.1 fusion.1
  7.7 0.1 copy.49
  7.8 0.1 copy.50
  7.8 0.0 copy-start.6
  7.8 0.0 copy-start.7
  7.9 0.0 copy-start.8
  7.9 0.0 copy-start.10
  7.9 12.5 %project_qkv.1 = (bf16[1024,768]{1,0:T(8,128)(2,1)}, bf16[1024,768]{1,0:T(8,128)(2,1)}, bf16[1024,768]{1,0:T(8,128)(2,1)}, bf16[1024,768]{1,0:T(8,128)(2,1)}, bf...) custom-call(f32[1024,768]{1,0:T(8,128)} %bitcast.37, s32[1024]{0:T(1024)} %bitcast.30, ...), custom_call_target="tpu_custom_call" | custom-call | flops 4000000000 | bytes 13000000 | tf_op jit(solution)/shard_map/project_qkv/pallas_call | solution.py:568
  20.4 1.7 copy.45.seg_far
  22.1 0.0 copy-done.6
  22.1 1.0 copy.43.qseg_ref.seg_own
  23.2 0.0 copy-done.7
  23.2 0.6 reshape.88.pbias
  23.8 0.0 copy-done.8
  23.8 0.6 reshape.89.gain
  24.3 0.0 copy-done.9
  24.3 0.6 reshape.90.shift
  24.9 0.0 copy-done.10
  24.9 0.6 reshape.92.dbias
  25.5 0.9 convert_reduce_fusion.1
  26.4 0.5 subtract_minimum_fusion
  27.0 35.1 %attend_forward.1 = (bf16[1024,768]{1,0:T(8,128)(2,1)}, f32[1024,128]{1,0:T(8,128)}) custom-call(s32[4]{0:T(128)} %get-tuple-element.89.start_ref, s32[4]{0:T(128)} %get-tuple-element.90.count_ref, s32[1]{0:T(128)} %bitcast.4.band_ref, bf16[1024,768]{1,0:T(8,128)(2,1)} %get-tuple-element.50.q_ref, s32[1024,1]{1,0:T(8,128)} %copy.43.qseg_ref.seg_own, ...), custom_call_target="tpu_custom_call" | custom-call | flops 30000001024 | bytes 10000000 | tf_op jit(solution)/shard_map/attend_forward/pallas_call | solution.py:128
  62.1 60.0 %mlp.1 = (f32[1024,768]{1,0:T(8,128)}, f32[1024,768]{1,0:T(8,128)}, bf16[1024,768]{1,0:T(8,128)(2,1)}, f32[8,768]{1,0:T(8,128)}, f32[8,3072]{1,0:T(8,128)}, /*in...) custom-call(f32[1024,768]{1,0:T(8,128)} %bitcast.38, ...), custom_call_target="tpu_custom_call" | custom-call | flops 40000000000 | bytes 40000000 | tf_op jit(solution)/shard_map/mlp/pallas_call | solution.py:490
  122.1 1.6 collective-permute-start
  123.7 2.8 %collective-permute-start.1 = (bf16[4,2,96,384]{3,2,1,0:T(8,128)(2,1)}, bf16[4,2,96,384]{3,2,1,0:T(8,128)(2,1)S(1)}, u32[]{:S(2)}, u32[]{:S(2)}) collective-permute-start(bf16[4,2,96,384]{3,2,1,0:T(8,128)(2,1)} %get-tuple-element.69), channel_id=1, source_target_pairs={{0,4},{2,6},{4,0},{6,2},{8,12},{10,14},{12,8},{14,10},{16,20},{18,... | collective-permute-start | bytes 1769480 | tf_op jit(solution)/shard_map/ppermute | solution.py:1074
  126.5 0.1 collective-permute-start.2
  126.6 0.1 collective-permute-start.3
  126.7 54.1 %attend_backward.1 = (bf16[1024,768]{1,0:T(8,128)(2,1)}, bf16[768,1024]{1,0:T(8,128)(2,1)}, bf16[768,1024]{1,0:T(8,128)(2,1)}, bf16[768,1024]{1,0:T(8,128)(2,1)}, bf16[768,1024]{1,0:T(8,128)(2,1)}) custom-call(s32[4]{0:T(128)} %get-tuple-element.89.start_ref, s32[4]{0:T(128)} %get-tuple-element.90.count_ref, s32[1]{0:T(128)} %bitcast.4.band_ref, ...), custom_call_target="tpu_custom_call" | custom-call | flops 44999999488 | bytes 20000000 | tf_op jit(solution)/shard_map/attend_backward/pallas_call | solution.py:242
  180.8 0.0 collective-permute-done.dar_hbm
  180.8 0.0 copy-start.11
  180.9 0.0 collective-permute-done.1.dbr_hbm
  180.9 0.0 copy-start.12
  180.9 0.0 collective-permute-done.2.uar_hbm
  180.9 0.0 copy-start.13
  180.9 0.0 collective-permute-done.3.ubr_hbm
  180.9 0.0 copy-start.14
  180.9 0.7 copy-done.11
  181.7 0.2 copy-done.12
  181.9 0.2 copy-done.13
  182.1 0.2 copy-done.14
  182.2 63.0 %finish.1 = (f32[1024,768]{1,0:T(8,128)}, f32[192,384]{1,0:T(8,128)}, f32[48,1536]{1,0:T(8,128)}, f32[48,1152]{1,0:T(8,128)}, f32[48,384]{1,0:T(8,128)}, /*index=5*/f32[16,768]{1,0:T(8,128)}) custom-call(bf16[1024,768]{1,0:T(8,128)(2,1)} %get-tuple-element.59.dq_hbm, bf16[768,1024]{1,0:T(8,128)(2,1)} %get-tuple-element.60.dko_hbm, ...), custom_call_target="tpu_custom_call" | custom-call | flops 20000000000 | bytes 40000000 | tf_op jit(solution)/shard_map/finish/pallas_call | solution.py:902
  245.2 0.7 slice.38
  246.0 0.7 slice.46
  246.7 0.1 constant_dynamic-slice_fusion
  246.8 0.5 slice_bitcast_fusion
  247.3 0.6 dynamic_slice.7
  248.0 0.0 copy-done
  248.0 1.7 copy.57
  249.7 1.4 copy-done.1
  251.0 1.7 copy.58
  252.7 0.0 copy-done.4
  252.7 0.7 copy.59
  253.4 0.0 copy-done.5
  253.4 0.6 copy.60
  254.0 0.0 copy-done.3
  254.0 0.7 copy.61
  254.7 0.0 copy-done.2
  254.7 0.7 copy.62
  (9 shorter events, 0.0 us)
Async XLA Ops:
  7.8 14.3 %copy-start.6 = (s32[1,1024]{1,0:T(1,128)S(1)}, s32[1,1024]{1,0:T(1,128)}, u32[]{:S(2)}) copy-start(s32[1,1024]{1,0:T(1,128)} %param.17) | copy-start | bytes 12292
  7.8 15.3 %copy-start.7 = (f32[768]{0:T(1024)S(1)}, f32[768]{0:T(1024)}, u32[]{:S(2)}) copy-start(f32[768]{0:T(1024)} %param.25) | copy-start | bytes 9220
  7.9 15.9 %copy-start.8 = (f32[768]{0:T(1024)S(1)}, f32[768]{0:T(1024)}, u32[]{:S(2)}) copy-start(f32[768]{0:T(1024)} %param.26) | copy-start | bytes 9220
  7.9 16.5 %copy-start.9 = (f32[768]{0:T(1024)S(1)}, f32[768]{0:T(1024)}, u32[]{:S(2)}) copy-start(f32[768]{0:T(1024)} %param.27) | copy-start | bytes 9220
  7.9 17.1 %copy-start.10 = (f32[768]{0:T(1024)S(1)}, f32[768]{0:T(1024)}, u32[]{:S(2)}) copy-start(f32[768]{0:T(1024)} %param.31) | copy-start | bytes 9220
  122.1 58.8 %collective-permute-start = (bf16[4,2,96,384]{3,2,1,0:T(8,128)(2,1)}, bf16[4,2,96,384]{3,2,1,0:T(8,128)(2,1)S(1)}, u32[]{:S(2)}, u32[]{:S(2)}) collective-permute-start(bf16[4,2,96,384]{3,2,1,0:T(8,128)(2,1)} %get-tuple-element.67), channel_id=1, source_target_pairs={{0,2},{2,0},{4,6},{6,4},{8,10},{10,8},{12,14},{14,12},{16,18},{18,... | collective-permute-start | bytes 1769480 | tf_op jit(solution)/shard_map/ppermute | solution.py:1074
  123.7 57.1 %collective-permute-start.1 = (bf16[4,2,96,384]{3,2,1,0:T(8,128)(2,1)}, bf16[4,2,96,384]{3,2,1,0:T(8,128)(2,1)S(1)}, u32[]{:S(2)}, u32[]{:S(2)}) collective-permute-start(bf16[4,2,96,384]{3,2,1,0:T(8,128)(2,1)} %get-tuple-element.69), channel_id=1, source_target_pairs={{0,4},{2,6},{4,0},{6,2},{8,12},{10,14},{12,8},{14,10},{16,20},{18,... | collective-permute-start | bytes 1769480 | tf_op jit(solution)/shard_map/ppermute | solution.py:1074
  126.5 54.4 %collective-permute-start.2 = (bf16[4,2,48,768]{3,2,1,0:T(8,128)(2,1)}, bf16[4,2,48,768]{3,2,1,0:T(8,128)(2,1)S(1)}, u32[]{:S(2)}, u32[]{:S(2)}) collective-permute-start(bf16[4,2,48,768]{3,2,1,0:T(8,128)(2,1)} %get-tuple-element.71), channel_id=1, source_target_pairs={{0,2},{2,0},{4,6},{6,4},{8,10},{10,8},{12,14},{14,12},{16,18},{18,... | collective-permute-start | bytes 1769480 | tf_op jit(solution)/shard_map/ppermute | solution.py:1074
  126.6 54.3 %collective-permute-start.3 = (bf16[4,2,48,768]{3,2,1,0:T(8,128)(2,1)}, bf16[4,2,48,768]{3,2,1,0:T(8,128)(2,1)S(1)}, u32[]{:S(2)}, u32[]{:S(2)}) collective-permute-start(bf16[4,2,48,768]{3,2,1,0:T(8,128)(2,1)} %get-tuple-element.73), channel_id=1, source_target_pairs={{0,4},{2,6},{4,0},{6,2},{8,12},{10,14},{12,8},{14,10},{16,20},{18,... | collective-permute-start | bytes 1769480 | tf_op jit(solution)/shard_map/ppermute | solution.py:1074
  180.8 0.8 copy-start.11
  180.9 1.0 copy-start.12
  180.9 1.2 copy-start.13
  180.9 1.3 copy-start.14
  182.2 65.8 %copy-start = (f32[1024,768]{1,0:T(8,128)S(1)}, f32[1024,768]{1,0:T(8,128)}, u32[]{:S(2)}) copy-start(f32[1024,768]{1,0:T(8,128)} %get-tuple-element.56) | copy-start | bytes 9437188
  248.0 3.0 %copy-start.1 = (f32[1024,768]{1,0:T(8,128)S(1)}, f32[1024,768]{1,0:T(8,128)}, u32[]{:S(2)}) copy-start(f32[1024,768]{1,0:T(8,128)} %get-tuple-element.77) | copy-start | bytes 9437188
  251.0 1.7 copy-start.4
  251.0 2.4 copy-start.5
  251.0 3.0 %copy-start.3 = (f32[48,1536]{1,0:T(8,128)S(1)}, f32[48,1536]{1,0:T(8,128)}, u32[]{:S(2)}) copy-start(f32[48,1536]{1,0:T(8,128)} %get-tuple-element.127) | copy-start | bytes 884740
  251.0 3.7 %copy-start.2 = (f32[192,384]{1,0:T(8,128)S(1)}, f32[192,384]{1,0:T(8,128)}, u32[]{:S(2)}) copy-start(f32[192,384]{1,0:T(8,128)} %get-tuple-element.129) | copy-start | bytes 884740

commit v3 on v2

--- a/solution.py
+++ b/solution.py
@@ -43,6 +43,23 @@
     return base
 
 
+def as_column(row):
+    return jnp.broadcast_to(row, (8, row.shape[1])).T[:, 0:1]
+
+
+def key_window(seg_own, seg_far, block, BQ, BK):
+    own, far = seg_own[...].astype(f32), seg_far[...].astype(f32)
+    mine = seg_own[:, pl.ds(pl.multiple_of(block * BQ, BQ), BQ)].astype(f32)
+    first, last = jnp.min(mine), jnp.max(mine)
+
+    def count(hits_own, hits_far):
+        return jnp.sum(hits_own.astype(f32) + hits_far.astype(f32)).astype(jnp.int32)
+
+    lo = (count(own < first, far < first) // 128) * 128
+    blocks = (count(own <= last, far <= last) - lo + BK - 1) // BK
+    return jnp.minimum(lo, 2 * own.shape[1] - blocks * BK), blocks
+
+
 def fill_pairs(src, dst, rows, low, extra):
     for p in range(PAIRS):
         pair = src[:, p * 128 : (p + 1) * 128]
@@ -53,14 +70,15 @@
 def fill_keys(band, i, k_own, k_far, v_own, v_far, seg_own, seg_far, kaug, vaug, value_extra):
     local = kaug.shape[1] // 2
     low, side = low_lanes(CHUNK), side_lanes(CHUNK)
+    here = pl.ds(pl.multiple_of(i * CHUNK, CHUNK), CHUNK)
     for k, v, seg, first in ((k_own, v_own, seg_own, band), (k_far, v_far, seg_far, 1 - band)):
         rows = pl.ds(pl.multiple_of(first * local + i * CHUNK, CHUNK), CHUNK)
-        extra = jnp.where(side < 16, jnp.where(side == seg[...], 0.0, NEG_LARGE), jnp.where(side < 19, -1.0, 0.0))
+        extra = jnp.where(side < 16, jnp.where(side == as_column(seg[:, here]), 0.0, NEG_LARGE), jnp.where(side < 19, -1.0, 0.0))
         fill_pairs(k, kaug, rows, low, extra.astype(bf16))
         fill_pairs(v, vaug, rows, low, value_extra)
 
 
-def attend_fwd_kernel(fills, BQ, BK, start_ref, count_ref, band_ref, q_ref, qseg_ref, k_own, k_far, v_own, v_far,
+def attend_fwd_kernel(fills, BQ, BK, band_ref, q_ref, k_own, k_far, v_own, v_far,
                       seg_own, seg_far, o_ref, lse_ref, kaug, vaug, qm, s_all, mx, acc):
     i = pl.program_id(0)
 
@@ -71,15 +89,16 @@
     @pl.when(i >= fills)
     def _():
         low, side = low_lanes(BQ), side_lanes(BQ)
-        own = (side == qseg_ref[...]).astype(f32).astype(bf16)
+        block = i - fills
+        ids = as_column(seg_own[:, pl.ds(pl.multiple_of(block * BQ, BQ), BQ)])
+        own = (side == ids).astype(f32).astype(bf16)
         for p in range(PAIRS):
             pair = q_ref[:, p * 128 : (p + 1) * 128]
             qm[2 * p] = jnp.where(low, pair, own)
             qm[2 * p + 1] = jnp.where(low, own, pair)
         mx[...] = jnp.full(mx.shape, -3e38, f32)
         acc[...] = jnp.zeros(acc.shape, f32)
-        start = start_ref[i - fills]
-        count = count_ref[i - fills]
+        start, count = key_window(seg_own, seg_far, block, BQ, BK)
 
         def first(j, c):
             at = pl.multiple_of(start + j * BK, 128)
@@ -118,20 +137,20 @@
         lse_ref[...] = lse
 
 
-def attend_forward(band, q, seg_own, seg_far, k_own, k_far, v_own, v_far, start, count, BQ=256, BK=256):
+def attend_forward(band, q, seg_own, seg_far, k_own, k_far, v_own, v_far, BQ=256, BK=256):
     rows, width = q.shape
     fills, steps = rows // CHUNK, rows // BQ
     mine = lambda i, *_: (jnp.clip(i - fills, 0, steps - 1), 0)
     fill = lambda i, *_: (jnp.minimum(i, fills - 1), 0)
     wide = pl.BlockSpec((CHUNK, width), fill)
-    thin = pl.BlockSpec((CHUNK, 1), fill)
+    thin = pl.BlockSpec((1, rows), lambda i, *_: (0, 0))
     return pl.pallas_call(
         functools.partial(attend_fwd_kernel, fills, BQ, BK),
         out_shape=(jax.ShapeDtypeStruct((rows, width), bf16), jax.ShapeDtypeStruct((rows, 128), f32)),
         grid_spec=pltpu.PrefetchScalarGridSpec(
-            num_scalar_prefetch=3,
+            num_scalar_prefetch=1,
             grid=(fills + steps,),
-            in_specs=[pl.BlockSpec((BQ, width), mine), pl.BlockSpec((BQ, 1), mine), wide, wide, wide, wide, thin, thin],
+            in_specs=[pl.BlockSpec((BQ, width), mine), wide, wide, wide, wide, thin, thin],
             out_specs=[pl.BlockSpec((BQ, width), mine), pl.BlockSpec((BQ, 128), mine)],
             scratch_shapes=[
                 pltpu.VMEM((HEADS, 2 * rows, 128), bf16),
@@ -145,11 +164,11 @@
         compiler_params=pltpu.CompilerParams(vmem_limit_bytes=56 * MIB),
         cost_estimate=pl.CostEstimate(flops=30 * 10**9, bytes_accessed=10 * 10**6, transcendentals=0),
         name="attend_forward",
-    )(start, count, band, q, seg_own, k_own, k_far, v_own, v_far, seg_own, seg_far)
-
-
-def attend_bwd_kernel(fills, steps, BQ, BK, start_ref, count_ref, band_ref, q_ref, do_ref, o_ref, lse_ref, qseg_ref,
-                      k_own, k_far, v_own, v_far, seg_own, seg_far, dq_ref, dkt_own, dkt_far, dvt_own, dvt_far,
+    )(band, q, k_own, k_far, v_own, v_far, seg_own, seg_far)
+
+
+def attend_bwd_kernel(fills, steps, BQ, BK, band_ref, q_ref, do_ref, o_ref, lse_ref,
+                      k_own, k_far, v_own, v_far, seg_own, seg_far, carried, dq_ref, dkt_own, dkt_far, dvt_own, dvt_far, carried_out,
                       kaug, vaug, qm, dom, lqt, ldot, dq_acc, dk_acc, dv_acc):
     i = pl.program_id(0)
     band = band_ref[0]
@@ -169,7 +188,10 @@
     @pl.when((i >= fills) & (i < fills + steps))
     def _():
         low, side = low_lanes(BQ), side_lanes(BQ)
-        own = (side == qseg_ref[...]).astype(f32)
+        block = i - fills
+        carried_out[...] = carried[...]
+        ids = as_column(seg_own[:, pl.ds(pl.multiple_of(block * BQ, BQ), BQ)])
+        own = (side == ids).astype(f32)
         for p in range(PAIRS):
             cols = slice(p * 128, (p + 1) * 128)
             q_pair, do_pair = q_ref[:, cols], do_ref[:, cols]
@@ -188,7 +210,7 @@
                 dst[p, 0:HEAD_DIM, BQ : 2 * BQ] = zero
                 dst[p, HEAD_DIM:128, BQ : 2 * BQ] = flipped[HEAD_DIM:128]
         dq_acc[...] = jnp.zeros(dq_acc.shape, f32)
-        start = start_ref[i - fills]
+        start, count = key_window(seg_own, seg_far, block, BQ, BK)
 
         def step(j, c):
             window = pl.ds(pl.multiple_of(start + j * BK, 128), BK)
@@ -213,7 +235,7 @@
                     kept = []
             return c
 
-        lax.fori_loop(0, count_ref[i - fills], step, 0)
+        lax.fori_loop(0, count, step, 0)
         for p in range(PAIRS):
             pair = jnp.where(low, dq_acc[2 * p], dq_acc[2 * p + 1]) * HEAD_DIM**-0.5
             dq_ref[:, p * 128 : (p + 1) * 128] = pair.astype(bf16)
@@ -229,24 +251,24 @@
                 dv_out[rows, :] = dv_acc[p, :, cols].astype(bf16)
 
 
-def attend_backward(band, q, do, o, lse, seg_own, seg_far, k_own, k_far, v_own, v_far, start, count, BQ=256, BK=256):
+def attend_backward(band, carried, q, do, o, lse, seg_own, seg_far, k_own, k_far, v_own, v_far, BQ=256, BK=256):
     rows, width = q.shape
     fills, steps = rows // CHUNK, rows // BQ
     mine = lambda i, *_: (jnp.clip(i - fills, 0, steps - 1), 0)
     fill = lambda i, *_: (jnp.minimum(i, fills - 1), 0)
     drain = lambda i, *_: (0, jnp.clip(i - fills - steps, 0, fills - 1))
     wide = pl.BlockSpec((CHUNK, width), fill)
-    thin = pl.BlockSpec((CHUNK, 1), fill)
+    thin = pl.BlockSpec((1, rows), lambda i, *_: (0, 0))
     block = pl.BlockSpec((BQ, width), mine)
     flat = jax.ShapeDtypeStruct((width, rows), bf16)
     return pl.pallas_call(
         functools.partial(attend_bwd_kernel, fills, steps, BQ, BK),
-        out_shape=(jax.ShapeDtypeStruct((rows, width), bf16), flat, flat, flat, flat),
+        out_shape=(jax.ShapeDtypeStruct((rows, width), bf16), flat, flat, flat, flat, jax.ShapeDtypeStruct(carried.shape, carried.dtype)),
         grid_spec=pltpu.PrefetchScalarGridSpec(
-            num_scalar_prefetch=3,
+            num_scalar_prefetch=1,
             grid=(fills + steps + fills,),
-            in_specs=[block, block, block, pl.BlockSpec((BQ, 128), mine), pl.BlockSpec((BQ, 1), mine), wide, wide, wide, wide, thin, thin],
-            out_specs=[block] + [pl.BlockSpec((width, CHUNK), drain)] * 4,
+            in_specs=[block, block, block, pl.BlockSpec((BQ, 128), mine), wide, wide, wide, wide, thin, thin, block],
+            out_specs=[block] + [pl.BlockSpec((width, CHUNK), drain)] * 4 + [block],
             scratch_shapes=[
                 pltpu.VMEM((HEADS, 2 * rows, 128), bf16),
                 pltpu.VMEM((HEADS, 2 * rows, 128), bf16),
@@ -262,41 +284,17 @@
         compiler_params=pltpu.CompilerParams(vmem_limit_bytes=56 * MIB),
         cost_estimate=pl.CostEstimate(flops=45 * 10**9, bytes_accessed=20 * 10**6, transcendentals=0),
         name="attend_backward",
-    )(start, count, band, q, do, o, lse, seg_own, k_own, k_far, v_own, v_far, seg_own, seg_far)
-
-
-def key_windows(seg_own, seg_far, band, BQ=256, BK=256):
-    keys = 2 * seg_own.shape[0]
-    blocks = seg_own.reshape(-1, BQ)
-    first, last = blocks[:, 0], blocks[:, -1]
-
-    def below(limit, strict):
-        def count(seg):
-            return jnp.sum((seg[None, :] < limit[:, None]) if strict else (seg[None, :] <= limit[:, None]), axis=1, dtype=jnp.int32)
-
-        return count(seg_own) + count(seg_far)
-
-    lo = below(first, True) // 128 * 128
-    count = (below(last, False) - lo + BK - 1) // BK
-    return jnp.minimum(lo, keys - count * BK), count
+    )(band, q, do, o, lse, k_own, k_far, v_own, v_far, seg_own, seg_far, carried)
 
 
 MESH = pl.DeviceIdType.MESH
 TN = (((0,), (0,)), ((), ()))
 SLICE = 768
-ERFC_RATE = 0.39
-ERFC_TERMS = (0.23532524, 0.09138829, 0.64955972, -0.63540067, 0.88666461, -0.22753718)
 
 
 def gelu_and_slope(u):
-    bell = jnp.exp(u * u * -0.5)
-    t = 1.0 / (1.0 + jnp.abs(u) * (ERFC_RATE * 0.5**0.5))
-    total = ERFC_TERMS[-1] * 0.5
-    for term in ERFC_TERMS[-2::-1]:
-        total = total * t + term * 0.5
-    half = total * t * bell
-    below = jnp.where(u < 0, half, 1.0 - half)
-    return u * below, below + u * bell * (0.5 / 3.141592653589793) ** 0.5
+    below = 0.5 + 0.5 * lax.erf(u * 0.5**0.5)
+    return u * below, below + u * jnp.exp(u * u * -0.5) * (0.5 / 3.141592653589793) ** 0.5
 
 
 def normalize(rows):
@@ -311,13 +309,17 @@
     ref[at, :] = jnp.where(first, sums, ref[at, :] + sums)
 
 
+def as_row(ref):
+    return ref[...].reshape(1, -1)
+
+
 def add_low(dst, a, b):
     dst[...] = (a[...].astype(f32) + b[...].astype(f32)).astype(bf16)
 
 
 def mlp_kernel(sorted_out, blocks, rows, slices, tok_ref, att_ref, cot_ref, wproj, wup, wdown, pbias, gain, shift, ubias, dbias,
                out_ref, rgrad_ref, agrad_ref, sums_ref, usums_ref, proj_out, *rest):
-    outs, scratch = rest[: 8 if sorted_out else 2], rest[8 if sorted_out else 2 :]
+    outs, scratch = rest[: 4 if sorted_out else 2], rest[4 if sorted_out else 2 :]
     hid, ugr, n2s, bgs, ags, ats, d_own, d_far, d_in, u_in, p_own, p_far, p_in, send_sem, recv_sem = scratch
     i = pl.program_id(0)
     me, band = lax.axis_index("dp"), lax.axis_index("band")
@@ -352,9 +354,9 @@
         first = i == 0
         att = att_ref[...]
         ats[here, :] = att
-        residual = tok_ref[...] + mm(att, wproj[...]) + pbias[...]
+        residual = tok_ref[...] + mm(att, wproj[...]) + as_row(pbias)
         xhat, scale = normalize(residual)
-        n2 = (xhat * gain[...] + shift[...]).astype(bf16)
+        n2 = (xhat * as_row(gain) + as_row(shift)).astype(bf16)
         n2s[here, :] = n2
         cot = cot_ref[...]
         bg = cot.astype(bf16)
@@ -362,17 +364,17 @@
         add_sums(sums_ref, 0, bg.astype(f32), first)
         for c in range(slices):
             cols = slice(c * SLICE, (c + 1) * SLICE)
-            hidden, slope = gelu_and_slope(mm(n2, wup[:, cols]) + ubias[:, cols])
+            hidden, slope = gelu_and_slope(mm(n2, wup[:, cols]) + ubias[cols].reshape(1, -1))
             hid[here, cols] = hidden.astype(bf16)
             grad = (mm(bg, wdown[cols, :], NT) * slope).astype(bf16)
             ugr[here, cols] = grad
             sums = jnp.sum(grad.astype(f32), axis=0, keepdims=True)
             usums_ref[0:1, cols] = jnp.where(first, sums, usums_ref[0:1, cols] + sums)
-        out_ref[...] = residual + mm(hid[here, :], wdown[...]) + dbias[...]
+        out_ref[...] = residual + mm(hid[here, :], wdown[...]) + as_row(dbias)
         e = mm(ugr[here, :], wup[...], NT)
         add_sums(sums_ref, 1, e * xhat, first)
         add_sums(sums_ref, 2, e, first)
-        f = e * gain[...]
+        f = e * as_row(gain)
         rgrad = cot + scale * (f - jnp.mean(f, axis=-1, keepdims=True) - xhat * jnp.mean(f * xhat, axis=-1, keepdims=True))
         rgrad_ref[...] = rgrad
         ag = rgrad.astype(bf16)
@@ -414,7 +416,7 @@
                 (outs[3], t, y, piece),
             ):
                 at = pl.ds(pl.multiple_of(j * SLICE + y_bit * 2 * shard + x_bit * shard + first, piece), piece)
-                add_low(out.at[j, t], d_own.at[at, :], d_in.at[at, :])
+                add_low(out.at[j, t, 0:piece], d_own.at[at, :], d_in.at[at, :])
 
     def join_up(c):
         u_copy(c).wait_recv()
@@ -426,11 +428,14 @@
 
         def one(s, carry):
             z, t = s >> 1, s & 1
-            for out, sends in ((outs[4 + 2 * c], 1), (outs[5 + 2 * c], 0)):
+            for out, sends in ((outs[2 * c], 1), (outs[2 * c + 1], 0)):
                 bit = (y if c else x) ^ sends
                 x_bit, y_bit = (t, bit) if c else (bit, t)
                 at = pl.ds(pl.multiple_of((z * 4 + y_bit * 2 + x_bit) * shard, shard), shard)
-                add_low(out.at[z, t], own.at[at, :], u_in.at[c, at, :])
+                for part in range(2):
+                    cols = slice(part * half, (part + 1) * half)
+                    to = slice((2 + part) * shard, (3 + part) * shard)
+                    add_low(out.at[z, t, to], own.at[at, cols], u_in.at[c, at, cols])
             return carry
 
         lax.fori_loop(0, 8, one, 0)
@@ -478,10 +483,10 @@
     def full(a):
         return pl.BlockSpec(a.shape, lambda i: (0,) * len(a.shape), pipeline_mode=one)
 
-    vectors = [v.reshape(1, -1) for v in (proj_bias, gain, shift, up_bias, down_bias)]
+    vectors = (proj_bias, gain, shift, up_bias, down_bias)
     shape = jax.ShapeDtypeStruct
     if sorted_out:
-        pieces = [shape((4, 2, ff // 32, half), bf16)] * 4 + [shape((4, 2, width // 16, ff // 4), bf16)] * 4
+        pieces = [shape((4, 2, ff // 16, half), bf16)] * 4
     else:
         pieces = [shape((ff, half), bf16), shape((width, ff // 2), bf16)]
     kept = [shape((8, width), f32), shape((8, ff), f32), shape((width, half), bf16)] + pieces
@@ -509,8 +514,8 @@
     )(tokens, attended, cotangent, w_proj, w_up, w_down, *vectors)
 
 
-def qkv_kernel(tok_ref, seg_ref, w_ref, gain, shift, qbias, vbias, q_ref, k_ref, v_ref, n_ref, k_far, v_far, seg_far,
-               k_all, v_all, send_sem, recv_sem):
+def qkv_kernel(steps, tok_ref, seg_ref, w_ref, gain, shift, qbias, vbias, q_ref, k_ref, v_ref, n_ref, k_far, v_far, seg_far,
+               n_all, k_all, v_all, send_sem, recv_sem):
     i = pl.program_id(0)
     last = pl.num_programs(0) - 1
     other = (lax.axis_index("dp"), 1 - lax.axis_index("band"))
@@ -534,20 +539,27 @@
         pl.semaphore_wait(barrier, 1)
         segs.start()
 
-    here = pl.ds(pl.multiple_of(i * rows, rows), rows)
-    xhat, _ = normalize(tok_ref[...])
-    n1 = (xhat * gain[...] + shift[...]).astype(bf16)
-    n_ref[...] = n1
-    k = mm(n1, w_ref[:, width : 2 * width]).astype(bf16)
-    k_ref[...] = k
-    k_all[here, :] = k
-    v = (mm(n1, w_ref[:, 2 * width :]) + vbias[...]).astype(bf16)
-    v_ref[...] = v
-    v_all[here, :] = v
-    for copy in copies(i):
-        copy.start()
-    q = (mm(n1, w_ref[:, :width]) + qbias[...]).astype(bf16)
-    q_ref[...] = q * jnp.asarray(HEAD_DIM**-0.5, bf16)
+    @pl.when(i < steps)
+    def _():
+        here = pl.ds(pl.multiple_of(i * rows, rows), rows)
+        xhat, _ = normalize(tok_ref[...])
+        n1 = (xhat * as_row(gain) + as_row(shift)).astype(bf16)
+        n_ref[...] = n1
+        n_all[here, :] = n1
+        k = mm(n1, w_ref[:, width : 2 * width]).astype(bf16)
+        k_ref[...] = k
+        k_all[here, :] = k
+        copies(i)[0].start()
+        v = (mm(n1, w_ref[:, 2 * width :]) + as_row(vbias)).astype(bf16)
+        v_ref[...] = v
+        v_all[here, :] = v
+        copies(i)[1].start()
+
+    @pl.when(i >= steps)
+    def _():
+        here = pl.ds(pl.multiple_of((i - steps) * rows, rows), rows)
+        q = (mm(n_all[here, :], w_ref[:, :width]) + as_row(qbias)).astype(bf16)
+        q_ref[...] = q * jnp.asarray(HEAD_DIM**-0.5, bf16)
 
     @pl.when(i == last)
     def _():
@@ -560,18 +572,20 @@
 def project_qkv(tokens, seg, w_qkv, gain, shift, query_bias, value_bias, rows=256):
     count, width = tokens.shape
     one = pl.Buffered(1)
-    block = pl.BlockSpec((rows, width), lambda i: (i, 0))
-    vectors = [v.reshape(1, -1) for v in (gain, shift, query_bias, value_bias)]
+    steps = count // rows
+    block = pl.BlockSpec((rows, width), lambda i: (jnp.minimum(i, steps - 1), 0))
+    late = pl.BlockSpec((rows, width), lambda i: (jnp.maximum(i - steps, 0), 0))
+    vectors = (gain, shift, query_bias, value_bias)
     hbm = pl.BlockSpec(memory_space=pl.ANY)
-    steps = count // rows
     low = jax.ShapeDtypeStruct((count, width), bf16)
     return pl.pallas_call(
-        qkv_kernel,
+        functools.partial(qkv_kernel, steps),
         out_shape=(low,) * 6 + (jax.ShapeDtypeStruct(seg.shape, seg.dtype),),
-        grid=(steps,),
-        in_specs=[block, hbm] + [pl.BlockSpec(a.shape, lambda i: (0, 0), pipeline_mode=one) for a in (w_qkv, *vectors)],
-        out_specs=[block] * 4 + [hbm] * 3,
+        grid=(2 * steps,),
+        in_specs=[block, hbm] + [pl.BlockSpec(a.shape, lambda i, n=a.ndim: (0,) * n, pipeline_mode=one) for a in (w_qkv, *vectors)],
+        out_specs=[late] + [block] * 3 + [hbm] * 3,
         scratch_shapes=[
+            pltpu.VMEM((count, width), bf16),
             pltpu.VMEM((count, width), bf16),
             pltpu.VMEM((count, width), bf16),
             pltpu.SemaphoreType.DMA((2 * steps + 1,)),
@@ -685,18 +699,17 @@
 
 
 def finish_kernel(
-    dq_hbm, dko_hbm, dkf_hbm, dvo_hbm, dvf_hbm, n_hbm, tok_hbm, rgrad_hbm, w_hbm, dak_hbm, dar_hbm, dbk_hbm, dbr_hbm,
-    uak_hbm, uar_hbm, ubk_hbm, ubr_hbm, proj_hbm, gain, msums, usums,
-    out_hbm, down_out, up_out, qkv_out, proj_out, vec_out,
-    packed, dko, dko_in, dvo, dvo_in, n1, tok, rgrad, wq, down, up, proj, far, far_in, tail,
-    one_d, one_u, one_t, two_d, two_u, two_t, thr_d, thr_u, thr_t, vec, vec_band, vec_x, vec_y, vec_z,
-    load_sem, store_sem, swap_send, swap_recv, send, recv, vsend, vrecv,
+    dq_hbm, dko_hbm, dkf_hbm, dvo_hbm, dvf_hbm, n_hbm, tok_hbm, rgrad_hbm, w_hbm, ak_hbm, ar_hbm, bk_hbm, br_hbm, proj_hbm, gain, msums, usums,
+    out, down_out, up_out, qkv_out, proj_out, vec_out, usum_out,
+    packed, dko, dko_in, dvo, dvo_in, n1, tok, wq, early, proj, cols, far_in, tail,
+    one_e, one_t, two_e, two_t, thr_e, thr_t, vec, vec_band, vec_x, vec_y, vec_z,
+    load_sem, swap_send, swap_recv, send, recv, vsend, vrecv,
 ):
     me = lax.axis_index("dp")
     band = lax.axis_index("band")
     x, y, z = me & 1, (me >> 1) & 1, me >> 2
     rows, width = tok.shape
-    half = far.shape[-1]
+    half = far_in.shape[-1]
     peer_band = (me, 1 - band)
     peer_x = (me ^ 1, band)
     peer_y = (me ^ 2, band)
@@ -708,13 +721,13 @@
         return copy
 
     loads = {
-        "down": (load(0, dak_hbm, down.at[0]), load(1, dar_hbm, one_d.at[0]), load(2, dbk_hbm, down.at[1]), load(3, dbr_hbm, one_d.at[1])),
-        "up": (load(13, uak_hbm, up.at[0]), load(14, uar_hbm, one_u.at[0]), load(15, ubk_hbm, up.at[1]), load(16, ubr_hbm, one_u.at[1])),
-        "keys": (load(4, dko_hbm, dko), load(5, dvo_hbm, dvo), load(6, dq_hbm, packed.at[:, 0:width])),
+        "early": (load(0, ak_hbm, early.at[0]), load(1, ar_hbm, one_e.at[0]), load(2, bk_hbm, early.at[1]), load(3, br_hbm, one_e.at[1])),
+        "queries": (load(6, dq_hbm, packed.at[:, 0:width]),),
         "normed": (load(7, n_hbm, n1),),
+        "keys": (load(4, dko_hbm, dko), load(5, dvo_hbm, dvo)),
         "proj": (load(8, proj_hbm, proj),),
         "weight": (load(10, w_hbm, wq),),
-        "rows": (load(11, tok_hbm, tok), load(12, rgrad_hbm, rgrad)),
+        "rows": (load(11, tok_hbm, tok), load(12, rgrad_hbm, out)),
     }
 
     def ready(name):
@@ -795,44 +808,70 @@
     everything = slice(None)
     wide_cut = ((everything, slice(0, 768)), (everything, slice(768, 1536)))
 
-    ready("down")
-    d_two = second_stage(0, lambda p, i, j: down.at[p, i, j], one_d, two_d, None)
-    ready("up")
-    u_two = second_stage(1, lambda p, i, j: up.at[p, i, j], one_u, two_u, None)
+    ready("early")
+    e_two = second_stage(0, lambda p, i, j: early.at[p, i, j], one_e, two_e, None)
 
     def tail_kept(piece, zz, t):
         return tail.at[zz, t, x, :, 0:768] if piece == 0 else tail.at[zz, y, t, :, 768:1536]
 
-    ready("keys")
-    swap_k.wait_recv()
-    swap_v.wait_recv()
-
-    def turn(i, c):
-        here = pl.ds(pl.multiple_of(i * 256, 256), 256)
-        for t, (own, other) in enumerate(((dko, dko_in), (dvo, dvo_in))):
+    def columns(t):
+        cols[:, :, :, :, t * width : (t + 1) * width] = (
+            mm(n1[...], packed[:, t * width : (t + 1) * width], TN).astype(bf16).reshape(cols.shape[:-1] + (width,))
+        )
+
+    def turn(t, own, other):
+        def step(i, c):
+            here = pl.ds(pl.multiple_of(i * 256, 256), 256)
             for p in range(width // 128):
                 at = slice(p * 128, (p + 1) * 128)
                 turned = (own[at, here].astype(f32) + other[at, here].astype(f32)).astype(bf16).T
-                packed[here, (t + 1) * width + p * 128 : (t + 1) * width + (p + 1) * 128] = turned
-        return c
-
-    lax.fori_loop(0, rows // 256, turn, 0)
+                packed[here, t * width + p * 128 : t * width + (p + 1) * 128] = turned
+            return c
+
+        lax.fori_loop(0, rows // 256, step, 0)
+
+    def swap(t, start, size, to):
+        return pltpu.make_async_remote_copy(
+            src_ref=cols.at[:, :, :, :, pl.ds(pl.multiple_of(start, 128), size)],
+            dst_ref=far_in.at[:, :, :, :, pl.ds(pl.multiple_of(to, 128), size)],
+            send_sem=swap_send.at[t],
+            recv_sem=swap_recv.at[t],
+            device_id=peer_band,
+            device_id_type=MESH,
+        )
+
+    third = width // 2
+    swap_near = swap(2, (3 - band) * third, third, band * width)
+    swap_wide = swap(3, (1 - band) * 2 * width, width, (1 - band) * third)
+    ready("queries")
     ready("normed")
-
-    def columns(which):
-        at = pl.ds(pl.multiple_of(which * half, 128), half)
-        return mm(n1[...], packed[:, at], TN).astype(bf16).reshape(far.shape)
-
-    far[...] = columns(1 - band)
-    swap_far = push(far, far_in, peer_band, swap_send.at[2], swap_recv.at[2])
-    tail[:, :, :, :, 0:half] = columns(band)
+    columns(0)
+
+    @pl.when(band == 1)
+    def _():
+        swap_wide.start()
+
+    ready("keys")
+    swap_k.wait_recv()
+    turn(1, dko, dko_in)
+    columns(1)
+    swap_near.start()
+    swap_v.wait_recv()
+    turn(2, dvo, dvo_in)
+    columns(2)
+
+    @pl.when(band == 0)
+    def _():
+        swap_wide.start()
+
     ready("proj")
     each_shard(lambda i, j, k: put(tail.at[i, j, k, :, half : 2 * width], proj.at[i, j, k]))
-    swap_far.wait_recv()
-    each_shard(lambda i, j, k: add_low(tail.at[i, j, k, :, 0:half], tail.at[i, j, k, :, 0:half], far_in.at[i, j, k]))
+    e_three = third_stage(0, one_e, two_e, thr_e, e_two)
+    swap_near.wait()
+    swap_wide.wait()
+    mine = pl.ds(pl.multiple_of(band * half, 128), half)
+    each_shard(lambda i, j, k: add_low(tail.at[i, j, k, :, 0:half], cols.at[i, j, k, :, mine], far_in.at[i, j, k]))
     t_one = first_stage(2, tail, one_t, wide_cut)
-    d_three = third_stage(0, one_d, two_d, thr_d, d_two)
-    u_three = third_stage(1, one_u, two_u, thr_u, u_two)
 
     ready("weight")
     ready("rows")
@@ -846,36 +885,43 @@
         vec[1:2, :] = vec[1:2, :] + jnp.sum(e, axis=0, keepdims=True)
         vec[2:3, :] = vec[2:3, :] + jnp.sum(packed[here, 0:width].astype(f32), axis=0, keepdims=True)
         vec[3:4, :] = vec[3:4, :] + jnp.sum(packed[here, 2 * width : 3 * width].astype(f32), axis=0, keepdims=True)
-        f = e * gain[...]
+        f = e * as_row(gain)
         back = scale * (f - jnp.mean(f, axis=-1, keepdims=True) - xhat * jnp.mean(f * xhat, axis=-1, keepdims=True))
-        rgrad[here, :] = rgrad[here, :] + back
+        out[here, :] = out[here, :] + back
         return c
 
     lax.fori_loop(0, rows // 256, rows_back, 0)
-    store = pltpu.make_async_copy(rgrad, out_hbm, store_sem)
-    store.start()
     vec[4:8, :] = msums[0:4, :]
     for t in range(usums.shape[1] // width):
         vec[8 + t : 9 + t, :] = usums[0:1, t * width : (t + 1) * width]
     v_band = push(vec, vec_band, peer_band, vsend.at[0], vrecv.at[0])
+    t_two = second_stage(2, tail_kept, one_t, two_t, t_one)
     v_band.wait()
     vec_band[...] = vec[...] + vec_band[...]
     v_x = push(vec_band, vec_x, peer_x, vsend.at[1], vrecv.at[1])
     v_x.wait()
     vec_x[...] = vec_band[...] + vec_x[...]
     v_y = push(vec_x, vec_y, peer_y, vsend.at[2], vrecv.at[2])
-    t_two = second_stage(2, tail_kept, one_t, two_t, t_one)
     v_y.wait()
     vec_y[...] = vec_x[...] + vec_y[...]
     v_z = [push(vec_y, vec_z.at[d], peers_z[d], vsend.at[3 + d], vrecv.at[3 + d]) for d in range(3)]
     t_three = third_stage(2, one_t, two_t, thr_t, t_two)
-    down_out[0:96, :] = last(two_d, thr_d, d_three, 0)
-    down_out[96:192, :] = last(two_d, thr_d, d_three, 1)
-    up_out[:, 0:768] = last(two_u, thr_u, u_three, 0)
-    up_out[:, 768:1536] = last(two_u, thr_u, u_three, 1)
     for copy in v_z:
         copy.wait_recv()
-    vec_out[...] = vec_y[...] + vec_z[0] + vec_z[1] + vec_z[2]
+    vec[...] = vec_y[...] + vec_z[0] + vec_z[1] + vec_z[2]
+    shard = vec_out.shape[1]
+    vec_out[...] = pltpu.roll(vec[0:8, :], width - me * shard, 1)[:, 0:shard]
+    wide = usum_out.shape[1]
+    per_row = width // wide
+    row = vec[pl.ds(8 + me // per_row, 1), :]
+    usum_out[...] = pltpu.roll(jnp.broadcast_to(row, (8, width)), width - (me % per_row) * wide, 1)[0:1, 0:wide]
+    shard = width // 16
+    for piece in range(2):
+        early_sum = last(two_e, thr_e, e_three, piece)
+        down_out[piece * 2 * shard : (piece + 1) * 2 * shard, :] = early_sum[0 : 2 * shard]
+        for part in range(2):
+            at = (2 * piece + part) * third
+            up_out[:, at : at + third] = early_sum[(2 + part) * shard : (3 + part) * shard]
     qkv_out[:, 0:768] = last(two_t, thr_t, t_three, 0)
     final = last(two_t, thr_t, t_three, 1)
     qkv_out[:, 768:half] = final[:, 0 : half - 768]
@@ -884,7 +930,6 @@
     for copy in pending:
         if id(copy) not in done:
             copy.wait_send()
-    store.wait()
 
 
 def finish(dq, dk_own, dk_far, dv_own, dv_far, normed, tokens, rgrad, w_qkv, pieces, proj, gain, msums, usums):
@@ -894,7 +939,7 @@
     shards = (4, 2, 2)
     u_shape, p_shape = shards + (width // 16, ff // 2), shards + (width // 16, width // 2)
     q_shape = shards + (width // 16, half)
-    d_piece, w_piece = (ff // 32, width // 2), (width // 16, ff // 4)
+    e_piece, w_piece = (ff // 16, width // 2), (width // 16, ff // 4)
     hbm, vmem = pl.BlockSpec(memory_space=pl.ANY), pl.BlockSpec(memory_space=pltpu.VMEM)
     shape = jax.ShapeDtypeStruct
     low = lambda *s: pltpu.VMEM(s, bf16)
@@ -907,51 +952,46 @@
             shape((width // 16, ff // 2), f32),
             shape((width // 16, half), f32),
             shape((width // 16, width // 2), f32),
-            shape((16, width), f32),
+            shape((8, width // 16), f32),
+            shape((1, ff // 16), f32),
         ),
-        in_specs=[hbm] * 18 + [vmem] * 3,
-        out_specs=[hbm] + [vmem] * 5,
+        in_specs=[hbm] * 14 + [vmem] * 3,
+        out_specs=[vmem] * 7,
         scratch_shapes=[
             low(rows, 3 * width),
             *([low(width, rows)] * 4),
             low(rows, width),
             pltpu.VMEM((rows, width), f32),
-            pltpu.VMEM((rows, width), f32),
             low(width, 3 * width),
-            low(2, 4, 2, *d_piece),
-            low(2, 4, 2, *w_piece),
+            low(2, 4, 2, *e_piece),
             low(*p_shape),
-            low(*q_shape),
+            low(*shards, width // 16, 3 * width),
             low(*q_shape),
             low(*u_shape),
-            low(2, 4, 2, *d_piece),
+            low(2, 4, 2, *e_piece),
             low(2, 4, 2, *w_piece),
-            low(2, 4, 2, *w_piece),
-            low(2, 4, *d_piece),
+            low(2, 4, *e_piece),
             low(2, 4, *w_piece),
-            low(2, 4, *w_piece),
-            low(2, 3, *d_piece),
-            low(2, 3, *w_piece),
+            low(2, 3, *e_piece),
             low(2, 3, *w_piece),
             pltpu.VMEM((16, width), f32),
             pltpu.VMEM((16, width), f32),
             pltpu.VMEM((16, width), f32),
             pltpu.VMEM((16, width), f32),
             pltpu.VMEM((3, 16, width), f32),
-            dma((17,)),
-            dma,
-            dma((3,)),
-            dma((3,)),
+            dma((13,)),
+            dma((4,)),
+            dma((4,)),
             dma((3, 2, 5)),
             dma((3, 2, 5)),
             dma((6,)),
             dma((6,)),
         ],
-        compiler_params=pltpu.CompilerParams(vmem_limit_bytes=60 * MIB, collective_id=0, has_side_effects=True),
+        compiler_params=pltpu.CompilerParams(vmem_limit_bytes=52 * MIB, collective_id=0, has_side_effects=True),
         cost_estimate=pl.CostEstimate(flops=20 * 10**9, bytes_accessed=40 * 10**6, transcendentals=0),
         name="finish",
     )(dq, dk_own, dk_far, dv_own, dv_far, normed, tokens, rgrad, w_qkv, *pieces, proj.reshape(p_shape),
-      gain.reshape(1, -1), msums, usums)
+      gain, msums, usums)
 
 
 def swap_band(x):
@@ -1045,12 +1085,11 @@
     band = lax.axis_index("band")
     band_at = band.astype(jnp.int32).reshape(1)
     tokens = inputs.reshape(-1, width)
-    seg_own = segment_ids.reshape(-1)
+    seg_own = segment_ids
     queries, k_own, v_own, normed, k_far, v_far, seg_far = project_qkv(
         tokens, seg_own, w_qkv, first_gain, first_bias, query_bias, value_bias
     )
-    start, count = key_windows(seg_own, seg_far, band)
-    keys = (seg_own[:, None], seg_far[:, None], k_own, k_far, v_own, v_far, start, count)
+    keys = (seg_own, seg_far, k_own, k_far, v_own, v_far)
     attended, log_totals = attend_forward(band_at, queries, *keys)
     output, residual_grad, attended_grad, mlp_sums, up_sums, proj, *pieces = mlp(
         size,
@@ -1070,21 +1109,17 @@
         turns = [[(i, i ^ bit) for i in range(size)] for bit in (1, 2)]
         pieces = [
             part
-            for t in range(4)
-            for part in (pieces[2 * t + 1], lax.ppermute(pieces[2 * t], "dp", turns[t % 2]))
+            for t in range(2)
+            for part in (pieces[2 * t + 1], lax.ppermute(pieces[2 * t], "dp", turns[t]))
         ]
-    query_grad, dk_own, dk_far, dv_own, dv_far = attend_backward(
-        band_at, queries, attended_grad, attended, log_totals, *keys
+    query_grad, dk_own, dk_far, dv_own, dv_far, output = attend_backward(
+        band_at, output, queries, attended_grad, attended, log_totals, *keys
     )
-    ups = up_bias.shape[0] // width
     if size == 16:
-        input_grad, down_sum, up_sum, qkv_sum, proj_sum, vec = finish(
+        input_grad, down_sum, up_sum, qkv_sum, proj_sum, vec, up_vec = finish(
             query_grad, dk_own, dk_far, dv_own, dv_far, normed, tokens, residual_grad, w_qkv, pieces, proj, first_gain, mlp_sums, up_sums
         )
-        shard = width // size
-        mine = lax.dynamic_slice_in_dim(vec[:8], lax.axis_index("dp") * shard, shard, 1)
-        vectors = [mine[t] for t in range(8)]
-        up_vector = lax.dynamic_slice_in_dim(vec[8 : 8 + ups].reshape(-1), lax.axis_index("dp") * ups * shard, ups * shard, 0)
+        vectors, up_vector = [vec[t] for t in range(8)], up_vec.reshape(-1)
     else:
         input_grad, down_sum, up_sum, qkv_sum, proj_sum, vectors, up_vector = finish_any(
             size, band_at, query_grad, dk_own, dk_far, dv_own, dv_far, normed, tokens, residual_grad, w_qkv, pieces, proj, first_gain, mlp_sums, up_sums

time: 256 us -> 231 us (0.902)
  local copies, waits for them, and re-layouts: 22.5 us -> 9 us
  Pallas kernels: 225 us -> 216 us
  other arithmetic: 2.79 us -> 0 us
    reshape x9 -> x0, local copies, waits for them, and re-layouts: 7.4 us -> none  [the longest x4 5.07 us: project_qkv(): vectors = [v.reshape(1, -1) for v in (gain, shift, query_bias, value_bias)]]
    pallas_call x1, Pallas kernels: 60 us -> 54.2 us  [mlp(): pl.pallas_call(functools.partial(mlp_kernel, sorted_out, blocks, rows, sl...]
    unnamed x39 -> x18, local copies, waits for them, and re-layouts: 9.5 us -> 8.45 us
  transfers between devices with their start and end apart: 4 -> 2, of which waited for: 0 -> 0; matrix products, arithmetic and copies ran while one was open for 0% -> 0% of each run, Pallas kernels for 21% -> 23%
where the time goes in v3:
time: 231 us
  Pallas kernels  216 us (94%)
  local copies, waits for them, and re-layouts  9 us (4%)
  starting transfers between devices  4.53 us (2%)
    pallas_call x1, Pallas kernels, finish(): pl.pallas_call(finish_kernel, out_shape=(shape((rows, width), f32), shape...  63.5 us
    pallas_call x1, Pallas kernels, mlp(): pl.pallas_call(functools.partial(mlp_kernel, sorted_out, blocks, rows, sl...  54.2 us
    pallas_call x1, Pallas kernels, attend_backward(): pl.pallas_call(functools.partial(attend_bwd_kernel, fills, steps, BQ, BK)...  53 us
    pallas_call x1, Pallas kernels, attend_forward(): pl.pallas_call(functools.partial(attend_fwd_kernel, fills, BQ, BK), out_s...  33.4 us
    pallas_call x1, Pallas kernels, project_qkv(): pl.pallas_call(functools.partial(qkv_kernel, steps), out_shape=(low,) * 6...  12.4 us
    unnamed x18, local copies, waits for them, and re-layouts  8.45 us
  transfers between devices with their start and end apart: 2, of which 0 were waited for; matrix products, arithmetic and copies ran while one was open for 0% of the time, Pallas kernels for 23%

profile of v3, /device:TPU:0, one launch (start us, length us, event | category | flops | bytes accessed | tf_op | source)
XLA Modules:
  0.0 230.7 jit_solution(15423894313512641208)
XLA Ops:
  0.6 12.4 %project_qkv.1 = (bf16[1024,768]{1,0:T(8,128)(2,1)}, bf16[1024,768]{1,0:T(8,128)(2,1)}, bf16[1024,768]{1,0:T(8,128)(2,1)}, bf16[1024,768]{1,0:T(8,128)(2,1)}, bf...) custom-call(f32[1024,768]{1,0:T(8,128)} %bitcast.27, s32[1,1024]{1,0:T(1,128)} %seg_own.3, ...), custom_call_target="tpu_custom_call" | custom-call | flops 4000000000 | bytes 13000000 | tf_op jit(solution)/shard_map/project_qkv/pallas_call | solution.py:581
  13.1 33.4 %attend_forward.1 = (bf16[1024,768]{1,0:T(8,128)(2,1)}, f32[1024,128]{1,0:T(8,128)}) custom-call(s32[1]{0:T(128)} %bitcast.band_ref, bf16[1024,768]{1,0:T(8,128)(2,1)} %get-tuple-element.47.q_ref, bf16[1024,768]{1,0:T(8,128)(2,1)} %get-tuple-element.48.k_own, bf16[1024,768]{1,0:T(8,128)(2,1)} %get-tuple-element.49.k_far, ...), custom_call_target="tpu_custom_call" | custom-call | flops 30000001024 | bytes 10000000 | tf_op jit(solution)/shard_map/attend_forward/pallas_call | solution.py:147
  46.4 54.2 %mlp.1 = (f32[1024,768]{1,0:T(8,128)}, f32[1024,768]{1,0:T(8,128)}, bf16[1024,768]{1,0:T(8,128)(2,1)}, f32[8,768]{1,0:T(8,128)}, f32[8,3072]{1,0:T(8,128)}, /*in...) custom-call(f32[1024,768]{1,0:T(8,128)} %bitcast.28, ...), custom_call_target="tpu_custom_call" | custom-call | flops 40000000000 | bytes 40000000 | tf_op jit(solution)/shard_map/mlp/pallas_call | solution.py:495
  100.7 0.5 collective-permute-start
  101.1 4.1 %collective-permute-start.1 = (bf16[4,2,192,384]{3,2,1,0:T(8,128)(2,1)}, bf16[4,2,192,384]{3,2,1,0:T(8,128)(2,1)S(1)}, u32[]{:S(2)}, u32[]{:S(2)}) collective-permute-start(bf16[4,2,192,384]{3,2,1,0:T(8,128)(2,1)} %get-tuple-element.68), channel_id=1, source_target_pairs={{0,4},{2,6},{4,0},{6,2},{8,12},{10,14},{12,8},{14,10},{16,20},{18,... | collective-permute-start | bytes 3538952 | tf_op jit(solution)/shard_map/ppermute | solution.py:1113
  105.2 0.0 copy-start
  105.2 0.0 copy-start.1
  105.2 0.0 copy-start.2
  105.2 0.0 copy-start.3
  105.2 53.0 %attend_backward.1 = (bf16[1024,768]{1,0:T(8,128)(2,1)}, bf16[768,1024]{1,0:T(8,128)(2,1)}, bf16[768,1024]{1,0:T(8,128)(2,1)}, bf16[768,1024]{1,0:T(8,128)(2,1)}...) custom-call(s32[1]{0:T(128)} %bitcast.band_ref, bf16[1024,768]{1,0:T(8,128)(2,1)} %get-tuple-element.47.q_ref, ...), custom_call_target="tpu_custom_call" | custom-call | flops 44999999488 | bytes 20000000 | tf_op jit(solution)/shard_map/attend_backward/pallas_call | solution.py:264
  158.2 0.0 collective-permute-done.ar_hbm
  158.2 0.0 copy-start.4
  158.2 0.0 collective-permute-done.1.br_hbm
  158.2 0.0 copy-start.5
  158.2 1.0 copy-done.4
  159.2 0.4 copy-done.5
  159.6 0.0 copy-done
  159.6 0.0 copy-done.1
  159.6 0.0 copy-done.2
  159.6 0.0 copy-done.3
  159.6 63.5 %finish.1 = (f32[1024,768]{1,0:T(8,128)}, f32[192,384]{1,0:T(8,128)S(1)}, f32[48,1536]{1,0:T(8,128)S(1)}, f32[48,1152]{1,0:T(8,128)S(1)}, f32[48,384]{1,0:T(8,12...) custom-call(bf16[1024,768]{1,0:T(8,128)(2,1)} %get-tuple-element.58.dq_hbm, ...), custom_call_target="tpu_custom_call" | custom-call | flops 20000000000 | bytes 40000000 | tf_op jit(solution)/shard_map/finish/pallas_call | solution.py:947
  223.1 0.5 slice_bitcast_fusion
  223.7 3.8 %copy.37 = f32[1,1024,768]{2,1,0:T(8,128)} copy(f32[1,1024,768]{2,1,0:T(8,128)} %bitcast.25) | data formatting | bytes 6291456
  227.4 0.7 copy.38
  228.1 0.6 copy.39
  228.7 0.7 copy.40
  229.4 0.6 copy.41
  230.0 0.7 copy.42
Async XLA Ops:
  100.7 57.5 %collective-permute-start = (bf16[4,2,192,384]{3,2,1,0:T(8,128)(2,1)}, bf16[4,2,192,384]{3,2,1,0:T(8,128)(2,1)S(1)}, u32[]{:S(2)}, u32[]{:S(2)}) collective-permute-start(bf16[4,2,192,384]{3,2,1,0:T(8,128)(2,1)} %get-tuple-element.66), channel_id=1, source_target_pairs={{0,2},{2,0},{4,6},{6,4},{8,10},{10,8},{12,14},{14,12},{16,18},{18,... | collective-permute-start | bytes 3538952 | tf_op jit(solution)/shard_map/ppermute | solution.py:1113
  101.1 57.1 %collective-permute-start.1 = (bf16[4,2,192,384]{3,2,1,0:T(8,128)(2,1)}, bf16[4,2,192,384]{3,2,1,0:T(8,128)(2,1)S(1)}, u32[]{:S(2)}, u32[]{:S(2)}) collective-permute-start(bf16[4,2,192,384]{3,2,1,0:T(8,128)(2,1)} %get-tuple-element.68), channel_id=1, source_target_pairs={{0,4},{2,6},{4,0},{6,2},{8,12},{10,14},{12,8},{14,10},{16,20},{18,... | collective-permute-start | bytes 3538952 | tf_op jit(solution)/shard_map/ppermute | solution.py:1113
  105.2 54.4 %copy-start = (f32[768]{0:T(1024)S(1)}, f32[768]{0:T(1024)}, u32[]{:S(2)}) copy-start(f32[768]{0:T(1024)} %gain.5) | copy-start | bytes 9220
  105.2 54.4 %copy-start.1 = (bf16[768,384]{1,0:T(8,128)(2,1)S(1)}, bf16[768,384]{1,0:T(8,128)(2,1)}, u32[]{:S(2)}) copy-start(bf16[768,384]{1,0:T(8,128)(2,1)} %get-tuple-element.69) | copy-start | bytes 1769476
  105.2 54.4 %copy-start.2 = (f32[8,3072]{1,0:T(8,128)S(1)}, f32[8,3072]{1,0:T(8,128)}, u32[]{:S(2)}) copy-start(f32[8,3072]{1,0:T(8,128)} %get-tuple-element.71.usums) | copy-start | bytes 294916
  105.2 54.4 %copy-start.3 = (f32[8,768]{1,0:T(8,128)S(1)}, f32[8,768]{1,0:T(8,128)}, u32[]{:S(2)}) copy-start(f32[8,768]{1,0:T(8,128)} %get-tuple-element.70.msums) | copy-start | bytes 73732
  158.2 1.0 copy-start.4
  158.2 1.4 copy-start.5

commit v4 on v3

--- a/solution.py
+++ b/solution.py
@@ -13,6 +13,7 @@
 NEG_LARGE = -1e30
 PAIRS = HEADS // 2
 CHUNK = 256
+EDGE = 64
 MIB = 1 << 20
 f32, bf16 = jnp.float32, jnp.bfloat16
 NN = (((1,), (0,)), ((), ()))
@@ -49,15 +50,34 @@
 
 def key_window(seg_own, seg_far, block, BQ, BK):
     own, far = seg_own[...].astype(f32), seg_far[...].astype(f32)
+
+    def below(limit):
+        return jnp.sum((own < limit).astype(f32) + (far < limit).astype(f32)).astype(jnp.int32)
+
     mine = seg_own[:, pl.ds(pl.multiple_of(block * BQ, BQ), BQ)].astype(f32)
-    first, last = jnp.min(mine), jnp.max(mine)
-
-    def count(hits_own, hits_far):
-        return jnp.sum(hits_own.astype(f32) + hits_far.astype(f32)).astype(jnp.int32)
-
-    lo = (count(own < first, far < first) // 128) * 128
-    blocks = (count(own <= last, far <= last) - lo + BK - 1) // BK
-    return jnp.minimum(lo, 2 * own.shape[1] - blocks * BK), blocks
+    row = lax.broadcasted_iota(jnp.int32, mine.shape, 1)
+    lo = (below(jnp.min(mine)) // 128) * 128
+    blocks = (below(jnp.max(mine) + 1.0) - lo + BK - 1) // BK
+    start = jnp.minimum(lo, 2 * own.shape[1] - blocks * BK)
+    early_end = below(jnp.min(jnp.where(row >= EDGE, mine, 99.0)))
+    late_start = below(jnp.max(jnp.where(row < BQ - EDGE, mine, -1.0)) + 1.0)
+    early = jnp.clip((early_end - start) // BK, 0, blocks)
+    late = jnp.clip((start + blocks * BK - late_start) // BK, 0, blocks - early)
+    return start, blocks, early, late
+
+
+def over_blocks(count, early, late, rows, body):
+    for first, end, part in (
+        (0, early, slice(0, EDGE)),
+        (early, count - late, slice(0, rows)),
+        (count - late, count, slice(rows - EDGE, rows)),
+    ):
+
+        def step(j, c, part=part):
+            body(j, part)
+            return c
+
+        lax.fori_loop(first, end, step, 0)
 
 
 def fill_pairs(src, dst, rows, low, extra):
@@ -98,33 +118,31 @@
             qm[2 * p + 1] = jnp.where(low, own, pair)
         mx[...] = jnp.full(mx.shape, -3e38, f32)
         acc[...] = jnp.zeros(acc.shape, f32)
-        start, count = key_window(seg_own, seg_far, block, BQ, BK)
-
-        def first(j, c):
+        start, count, early, late = key_window(seg_own, seg_far, block, BQ, BK)
+
+        def first(j, part):
             at = pl.multiple_of(start + j * BK, 128)
             out = pl.ds(pl.multiple_of(j * BK, BK), BK)
             for h in range(HEADS):
-                s = mm(qm[h], kaug[h, pl.ds(at, BK), :], NT)
-                s_all[h, :, out] = s
-                m = mx[h]
+                s = mm(qm[h, part, :], kaug[h, pl.ds(at, BK), :], NT)
+                s_all[h, part, out] = s
+                m = mx[h, part, :]
                 for t in range(BK // 128):
                     m = jnp.maximum(m, s[:, t * 128 : (t + 1) * 128])
-                mx[h] = m
-            return c
-
-        lax.fori_loop(0, count, first, 0)
+                mx[h, part, :] = m
+
+        over_blocks(count, early, late, BQ, first)
         for h in range(HEADS):
             mx[h] = jnp.broadcast_to(jnp.max(mx[h], axis=1, keepdims=True), (BQ, 128))
 
-        def second(j, c):
+        def second(j, part):
             at = pl.multiple_of(start + j * BK, 128)
             src = pl.ds(pl.multiple_of(j * BK, BK), BK)
             for h in range(HEADS):
-                p = jnp.exp(s_all[h, :, src] - jnp.concatenate([mx[h]] * (BK // 128), axis=1)).astype(bf16)
-                acc[h] += mm(p, vaug[h, pl.ds(at, BK), :])
-            return c
-
-        lax.fori_loop(0, count, second, 0)
+                p = jnp.exp(s_all[h, part, src] - jnp.concatenate([mx[h, part, :]] * (BK // 128), axis=1)).astype(bf16)
+                acc[h, part, :] += mm(p, vaug[h, pl.ds(at, BK), :])
+
+        over_blocks(count, early, late, BQ, second)
         lane = lax.broadcasted_iota(jnp.int32, (BQ, 128), 1)
         lse = jnp.zeros((BQ, 128), f32)
         for p in range(PAIRS):
@@ -169,7 +187,7 @@
 
 def attend_bwd_kernel(fills, steps, BQ, BK, band_ref, q_ref, do_ref, o_ref, lse_ref,
                       k_own, k_far, v_own, v_far, seg_own, seg_far, carried, dq_ref, dkt_own, dkt_far, dvt_own, dvt_far, carried_out,
-                      kaug, vaug, qm, dom, lqt, ldot, dq_acc, dk_acc, dv_acc):
+                      kaug, vaug, qm, dom, lqt, ldot, eqt, edot, dq_acc, dk_acc, dv_acc):
     i = pl.program_id(0)
     band = band_ref[0]
     local = kaug.shape[1] // 2
@@ -202,21 +220,25 @@
                 delta = jnp.sum(jnp.where(mine, prod, 0.0), axis=1, keepdims=True)
                 qm[h] = jnp.where(mine, q_pair, place(side, split3(lse_ref[:, h : h + 1]), own).astype(bf16))
                 dom[h] = jnp.where(mine, do_pair, place(side, split3(delta), jnp.zeros_like(own)).astype(bf16))
-            zero = jnp.zeros((HEAD_DIM, BQ), bf16)
-            for pair, dst in ((q_pair, lqt), (do_pair, ldot)):
+            for pair, dst, edges in ((q_pair, lqt, eqt), (do_pair, ldot, edot)):
                 flipped = pair.T
-                dst[p, 0:HEAD_DIM, 0:BQ] = flipped[0:HEAD_DIM]
-                dst[p, HEAD_DIM:128, 0:BQ] = zero
-                dst[p, 0:HEAD_DIM, BQ : 2 * BQ] = zero
-                dst[p, HEAD_DIM:128, BQ : 2 * BQ] = flipped[HEAD_DIM:128]
+                upper = lax.broadcasted_iota(jnp.int32, flipped.shape, 0) < HEAD_DIM
+                zero = jnp.zeros_like(flipped)
+                even, odd = jnp.where(upper, flipped, zero), jnp.where(upper, zero, flipped)
+                dst[p, :, 0:BQ] = even
+                dst[p, :, BQ : 2 * BQ] = odd
+                edges[0, p] = jnp.concatenate([even[:, 0:EDGE], odd[:, 0:EDGE]], axis=1)
+                edges[1, p] = jnp.concatenate([even[:, BQ - EDGE :], odd[:, BQ - EDGE :]], axis=1)
+        lefts = {-1: (lqt, ldot), 0: (eqt.at[0], edot.at[0]), BQ - EDGE: (eqt.at[1], edot.at[1])}
         dq_acc[...] = jnp.zeros(dq_acc.shape, f32)
-        start, count = key_window(seg_own, seg_far, block, BQ, BK)
-
-        def step(j, c):
+        start, count, early, late = key_window(seg_own, seg_far, block, BQ, BK)
+
+        def step(j, part):
             window = pl.ds(pl.multiple_of(start + j * BK, 128), BK)
+            left_q, left_do = lefts[part.start if part.stop - part.start < BQ else -1]
 
             def scores(h):
-                return mm(qm[h], kaug[h, window, :], NT), mm(dom[h], vaug[h, window, :], NT)
+                return mm(qm[h, part, :], kaug[h, window, :], NT), mm(dom[h, part, :], vaug[h, window, :], NT)
 
             ahead = scores(0)
             kept = []
@@ -228,14 +250,13 @@
                 prob = jnp.exp(s)
                 ds = (prob * dp).astype(bf16)
                 kept.append((prob.astype(bf16), ds))
-                dq_acc[h] += mm(ds, kaug[h, window, :])
+                dq_acc[h, part, :] += mm(ds, kaug[h, window, :])
                 if h % 2:
-                    dv_acc[p, :, window] += mm(ldot[p], jnp.concatenate([kept[0][0], kept[1][0]], axis=0))
-                    dk_acc[p, :, window] += mm(lqt[p], jnp.concatenate([kept[0][1], kept[1][1]], axis=0))
+                    dv_acc[p, :, window] += mm(left_do[p], jnp.concatenate([kept[0][0], kept[1][0]], axis=0))
+                    dk_acc[p, :, window] += mm(left_q[p], jnp.concatenate([kept[0][1], kept[1][1]], axis=0))
                     kept = []
-            return c
-
-        lax.fori_loop(0, count, step, 0)
+
+        over_blocks(count, early, late, BQ, step)
         for p in range(PAIRS):
             pair = jnp.where(low, dq_acc[2 * p], dq_acc[2 * p + 1]) * HEAD_DIM**-0.5
             dq_ref[:, p * 128 : (p + 1) * 128] = pair.astype(bf16)
@@ -276,6 +297,8 @@
                 pltpu.VMEM((HEADS, BQ, 128), bf16),
                 pltpu.VMEM((PAIRS, 128, 2 * BQ), bf16),
                 pltpu.VMEM((PAIRS, 128, 2 * BQ), bf16),
+                pltpu.VMEM((2, PAIRS, 128, 2 * EDGE), bf16),
+                pltpu.VMEM((2, PAIRS, 128, 2 * EDGE), bf16),
                 pltpu.VMEM((HEADS, BQ, 128), f32),
                 pltpu.VMEM((PAIRS, 128, 2 * rows), f32),
                 pltpu.VMEM((PAIRS, 128, 2 * rows), f32),
@@ -318,8 +341,8 @@
 
 
 def mlp_kernel(sorted_out, blocks, rows, slices, tok_ref, att_ref, cot_ref, wproj, wup, wdown, pbias, gain, shift, ubias, dbias,
-               out_ref, rgrad_ref, agrad_ref, sums_ref, usums_ref, proj_out, *rest):
-    outs, scratch = rest[: 4 if sorted_out else 2], rest[4 if sorted_out else 2 :]
+               out_ref, rgrad_ref, agrad_ref, sums_ref, usums_ref, *rest):
+    outs, scratch = rest[: 8 if sorted_out else 3], rest[8 if sorted_out else 3 :]
     hid, ugr, n2s, bgs, ags, ats, d_own, d_far, d_in, u_in, p_own, p_far, p_in, send_sem, recv_sem = scratch
     i = pl.program_id(0)
     me, band = lax.axis_index("dp"), lax.axis_index("band")
@@ -400,45 +423,73 @@
 
     x, y = me & 1, (me >> 1) & 1
 
-    def join_down(j):
+    z = me >> 2
+    shard = width // 16
+
+    def down_arrived(j):
         d_copy(j).wait_recv()
         if not sorted_out:
             at = pl.ds(pl.multiple_of(j * SLICE, SLICE), SLICE)
             add_low(outs[0].at[at, :], d_own.at[at, :], d_in.at[at, :])
             return
-        shard = SLICE // 4
-        piece = shard // 2
         for t in range(2):
             for out, x_bit, y_bit, first in (
                 (outs[0], 1 - x, t, 0),
                 (outs[1], x, t, 0),
-                (outs[2], t, 1 - y, piece),
-                (outs[3], t, y, piece),
+                (outs[2], t, 1 - y, shard),
+                (outs[3], t, y, shard),
             ):
-                at = pl.ds(pl.multiple_of(j * SLICE + y_bit * 2 * shard + x_bit * shard + first, piece), piece)
-                add_low(out.at[j, t, 0:piece], d_own.at[at, :], d_in.at[at, :])
-
-    def join_up(c):
+                at = pl.ds(pl.multiple_of(j * SLICE + (y_bit * 2 + x_bit) * 4 * shard + first, shard), shard)
+                add_low(out.at[j, t, 0:shard], d_own.at[at, :], d_in.at[at, :])
+
+    def down_along_z(d):
+        if sorted_out:
+            for t in range(4):
+                at = pl.ds(pl.multiple_of(((z + d) & 3) * SLICE + t * 4 * shard + 2 * shard, shard), 2 * shard)
+                add_low(outs[4 + d].at[t // 2, t % 2, 0 : 2 * shard], d_own.at[at, :], d_in.at[at, :])
+
+    def up_arrived(c):
         u_copy(c).wait_recv()
         own = hid.at[0:width, (per_half + c) * SLICE : (per_half + c + 1) * SLICE]
         if not sorted_out:
             add_low(outs[1].at[:, c * SLICE : (c + 1) * SLICE], own, u_in.at[c])
             return
-        shard = width // 16
+
+        def fold(dst, s, part):
+            at = pl.ds(pl.multiple_of(s * shard, shard), shard)
+            cols = slice(part * half, (part + 1) * half)
+            add_low(dst, own.at[at, cols], u_in.at[c, at, cols])
+
+        def near(s, carry):
+            zz, t = s >> 1, s & 1
+            for sends in range(2):
+                fold(outs[1 - sends].at[zz, t, shard : 2 * shard], zz * 4 + t * 2 + (x ^ sends), 0)
+                fold(outs[3 - sends].at[zz, t, shard : 2 * shard], zz * 4 + (y ^ sends) * 2 + t, 1)
+            return carry
+
+        def along(s, carry):
+            for d in range(4):
+                for part in range(2):
+                    to = slice((2 + part) * shard, (3 + part) * shard)
+                    fold(outs[4 + d].at[s >> 1, s & 1, to], ((z + d) & 3) * 4 + s, part)
+            return carry
+
+        lax.fori_loop(0, 8 if c == 0 else 4, near if c == 0 else along, 0, unroll=2)
+
+    def proj_arrived():
+        p_copy().wait_recv()
+        if not sorted_out:
+            add_low(outs[2], p_own, p_in)
+            return
 
         def one(s, carry):
-            z, t = s >> 1, s & 1
-            for out, sends in ((outs[2 * c], 1), (outs[2 * c + 1], 0)):
-                bit = (y if c else x) ^ sends
-                x_bit, y_bit = (t, bit) if c else (bit, t)
-                at = pl.ds(pl.multiple_of((z * 4 + y_bit * 2 + x_bit) * shard, shard), shard)
-                for part in range(2):
-                    cols = slice(part * half, (part + 1) * half)
-                    to = slice((2 + part) * shard, (3 + part) * shard)
-                    add_low(out.at[z, t, to], own.at[at, cols], u_in.at[c, at, cols])
+            zz, t = s >> 1, s & 1
+            for sends in range(2):
+                at = pl.ds(pl.multiple_of((zz * 4 + t * 2 + (x ^ sends)) * shard, shard), shard)
+                add_low(outs[1 - sends].at[zz, t, 2 * shard : 3 * shard], p_own.at[at, :], p_in.at[at, :])
             return carry
 
-        lax.fori_loop(0, 8, one, 0)
+        lax.fori_loop(0, 8, one, 0, unroll=4)
 
     middle = blocks + slices
     for c in range(per_half):
@@ -448,21 +499,22 @@
         def _(c=c, at=at):
             hid[0:width, at] = up_slice((1 - band) * per_half + c)
             u_copy(c).start()
-            join_down(c)
+            for j in range(2 * c, 2 * c + 2):
+                down_arrived(j)
 
         @pl.when(i == middle + per_half + c)
         def _(c=c):
             hid[0:width, (per_half + c) * SLICE : (per_half + c + 1) * SLICE] = up_slice(band * per_half + c)
-            join_down(per_half + c)
+            for d in range(2 * c, 2 * c + 2):
+                down_along_z(d)
 
     @pl.when(i == middle + slices)
     def _():
         columns(mm(ats[...], ags[...], TN), p_own, p_far, slice(None))
         p_copy().start()
         for c in range(per_half):
-            join_up(c)
-        p_copy().wait_recv()
-        add_low(proj_out, p_own, p_in)
+            up_arrived(c)
+        proj_arrived()
         for j in range(slices):
             d_copy(j).wait_send()
         for c in range(per_half):
@@ -486,10 +538,12 @@
     vectors = (proj_bias, gain, shift, up_bias, down_bias)
     shape = jax.ShapeDtypeStruct
     if sorted_out:
-        pieces = [shape((4, 2, ff // 16, half), bf16)] * 4
+        sixteenth = width // 16
+        pieces = [shape((4, 2, n * sixteenth, half), bf16) for n in (3, 3, 2, 2)]
+        pieces += [shape((2, 2, 4 * sixteenth, half), bf16)] * 4
     else:
-        pieces = [shape((ff, half), bf16), shape((width, ff // 2), bf16)]
-    kept = [shape((8, width), f32), shape((8, ff), f32), shape((width, half), bf16)] + pieces
+        pieces = [shape((ff, half), bf16), shape((width, ff // 2), bf16), shape((width, half), bf16)]
+    kept = [shape((8, width), f32), shape((8, ff), f32)] + pieces
     low = lambda *s: pltpu.VMEM(s, bf16)
     copies = slices + per_half + 1
     return pl.pallas_call(
@@ -699,10 +753,10 @@
 
 
 def finish_kernel(
-    dq_hbm, dko_hbm, dkf_hbm, dvo_hbm, dvf_hbm, n_hbm, tok_hbm, rgrad_hbm, w_hbm, ak_hbm, ar_hbm, bk_hbm, br_hbm, proj_hbm, gain, msums, usums,
+    dq_hbm, dko_hbm, dkf_hbm, dvo_hbm, dvf_hbm, n_hbm, tok_hbm, rgrad_hbm, w_hbm, ak_hbm, bk_hbm, ck_hbm, ar_hbm, br_hbm, c1_hbm, c2_hbm, c3_hbm, gain, msums, usums,
     out, down_out, up_out, qkv_out, proj_out, vec_out, usum_out,
-    packed, dko, dko_in, dvo, dvo_in, n1, tok, wq, early, proj, cols, far_in, tail,
-    one_e, one_t, two_e, two_t, thr_e, thr_t, vec, vec_band, vec_x, vec_y, vec_z,
+    packed, dko, dko_in, dvo, dvo_in, n1, tok, wq, ak, bk, ck, cols, far_in, tail,
+    a_one, b_one, c_one, a_two, b_two, c_two, a_thr, b_thr, c_thr, ta_one, tb_one, ta_two, tb_two, ta_thr, tb_thr, vec, vec_band, vec_x, vec_y, vec_z,
     load_sem, swap_send, swap_recv, send, recv, vsend, vrecv,
 ):
     me = lax.axis_index("dp")
@@ -721,11 +775,11 @@
         return copy
 
     loads = {
-        "early": (load(0, ak_hbm, early.at[0]), load(1, ar_hbm, one_e.at[0]), load(2, bk_hbm, early.at[1]), load(3, br_hbm, one_e.at[1])),
+        "early": (load(0, ak_hbm, ak), load(1, ar_hbm, a_one), load(2, bk_hbm, bk), load(3, br_hbm, b_one)),
+        "along": (load(8, ck_hbm, ck), load(13, c1_hbm, c_one.at[0]), load(14, c2_hbm, c_one.at[1]), load(15, c3_hbm, c_one.at[2])),
         "queries": (load(6, dq_hbm, packed.at[:, 0:width]),),
         "normed": (load(7, n_hbm, n1),),
         "keys": (load(4, dko_hbm, dko), load(5, dvo_hbm, dvo)),
-        "proj": (load(8, proj_hbm, proj),),
         "weight": (load(10, w_hbm, wq),),
         "rows": (load(11, tok_hbm, tok), load(12, rgrad_hbm, out)),
     }
@@ -758,61 +812,49 @@
             body(s >> 2, (s >> 1) & 1, s & 1)
             return c
 
-        lax.fori_loop(0, 16, step, 0)
-
-    def first_stage(t, work, one, cut):
-        a, b = cut
-        return (
-            push(work.at[:, :, 1 - x, a[0], a[1]], one.at[0], peer_x, send.at[t, 0, 0], recv.at[t, 0, 0]),
-            push(work.at[:, 1 - y, :, b[0], b[1]], one.at[1], peer_y, send.at[t, 1, 0], recv.at[t, 1, 0]),
-        )
-
-    def second_stage(t, kept, one, two, copies):
-        out = []
-        for piece, mine, peer in ((0, y, peer_y), (1, x, peer_x)):
-            if copies is not None:
-                copies[piece].wait_recv()
-
-            def total(s, c, piece=piece):
-                add_low(one.at[piece, s >> 1, s & 1], one.at[piece, s >> 1, s & 1], kept(piece, s >> 1, s & 1))
-                return c
-
-            lax.fori_loop(0, 8, total, 0)
-            out.append(push(one.at[piece, :, 1 - mine], two.at[piece], peer, send.at[t, piece, 1], recv.at[t, piece, 1]))
-        return out
-
-    def third_stage(t, one, two, three, copies):
-        out = []
-        for piece, mine in ((0, y), (1, x)):
-            copies[piece].wait_recv()
-
-            def total(zz, c, piece=piece, mine=mine):
-                add_low(two.at[piece, zz], two.at[piece, zz], one.at[piece, zz, mine])
-                return c
-
-            lax.fori_loop(0, 4, total, 0)
-            for d in (1, 2, 3):
-                out.append(
-                    push(two.at[piece, (z + d) & 3], three.at[piece, d - 1], peers_z[d - 1], send.at[t, piece, 1 + d], recv.at[t, piece, 1 + d])
-                )
-        return out
-
-    def last(two, three, copies, piece):
+        lax.fori_loop(0, 16, step, 0, unroll=4)
+
+    def second_stage(t, kept, one, two, mine, peer):
+        def total(s, c):
+            add_low(one.at[s >> 1, s & 1], one.at[s >> 1, s & 1], kept(s >> 1, s & 1))
+            return c
+
+        lax.fori_loop(0, 8, total, 0, unroll=True)
+        return push(one.at[:, 1 - mine], two, peer, send.at[t, 0], recv.at[t, 0])
+
+    def third_stage(t, one, two, three, mine, copy):
+        copy.wait_recv()
+
+        def total(zz, c):
+            add_low(two.at[zz], two.at[zz], one.at[zz, mine])
+            return c
+
+        lax.fori_loop(0, 4, total, 0, unroll=True)
+        return [push(two.at[(z + d) & 3], three.at[d - 1], peers_z[d - 1], send.at[t, d], recv.at[t, d]) for d in (1, 2, 3)]
+
+    def last(two, three, copies):
+        for copy in copies:
+            copy.wait_recv()
+        total = two[z].astype(f32)
         for d in range(3):
-            copies[3 * piece + d].wait_recv()
-        total = two[piece, z].astype(f32)
+            total = total + three[d].astype(f32)
+        return total
+
+    ready("early")
+    a_copy = second_stage(0, lambda i, j: ak.at[i, j], a_one, a_two, y, peer_y)
+    b_copy = second_stage(1, lambda i, j: bk.at[i, j], b_one, b_two, x, peer_x)
+    ready("along")
+
+    def along(s, c):
+        i, j = s >> 1, s & 1
+        total = ck[i, j].astype(f32)
         for d in range(3):
-            total = total + three[piece, d].astype(f32)
-        return total
-
-    everything = slice(None)
-    wide_cut = ((everything, slice(0, 768)), (everything, slice(768, 1536)))
-
-    ready("early")
-    e_two = second_stage(0, lambda p, i, j: early.at[p, i, j], one_e, two_e, None)
-
-    def tail_kept(piece, zz, t):
-        return tail.at[zz, t, x, :, 0:768] if piece == 0 else tail.at[zz, y, t, :, 768:1536]
+            total = total + c_one[d, i, j].astype(f32)
+        ck[i, j] = total.astype(bf16)
+        return c
+
+    lax.fori_loop(0, 4, along, 0, unroll=True)
+    c_copy = push(ck.at[:, 1 - x], c_two, peer_x, send.at[2, 0], recv.at[2, 0])
 
     def columns(t):
         cols[:, :, :, :, t * width : (t + 1) * width] = (
@@ -864,14 +906,19 @@
     def _():
         swap_wide.start()
 
-    ready("proj")
-    each_shard(lambda i, j, k: put(tail.at[i, j, k, :, half : 2 * width], proj.at[i, j, k]))
-    e_three = third_stage(0, one_e, two_e, thr_e, e_two)
+    a_copies = third_stage(0, a_one, a_two, a_thr, y, a_copy)
+    b_copies = third_stage(1, b_one, b_two, b_thr, x, b_copy)
     swap_near.wait()
     swap_wide.wait()
     mine = pl.ds(pl.multiple_of(band * half, 128), half)
-    each_shard(lambda i, j, k: add_low(tail.at[i, j, k, :, 0:half], cols.at[i, j, k, :, mine], far_in.at[i, j, k]))
-    t_one = first_stage(2, tail, one_t, wide_cut)
+    each_shard(lambda i, j, k: add_low(tail.at[i, j, k], cols.at[i, j, k, :, mine], far_in.at[i, j, k]))
+    cut = ta_one.shape[-1]
+    ta_first = push(tail.at[:, :, 1 - x, :, 0:cut], ta_one, peer_x, send.at[3, 4], recv.at[3, 4])
+    tb_first = push(tail.at[:, 1 - y, :, :, cut:half], tb_one, peer_y, send.at[4, 4], recv.at[4, 4])
+    c_copy.wait_recv()
+    add_low(c_two.at[0], c_two.at[0], ck.at[0, x])
+    add_low(c_two.at[1], c_two.at[1], ck.at[1, x])
+    c_last = push(c_two.at[1 - y], c_thr, peer_y, send.at[2, 1], recv.at[2, 1])
 
     ready("weight")
     ready("rows")
@@ -895,7 +942,10 @@
     for t in range(usums.shape[1] // width):
         vec[8 + t : 9 + t, :] = usums[0:1, t * width : (t + 1) * width]
     v_band = push(vec, vec_band, peer_band, vsend.at[0], vrecv.at[0])
-    t_two = second_stage(2, tail_kept, one_t, two_t, t_one)
+    ta_first.wait_recv()
+    ta_copy = second_stage(3, lambda i, j: tail.at[i, j, x, :, 0:cut], ta_one, ta_two, y, peer_y)
+    tb_first.wait_recv()
+    tb_copy = second_stage(4, lambda i, j: tail.at[i, y, j, :, cut:half], tb_one, tb_two, x, peer_x)
     v_band.wait()
     vec_band[...] = vec[...] + vec_band[...]
     v_x = push(vec_band, vec_x, peer_x, vsend.at[1], vrecv.at[1])
@@ -905,7 +955,8 @@
     v_y.wait()
     vec_y[...] = vec_x[...] + vec_y[...]
     v_z = [push(vec_y, vec_z.at[d], peers_z[d], vsend.at[3 + d], vrecv.at[3 + d]) for d in range(3)]
-    t_three = third_stage(2, one_t, two_t, thr_t, t_two)
+    ta_copies = third_stage(3, ta_one, ta_two, ta_thr, y, ta_copy)
+    tb_copies = third_stage(4, tb_one, tb_two, tb_thr, x, tb_copy)
     for copy in v_z:
         copy.wait_recv()
     vec[...] = vec_y[...] + vec_z[0] + vec_z[1] + vec_z[2]
@@ -916,30 +967,34 @@
     row = vec[pl.ds(8 + me // per_row, 1), :]
     usum_out[...] = pltpu.roll(jnp.broadcast_to(row, (8, width)), width - (me % per_row) * wide, 1)[0:1, 0:wide]
     shard = width // 16
-    for piece in range(2):
-        early_sum = last(two_e, thr_e, e_three, piece)
-        down_out[piece * 2 * shard : (piece + 1) * 2 * shard, :] = early_sum[0 : 2 * shard]
-        for part in range(2):
-            at = (2 * piece + part) * third
-            up_out[:, at : at + third] = early_sum[(2 + part) * shard : (3 + part) * shard]
-    qkv_out[:, 0:768] = last(two_t, thr_t, t_three, 0)
-    final = last(two_t, thr_t, t_three, 1)
-    qkv_out[:, 768:half] = final[:, 0 : half - 768]
-    proj_out[...] = final[:, half - 768 :]
+    a_sum, b_sum = last(a_two, a_thr, a_copies), last(b_two, b_thr, b_copies)
+    c_last.wait_recv()
+    c_sum = c_two[y].astype(f32) + c_thr[...].astype(f32)
+    down_out[0:shard, :] = a_sum[0:shard]
+    down_out[shard : 2 * shard, :] = b_sum[0:shard]
+    down_out[2 * shard : 4 * shard, :] = c_sum[0 : 2 * shard]
+    ups = (a_sum[shard : 2 * shard], b_sum[shard : 2 * shard], c_sum[2 * shard : 3 * shard], c_sum[3 * shard : 4 * shard])
+    for t, part in enumerate(ups):
+        up_out[:, t * third : (t + 1) * third] = part
+    proj_out[...] = a_sum[2 * shard : 3 * shard]
+    qkv_out[:, 0:cut] = last(ta_two, ta_thr, ta_copies)
+    qkv_out[:, cut:half] = last(tb_two, tb_thr, tb_copies)
     done = {id(c) for c in (v_band, v_x, v_y)}
     for copy in pending:
         if id(copy) not in done:
             copy.wait_send()
 
 
-def finish(dq, dk_own, dk_far, dv_own, dv_far, normed, tokens, rgrad, w_qkv, pieces, proj, gain, msums, usums):
+def finish(dq, dk_own, dk_far, dv_own, dv_far, normed, tokens, rgrad, w_qkv, pieces, gain, msums, usums):
     rows, width = tokens.shape
     ff = usums.shape[1]
     half = 3 * width // 2
     shards = (4, 2, 2)
-    u_shape, p_shape = shards + (width // 16, ff // 2), shards + (width // 16, width // 2)
-    q_shape = shards + (width // 16, half)
-    e_piece, w_piece = (ff // 16, width // 2), (width // 16, ff // 4)
+    third, shard = width // 2, width // 16
+    q_shape = shards + (shard, half)
+    a_piece, b_piece, c_piece = (3 * shard, third), (2 * shard, third), (4 * shard, third)
+    cut = half // 256 * 128 + 128
+    ta_piece, tb_piece = (shard, cut), (shard, half - cut)
     hbm, vmem = pl.BlockSpec(memory_space=pl.ANY), pl.BlockSpec(memory_space=pltpu.VMEM)
     shape = jax.ShapeDtypeStruct
     low = lambda *s: pltpu.VMEM(s, bf16)
@@ -955,7 +1010,7 @@
             shape((8, width // 16), f32),
             shape((1, ff // 16), f32),
         ),
-        in_specs=[hbm] * 14 + [vmem] * 3,
+        in_specs=[hbm] * 17 + [vmem] * 3,
         out_specs=[vmem] * 7,
         scratch_shapes=[
             low(rows, 3 * width),
@@ -963,34 +1018,44 @@
             low(rows, width),
             pltpu.VMEM((rows, width), f32),
             low(width, 3 * width),
-            low(2, 4, 2, *e_piece),
-            low(*p_shape),
-            low(*shards, width // 16, 3 * width),
+            low(4, 2, *a_piece),
+            low(4, 2, *b_piece),
+            low(2, 2, *c_piece),
+            low(*shards, shard, 3 * width),
             low(*q_shape),
-            low(*u_shape),
-            low(2, 4, 2, *e_piece),
-            low(2, 4, 2, *w_piece),
-            low(2, 4, *e_piece),
-            low(2, 4, *w_piece),
-            low(2, 3, *e_piece),
-            low(2, 3, *w_piece),
+            low(*q_shape),
+            low(4, 2, *a_piece),
+            low(4, 2, *b_piece),
+            low(3, 2, 2, *c_piece),
+            low(4, *a_piece),
+            low(4, *b_piece),
+            low(2, *c_piece),
+            low(3, *a_piece),
+            low(3, *b_piece),
+            low(*c_piece),
+            low(4, 2, *ta_piece),
+            low(4, 2, *tb_piece),
+            low(4, *ta_piece),
+            low(4, *tb_piece),
+            low(3, *ta_piece),
+            low(3, *tb_piece),
             pltpu.VMEM((16, width), f32),
             pltpu.VMEM((16, width), f32),
             pltpu.VMEM((16, width), f32),
             pltpu.VMEM((16, width), f32),
             pltpu.VMEM((3, 16, width), f32),
-            dma((13,)),
+            dma((16,)),
             dma((4,)),
             dma((4,)),
-            dma((3, 2, 5)),
-            dma((3, 2, 5)),
+            dma((5, 5)),
+            dma((5, 5)),
             dma((6,)),
             dma((6,)),
         ],
         compiler_params=pltpu.CompilerParams(vmem_limit_bytes=52 * MIB, collective_id=0, has_side_effects=True),
         cost_estimate=pl.CostEstimate(flops=20 * 10**9, bytes_accessed=40 * 10**6, transcendentals=0),
         name="finish",
-    )(dq, dk_own, dk_far, dv_own, dv_far, normed, tokens, rgrad, w_qkv, *pieces, proj.reshape(p_shape),
+    )(dq, dk_own, dk_far, dv_own, dv_far, normed, tokens, rgrad, w_qkv, *pieces,
       gain, msums, usums)
 
 
@@ -1030,7 +1095,7 @@
         return self.x
 
 
-def finish_any(size, band_at, query_grad, dk_own, dk_far, dv_own, dv_far, normed, tokens, residual_grad, w_qkv, pieces, proj, gain, msums, usums):
+def finish_any(size, band_at, query_grad, dk_own, dk_far, dv_own, dv_far, normed, tokens, residual_grad, w_qkv, pieces, gain, msums, usums):
     width = tokens.shape[1]
     rising = list(range(size.bit_length() - 1))
     turned = [1, 0] + rising[2:]
@@ -1055,7 +1120,7 @@
         total(pieces[0], rising),
         total(pieces[1], turned),
         total(join(qkv_own, qkv_far), rising),
-        total(proj, turned),
+        total(pieces[2], turned),
         [thin_sum[:, t] for t in range(8)],
         thin_sum[:, 8 : 8 + ups].reshape(-1),
     )
@@ -1091,7 +1156,7 @@
     )
     keys = (seg_own, seg_far, k_own, k_far, v_own, v_far)
     attended, log_totals = attend_forward(band_at, queries, *keys)
-    output, residual_grad, attended_grad, mlp_sums, up_sums, proj, *pieces = mlp(
+    output, residual_grad, attended_grad, mlp_sums, up_sums, *pieces = mlp(
         size,
         tokens,
         attended,
@@ -1107,22 +1172,20 @@
     )
     if size == 16:
         turns = [[(i, i ^ bit) for i in range(size)] for bit in (1, 2)]
-        pieces = [
-            part
-            for t in range(2)
-            for part in (pieces[2 * t + 1], lax.ppermute(pieces[2 * t], "dp", turns[t]))
-        ]
+        turns += [[(i, (i + 4 * d) % size) for i in range(size)] for d in (1, 2, 3)]
+        sent = (pieces[0], pieces[2], *pieces[5:8])
+        pieces = [pieces[1], pieces[3], pieces[4]] + [lax.ppermute(a, "dp", turn) for a, turn in zip(sent, turns)]
     query_grad, dk_own, dk_far, dv_own, dv_far, output = attend_backward(
         band_at, output, queries, attended_grad, attended, log_totals, *keys
     )
     if size == 16:
         input_grad, down_sum, up_sum, qkv_sum, proj_sum, vec, up_vec = finish(
-            query_grad, dk_own, dk_far, dv_own, dv_far, normed, tokens, residual_grad, w_qkv, pieces, proj, first_gain, mlp_sums, up_sums
+            query_grad, dk_own, dk_far, dv_own, dv_far, normed, tokens, residual_grad, w_qkv, pieces, first_gain, mlp_sums, up_sums
         )
         vectors, up_vector = [vec[t] for t in range(8)], up_vec.reshape(-1)
     else:
         input_grad, down_sum, up_sum, qkv_sum, proj_sum, vectors, up_vector = finish_any(
-            size, band_at, query_grad, dk_own, dk_far, dv_own, dv_far, normed, tokens, residual_grad, w_qkv, pieces, proj, first_gain, mlp_sums, up_sums
+            size, band_at, query_grad, dk_own, dk_far, dv_own, dv_far, normed, tokens, residual_grad, w_qkv, pieces, first_gain, mlp_sums, up_sums
         )
     return (
         output.reshape(local_shape),

time: 231 us -> 224 us (0.970)
  Pallas kernels: 216 us -> 203 us
  starting transfers between devices: 4.53 us -> 9.69 us
    pallas_call x1, Pallas kernels: 63.5 us -> 51.2 us  [finish(): pl.pallas_call(finish_kernel, out_shape=(shape((rows, width), f32), shape...]
    ppermute x2 -> x5, starting transfers between devices: 4.53 us -> 9.69 us  [local(): lax.ppermute(a, 'dp', turn)]
    unnamed x18 -> x24, local copies, waits for them, and re-layouts: 8.45 us -> 8.68 us
  transfers between devices with their start and end apart: 2 -> 5, of which waited for: 0 -> 0; matrix products, arithmetic and copies ran while one was open for 0% -> 0% of each run, Pallas kernels for 23% -> 24%
where the time goes in v4:
time: 224 us; the launch traced here: 223 us
  Pallas kernels  203 us (91%)
  starting transfers between devices  9.69 us (4%)
  local copies, waits for them, and re-layouts  9.22 us (4%)
    pallas_call x1, Pallas kernels, mlp(): pl.pallas_call(functools.partial(mlp_kernel, sorted_out, blocks, rows, sl...  53.5 us
    pallas_call x1, Pallas kernels, attend_backward(): pl.pallas_call(functools.partial(attend_bwd_kernel, fills, steps, BQ, BK)...  52.9 us
    pallas_call x1, Pallas kernels, finish(): pl.pallas_call(finish_kernel, out_shape=(shape((rows, width), f32), shape...  51.2 us
    pallas_call x1, Pallas kernels, attend_forward(): pl.pallas_call(functools.partial(attend_fwd_kernel, fills, BQ, BK), out_s...  33.4 us
    pallas_call x1, Pallas kernels, project_qkv(): pl.pallas_call(functools.partial(qkv_kernel, steps), out_shape=(low,) * 6...  12.4 us
    ppermute x5, starting transfers between devices, local(): lax.ppermute(a, 'dp', turn)  9.69 us
    unnamed x24, local copies, waits for them, and re-layouts  8.68 us
  transfers between devices with their start and end apart: 5, of which 0 were waited for; matrix products, arithmetic and copies ran while one was open for 0% of the time, Pallas kernels for 24%

profile of v4, /device:TPU:0, one launch (start us, length us, event | category | flops | bytes accessed | tf_op | source)
XLA Modules:
  0.0 223.2 jit_solution(9433577981839608712)
XLA Ops:
  0.6 12.4 %project_qkv.1 = (bf16[1024,768]{1,0:T(8,128)(2,1)}, bf16[1024,768]{1,0:T(8,128)(2,1)}, bf16[1024,768]{1,0:T(8,128)(2,1)}, bf16[1024,768]{1,0:T(8,128)(2,1)}, bf...) custom-call(f32[1024,768]{1,0:T(8,128)} %bitcast.25, s32[1,1024]{1,0:T(1,128)} %seg_own.3, ...), custom_call_target="tpu_custom_call" | custom-call | flops 4000000000 | bytes 13000000 | tf_op jit(solution)/shard_map/project_qkv/pallas_call | solution.py:635
  13.1 33.4 %attend_forward.1 = (bf16[1024,768]{1,0:T(8,128)(2,1)}, f32[1024,128]{1,0:T(8,128)}) custom-call(s32[1]{0:T(128)} %bitcast.band_ref, bf16[1024,768]{1,0:T(8,128)(2,1)} %get-tuple-element.50.q_ref, bf16[1024,768]{1,0:T(8,128)(2,1)} %get-tuple-element.51.k_own, bf16[1024,768]{1,0:T(8,128)(2,1)} %get-tuple-element.52.k_far, ...), custom_call_target="tpu_custom_call" | custom-call | flops 30000001024 | bytes 10000000 | tf_op jit(solution)/shard_map/attend_forward/pallas_call | solution.py:165
  46.5 53.5 %mlp.1 = (f32[1024,768]{1,0:T(8,128)}, f32[1024,768]{1,0:T(8,128)}, bf16[1024,768]{1,0:T(8,128)(2,1)}, f32[8,768]{1,0:T(8,128)}, f32[8,3072]{1,0:T(8,128)}, /*in...) custom-call(f32[1024,768]{1,0:T(8,128)} %bitcast.26, ...), custom_call_target="tpu_custom_call" | custom-call | flops 40000000000 | bytes 40000000 | tf_op jit(solution)/shard_map/mlp/pallas_call | solution.py:549
  100.0 1.9 collective-permute-start.1
  101.9 0.3 collective-permute-start.2
  102.2 4.6 %collective-permute-start.3 = (bf16[2,2,192,384]{3,2,1,0:T(8,128)(2,1)}, bf16[2,2,192,384]{3,2,1,0:T(8,128)(2,1)S(1)}, u32[]{:S(2)}, u32[]{:S(2)}) collective-permute-start(bf16[2,2,192,384]{3,2,1,0:T(8,128)(2,1)} %get-tuple-element.74), channel_id=1, source_target_pairs={{0,16},{2,18},{4,20},{6,22},{8,24},{10,26},{12,28},{14,30},{16,0},... | collective-permute-start | bytes 1769480 | tf_op jit(solution)/shard_map/ppermute | solution.py:1177
  106.8 1.3 collective-permute-start.4
  108.1 1.6 collective-permute-start
  109.7 0.0 copy-start
  109.7 0.0 copy-start.1
  109.7 0.0 copy-start.2
  109.7 0.0 copy-start.3
  109.7 52.9 %attend_backward.1 = (bf16[1024,768]{1,0:T(8,128)(2,1)}, bf16[768,1024]{1,0:T(8,128)(2,1)}, bf16[768,1024]{1,0:T(8,128)(2,1)}, bf16[768,1024]{1,0:T(8,128)(2,1)}...) custom-call(s32[1]{0:T(128)} %bitcast.band_ref, bf16[1024,768]{1,0:T(8,128)(2,1)} %get-tuple-element.50.q_ref, ...), custom_call_target="tpu_custom_call" | custom-call | flops 44999999488 | bytes 20000000 | tf_op jit(solution)/shard_map/attend_backward/pallas_call | solution.py:285
  162.6 0.0 collective-permute-done.1.br_hbm
  162.7 0.0 copy-start.5
  162.7 0.0 collective-permute-done.2.c1_hbm
  162.7 0.0 copy-start.6
  162.7 0.0 collective-permute-done.3.c2_hbm
  162.7 0.0 copy-start.7
  162.7 0.0 collective-permute-done.4.c3_hbm
  162.7 0.0 copy-start.8
  162.7 0.0 collective-permute-done.ar_hbm
  162.7 0.0 copy-start.4
  162.7 0.7 copy-done.5
  163.5 0.2 copy-done.6
  163.7 0.2 copy-done.7
  163.9 0.2 copy-done.8
  164.1 0.3 copy-done.4
  164.3 0.0 copy-done
  164.3 0.0 copy-done.1
  164.3 0.0 copy-done.2
  164.3 0.0 copy-done.3
  164.4 51.2 %finish.1 = (f32[1024,768]{1,0:T(8,128)}, f32[192,384]{1,0:T(8,128)S(1)}, f32[48,1536]{1,0:T(8,128)S(1)}, f32[48,1152]{1,0:T(8,128)S(1)}, f32[48,384]{1,0:T(8,12...) custom-call(bf16[1024,768]{1,0:T(8,128)(2,1)} %get-tuple-element.61.dq_hbm, ...), custom_call_target="tpu_custom_call" | custom-call | flops 20000000000 | bytes 40000000 | tf_op jit(solution)/shard_map/finish/pallas_call | solution.py:1002
  215.6 0.5 slice_bitcast_fusion
  216.1 3.8 %copy.37 = f32[1,1024,768]{2,1,0:T(8,128)} copy(f32[1,1024,768]{2,1,0:T(8,128)} %bitcast.23) | data formatting | bytes 6291456
  219.9 0.7 copy.38
  220.6 0.6 copy.39
  221.2 0.7 copy.40
  221.9 0.6 copy.41
  222.5 0.7 copy.42
Async XLA Ops:
  100.0 62.6 %collective-permute-start.1 = (bf16[4,2,96,384]{3,2,1,0:T(8,128)(2,1)}, bf16[4,2,96,384]{3,2,1,0:T(8,128)(2,1)S(1)}, u32[]{:S(2)}, u32[]{:S(2)}) collective-permute-start(bf16[4,2,96,384]{3,2,1,0:T(8,128)(2,1)} %get-tuple-element.72), channel_id=1, source_target_pairs={{0,4},{2,6},{4,0},{6,2},{8,12},{10,14},{12,8},{14,10},{16,20},{18,... | collective-permute-start | bytes 1769480 | tf_op jit(solution)/shard_map/ppermute | solution.py:1177
  101.9 60.8 %collective-permute-start.2 = (bf16[2,2,192,384]{3,2,1,0:T(8,128)(2,1)}, bf16[2,2,192,384]{3,2,1,0:T(8,128)(2,1)S(1)}, u32[]{:S(2)}, u32[]{:S(2)}) collective-permute-start(bf16[2,2,192,384]{3,2,1,0:T(8,128)(2,1)} %get-tuple-element.73), channel_id=1, source_target_pairs={{0,8},{2,10},{4,12},{6,14},{8,16},{10,18},{12,20},{14,22},{16,24},... | collective-permute-start | bytes 1769480 | tf_op jit(solution)/shard_map/ppermute | solution.py:1177
  102.2 60.5 %collective-permute-start.3 = (bf16[2,2,192,384]{3,2,1,0:T(8,128)(2,1)}, bf16[2,2,192,384]{3,2,1,0:T(8,128)(2,1)S(1)}, u32[]{:S(2)}, u32[]{:S(2)}) collective-permute-start(bf16[2,2,192,384]{3,2,1,0:T(8,128)(2,1)} %get-tuple-element.74), channel_id=1, source_target_pairs={{0,16},{2,18},{4,20},{6,22},{8,24},{10,26},{12,28},{14,30},{16,0},... | collective-permute-start | bytes 1769480 | tf_op jit(solution)/shard_map/ppermute | solution.py:1177
  106.8 55.9 %collective-permute-start.4 = (bf16[2,2,192,384]{3,2,1,0:T(8,128)(2,1)}, bf16[2,2,192,384]{3,2,1,0:T(8,128)(2,1)S(1)}, u32[]{:S(2)}, u32[]{:S(2)}) collective-permute-start(bf16[2,2,192,384]{3,2,1,0:T(8,128)(2,1)} %get-tuple-element.75), channel_id=1, source_target_pairs={{0,24},{2,26},{4,28},{6,30},{8,0},{10,2},{12,4},{14,6},{16,8},{18,... | collective-permute-start | bytes 1769480 | tf_op jit(solution)/shard_map/ppermute | solution.py:1177
  108.1 54.6 %collective-permute-start = (bf16[4,2,144,384]{3,2,1,0:T(8,128)(2,1)}, bf16[4,2,144,384]{3,2,1,0:T(8,128)(2,1)S(1)}, u32[]{:S(2)}, u32[]{:S(2)}) collective-permute-start(bf16[4,2,144,384]{3,2,1,0:T(8,128)(2,1)} %get-tuple-element.71), channel_id=1, source_target_pairs={{0,2},{2,0},{4,6},{6,4},{8,10},{10,8},{12,14},{14,12},{16,18},{18,... | collective-permute-start | bytes 2654216 | tf_op jit(solution)/shard_map/ppermute | solution.py:1177
  109.7 54.6 %copy-start = (f32[768]{0:T(1024)S(1)}, f32[768]{0:T(1024)}, u32[]{:S(2)}) copy-start(f32[768]{0:T(1024)} %gain.5) | copy-start | bytes 9220
  109.7 54.6 %copy-start.1 = (bf16[4,2,96,384]{3,2,1,0:T(8,128)(2,1)S(1)}, bf16[4,2,96,384]{3,2,1,0:T(8,128)(2,1)}, u32[]{:S(2)}) copy-start(bf16[4,2,96,384]{3,2,1,0:T(8,128)(2,1)} %get-tuple-element.69.bk_hbm) | copy-start | bytes 1769476
  109.7 54.6 %copy-start.2 = (f32[8,3072]{1,0:T(8,128)S(1)}, f32[8,3072]{1,0:T(8,128)}, u32[]{:S(2)}) copy-start(f32[8,3072]{1,0:T(8,128)} %get-tuple-element.77.usums) | copy-start | bytes 294916
  109.7 54.6 %copy-start.3 = (f32[8,768]{1,0:T(8,128)S(1)}, f32[8,768]{1,0:T(8,128)}, u32[]{:S(2)}) copy-start(f32[8,768]{1,0:T(8,128)} %get-tuple-element.76.msums) | copy-start | bytes 73732
  162.7 0.8 copy-start.5
  162.7 1.0 copy-start.6
  162.7 1.2 copy-start.7
  162.7 1.4 copy-start.8
  162.7 1.6 copy-start.4

commit v5 on v4

--- a/solution.py
+++ b/solution.py
@@ -99,7 +99,7 @@
 
 
 def attend_fwd_kernel(fills, BQ, BK, band_ref, q_ref, k_own, k_far, v_own, v_far,
-                      seg_own, seg_far, o_ref, lse_ref, kaug, vaug, qm, s_all, mx, acc):
+                      seg_own, seg_far, o_ref, qaug_ref, kaug, vaug, qm, s_all, mx, acc):
     i = pl.program_id(0)
 
     @pl.when(i < fills)
@@ -143,16 +143,15 @@
                 acc[h, part, :] += mm(p, vaug[h, pl.ds(at, BK), :])
 
         over_blocks(count, early, late, BQ, second)
-        lane = lax.broadcasted_iota(jnp.int32, (BQ, 128), 1)
-        lse = jnp.zeros((BQ, 128), f32)
+        ids = (side == ids).astype(f32)
         for p in range(PAIRS):
             even, odd = acc[2 * p], acc[2 * p + 1]
-            swapped = pltpu.roll(even, HEAD_DIM, 1)
-            total = jnp.where(low, swapped, pltpu.roll(odd, HEAD_DIM, 1))
+            total = jnp.where(low, pltpu.roll(even, HEAD_DIM, 1), pltpu.roll(odd, HEAD_DIM, 1))
             o_ref[:, p * 128 : (p + 1) * 128] = (jnp.where(low, even, odd) / total).astype(bf16)
-            lse = jnp.where(lane == 2 * p, mx[2 * p] + jnp.log(swapped), lse)
-            lse = jnp.where(lane == 2 * p + 1, mx[2 * p + 1] + jnp.log(odd), lse)
-        lse_ref[...] = lse
+            pair = q_ref[:, p * 128 : (p + 1) * 128]
+            extra = [place(side, split3(mx[2 * p + e] + jnp.log(sums)), ids).astype(bf16) for e, sums in enumerate((even, odd))]
+            qaug_ref[2 * p] = jnp.where(low, pair, extra[0])
+            qaug_ref[2 * p + 1] = jnp.where(low, extra[1], pair)
 
 
 def attend_forward(band, q, seg_own, seg_far, k_own, k_far, v_own, v_far, BQ=256, BK=256):
@@ -164,12 +163,12 @@
     thin = pl.BlockSpec((1, rows), lambda i, *_: (0, 0))
     return pl.pallas_call(
         functools.partial(attend_fwd_kernel, fills, BQ, BK),
-        out_shape=(jax.ShapeDtypeStruct((rows, width), bf16), jax.ShapeDtypeStruct((rows, 128), f32)),
+        out_shape=(jax.ShapeDtypeStruct((rows, width), bf16), jax.ShapeDtypeStruct((HEADS, rows, 128), bf16)),
         grid_spec=pltpu.PrefetchScalarGridSpec(
             num_scalar_prefetch=1,
             grid=(fills + steps,),
             in_specs=[pl.BlockSpec((BQ, width), mine), wide, wide, wide, wide, thin, thin],
-            out_specs=[pl.BlockSpec((BQ, width), mine), pl.BlockSpec((BQ, 128), mine)],
+            out_specs=[pl.BlockSpec((BQ, width), mine), pl.BlockSpec((HEADS, BQ, 128), lambda i, *_: (0, jnp.clip(i - fills, 0, steps - 1), 0))],
             scratch_shapes=[
                 pltpu.VMEM((HEADS, 2 * rows, 128), bf16),
                 pltpu.VMEM((HEADS, 2 * rows, 128), bf16),
@@ -185,9 +184,9 @@
     )(band, q, k_own, k_far, v_own, v_far, seg_own, seg_far)
 
 
-def attend_bwd_kernel(fills, steps, BQ, BK, band_ref, q_ref, do_ref, o_ref, lse_ref,
+def attend_bwd_kernel(fills, steps, BQ, BK, band_ref, qm, do_ref, o_ref,
                       k_own, k_far, v_own, v_far, seg_own, seg_far, carried, dq_ref, dkt_own, dkt_far, dvt_own, dvt_far, carried_out,
-                      kaug, vaug, qm, dom, lqt, ldot, eqt, edot, dq_acc, dk_acc, dv_acc):
+                      kaug, vaug, dom, lqt, ldot, eqt, edot, dq_acc, dk_acc, dv_acc):
     i = pl.program_id(0)
     band = band_ref[0]
     local = kaug.shape[1] // 2
@@ -208,18 +207,19 @@
         low, side = low_lanes(BQ), side_lanes(BQ)
         block = i - fills
         carried_out[...] = carried[...]
-        ids = as_column(seg_own[:, pl.ds(pl.multiple_of(block * BQ, BQ), BQ)])
-        own = (side == ids).astype(f32)
+        lane = lax.broadcasted_iota(jnp.int32, (256, 256), 0) & 127
+        column = lax.broadcasted_iota(jnp.int32, (256, 256), 1)
+        adder = ((lane < HEAD_DIM) == (column < 128)).astype(f32).astype(bf16)
         for p in range(PAIRS):
             cols = slice(p * 128, (p + 1) * 128)
-            q_pair, do_pair = q_ref[:, cols], do_ref[:, cols]
+            q_pair, do_pair = jnp.where(low, qm[2 * p], qm[2 * p + 1]), do_ref[:, cols]
             prod = do_pair.astype(f32) * o_ref[:, cols].astype(f32)
+            high = prod.astype(bf16)
+            rest = (prod - high.astype(f32)).astype(bf16)
+            delta = mm(jnp.concatenate([high, rest], axis=1), adder)
             for e in range(2):
-                mine = low if e == 0 else jnp.logical_not(low)
-                h = 2 * p + e
-                delta = jnp.sum(jnp.where(mine, prod, 0.0), axis=1, keepdims=True)
-                qm[h] = jnp.where(mine, q_pair, place(side, split3(lse_ref[:, h : h + 1]), own).astype(bf16))
-                dom[h] = jnp.where(mine, do_pair, place(side, split3(delta), jnp.zeros_like(own)).astype(bf16))
+                extra = place(side, split3(delta[:, e * 128 : (e + 1) * 128]), jnp.zeros((BQ, 128), f32)).astype(bf16)
+                dom[2 * p + e] = jnp.where(low, do_pair, extra) if e == 0 else jnp.where(low, extra, do_pair)
             for pair, dst, edges in ((q_pair, lqt, eqt), (do_pair, ldot, edot)):
                 flipped = pair.T
                 upper = lax.broadcasted_iota(jnp.int32, flipped.shape, 0) < HEAD_DIM
@@ -272,8 +272,8 @@
                 dv_out[rows, :] = dv_acc[p, :, cols].astype(bf16)
 
 
-def attend_backward(band, carried, q, do, o, lse, seg_own, seg_far, k_own, k_far, v_own, v_far, BQ=256, BK=256):
-    rows, width = q.shape
+def attend_backward(band, carried, qaug, do, o, seg_own, seg_far, k_own, k_far, v_own, v_far, BQ=256, BK=256):
+    rows, width = do.shape
     fills, steps = rows // CHUNK, rows // BQ
     mine = lambda i, *_: (jnp.clip(i - fills, 0, steps - 1), 0)
     fill = lambda i, *_: (jnp.minimum(i, fills - 1), 0)
@@ -288,12 +288,11 @@
         grid_spec=pltpu.PrefetchScalarGridSpec(
             num_scalar_prefetch=1,
             grid=(fills + steps + fills,),
-            in_specs=[block, block, block, pl.BlockSpec((BQ, 128), mine), wide, wide, wide, wide, thin, thin, block],
+            in_specs=[pl.BlockSpec((HEADS, BQ, 128), lambda i, *_: (0, jnp.clip(i - fills, 0, steps - 1), 0)), block, block, wide, wide, wide, wide, thin, thin, block],
             out_specs=[block] + [pl.BlockSpec((width, CHUNK), drain)] * 4 + [block],
             scratch_shapes=[
                 pltpu.VMEM((HEADS, 2 * rows, 128), bf16),
                 pltpu.VMEM((HEADS, 2 * rows, 128), bf16),
-                pltpu.VMEM((HEADS, BQ, 128), bf16),
                 pltpu.VMEM((HEADS, BQ, 128), bf16),
                 pltpu.VMEM((PAIRS, 128, 2 * BQ), bf16),
                 pltpu.VMEM((PAIRS, 128, 2 * BQ), bf16),
@@ -307,7 +306,7 @@
         compiler_params=pltpu.CompilerParams(vmem_limit_bytes=56 * MIB),
         cost_estimate=pl.CostEstimate(flops=45 * 10**9, bytes_accessed=20 * 10**6, transcendentals=0),
         name="attend_backward",
-    )(band, q, do, o, lse, k_own, k_far, v_own, v_far, seg_own, seg_far, carried)
+    )(band, qaug, do, o, k_own, k_far, v_own, v_far, seg_own, seg_far, carried)
 
 
 MESH = pl.DeviceIdType.MESH
@@ -590,8 +589,13 @@
     def _():
         barrier = pltpu.get_barrier_semaphore()
         pl.semaphore_signal(barrier, inc=1, device_id=other, device_id_type=MESH)
-        pl.semaphore_wait(barrier, 1)
+
+    @pl.when(i == 1)
+    def _():
+        pl.semaphore_wait(pltpu.get_barrier_semaphore(), 1)
         segs.start()
+        for copy in copies(0):
+            copy.start()
 
     @pl.when(i < steps)
     def _():
@@ -603,11 +607,14 @@
         k = mm(n1, w_ref[:, width : 2 * width]).astype(bf16)
         k_ref[...] = k
         k_all[here, :] = k
-        copies(i)[0].start()
         v = (mm(n1, w_ref[:, 2 * width :]) + as_row(vbias)).astype(bf16)
         v_ref[...] = v
         v_all[here, :] = v
-        copies(i)[1].start()
+
+    @pl.when((i >= 1) & (i < steps))
+    def _():
+        for copy in copies(i):
+            copy.start()
 
     @pl.when(i >= steps)
     def _():
@@ -754,7 +761,7 @@
 
 def finish_kernel(
     dq_hbm, dko_hbm, dkf_hbm, dvo_hbm, dvf_hbm, n_hbm, tok_hbm, rgrad_hbm, w_hbm, ak_hbm, bk_hbm, ck_hbm, ar_hbm, br_hbm, c1_hbm, c2_hbm, c3_hbm, gain, msums, usums,
-    out, down_out, up_out, qkv_out, proj_out, vec_out, usum_out,
+    out, down_out, wide_out, vec_out, usum_out,
     packed, dko, dko_in, dvo, dvo_in, n1, tok, wq, ak, bk, ck, cols, far_in, tail,
     a_one, b_one, c_one, a_two, b_two, c_two, a_thr, b_thr, c_thr, ta_one, tb_one, ta_two, tb_two, ta_thr, tb_thr, vec, vec_band, vec_x, vec_y, vec_z,
     load_sem, swap_send, swap_recv, send, recv, vsend, vrecv,
@@ -949,14 +956,14 @@
     v_band.wait()
     vec_band[...] = vec[...] + vec_band[...]
     v_x = push(vec_band, vec_x, peer_x, vsend.at[1], vrecv.at[1])
+    ta_copies = third_stage(3, ta_one, ta_two, ta_thr, y, ta_copy)
+    tb_copies = third_stage(4, tb_one, tb_two, tb_thr, x, tb_copy)
     v_x.wait()
     vec_x[...] = vec_band[...] + vec_x[...]
     v_y = push(vec_x, vec_y, peer_y, vsend.at[2], vrecv.at[2])
     v_y.wait()
     vec_y[...] = vec_x[...] + vec_y[...]
     v_z = [push(vec_y, vec_z.at[d], peers_z[d], vsend.at[3 + d], vrecv.at[3 + d]) for d in range(3)]
-    ta_copies = third_stage(3, ta_one, ta_two, ta_thr, y, ta_copy)
-    tb_copies = third_stage(4, tb_one, tb_two, tb_thr, x, tb_copy)
     for copy in v_z:
         copy.wait_recv()
     vec[...] = vec_y[...] + vec_z[0] + vec_z[1] + vec_z[2]
@@ -975,10 +982,10 @@
     down_out[2 * shard : 4 * shard, :] = c_sum[0 : 2 * shard]
     ups = (a_sum[shard : 2 * shard], b_sum[shard : 2 * shard], c_sum[2 * shard : 3 * shard], c_sum[3 * shard : 4 * shard])
     for t, part in enumerate(ups):
-        up_out[:, t * third : (t + 1) * third] = part
-    proj_out[...] = a_sum[2 * shard : 3 * shard]
-    qkv_out[:, 0:cut] = last(ta_two, ta_thr, ta_copies)
-    qkv_out[:, cut:half] = last(tb_two, tb_thr, tb_copies)
+        wide_out[:, half + t * third : half + (t + 1) * third] = part
+    wide_out[:, half + 4 * third :] = a_sum[2 * shard : 3 * shard]
+    wide_out[:, 0:cut] = last(ta_two, ta_thr, ta_copies)
+    wide_out[:, cut:half] = last(tb_two, tb_thr, tb_copies)
     done = {id(c) for c in (v_band, v_x, v_y)}
     for copy in pending:
         if id(copy) not in done:
@@ -1004,14 +1011,12 @@
         out_shape=(
             shape((rows, width), f32),
             shape((ff // 16, width // 2), f32),
-            shape((width // 16, ff // 2), f32),
-            shape((width // 16, half), f32),
-            shape((width // 16, width // 2), f32),
+            shape((width // 16, half + ff // 2 + width // 2), f32),
             shape((8, width // 16), f32),
             shape((1, ff // 16), f32),
         ),
         in_specs=[hbm] * 17 + [vmem] * 3,
-        out_specs=[vmem] * 7,
+        out_specs=[vmem] * 5,
         scratch_shapes=[
             low(rows, 3 * width),
             *([low(width, rows)] * 4),
@@ -1155,7 +1160,7 @@
         tokens, seg_own, w_qkv, first_gain, first_bias, query_bias, value_bias
     )
     keys = (seg_own, seg_far, k_own, k_far, v_own, v_far)
-    attended, log_totals = attend_forward(band_at, queries, *keys)
+    attended, query_lanes = attend_forward(band_at, queries, *keys)
     output, residual_grad, attended_grad, mlp_sums, up_sums, *pieces = mlp(
         size,
         tokens,
@@ -1176,12 +1181,14 @@
         sent = (pieces[0], pieces[2], *pieces[5:8])
         pieces = [pieces[1], pieces[3], pieces[4]] + [lax.ppermute(a, "dp", turn) for a, turn in zip(sent, turns)]
     query_grad, dk_own, dk_far, dv_own, dv_far, output = attend_backward(
-        band_at, output, queries, attended_grad, attended, log_totals, *keys
+        band_at, output, query_lanes, attended_grad, attended, *keys
     )
     if size == 16:
-        input_grad, down_sum, up_sum, qkv_sum, proj_sum, vec, up_vec = finish(
+        input_grad, down_sum, wide_sum, vec, up_vec = finish(
             query_grad, dk_own, dk_far, dv_own, dv_far, normed, tokens, residual_grad, w_qkv, pieces, first_gain, mlp_sums, up_sums
         )
+        first, second = 3 * width // 2, 3 * width // 2 + w_up.shape[1] // 2
+        qkv_sum, up_sum, proj_sum = wide_sum[:, :first], wide_sum[:, first:second], wide_sum[:, second:]
         vectors, up_vector = [vec[t] for t in range(8)], up_vec.reshape(-1)
     else:
         input_grad, down_sum, up_sum, qkv_sum, proj_sum, vectors, up_vector = finish_any(

time: 224 us -> 216 us (0.964)
  Pallas kernels: 203 us -> 195 us
    pallas_call x1, Pallas kernels: 52.9 us -> 48.2 us  [attend_backward(): pl.pallas_call(functools.partial(attend_bwd_kernel, fills, steps, BQ, BK)...]
    pallas_call x1, Pallas kernels: 51.2 us -> 47.7 us  [finish(): pl.pallas_call(finish_kernel, out_shape=(shape((rows, width), f32), shape...]
    unnamed x24 -> x21, local copies, waits for them, and re-layouts: 8.68 us -> 6.65 us
  transfers between devices with their start and end apart: 5 -> 5, of which waited for: 0 -> 0; matrix products, arithmetic and copies ran while one was open for 0% -> 0% of each run, Pallas kernels for 24% -> 22%
where the time goes in v5:
time: 216 us; the launch traced here: 215 us
  Pallas kernels  195 us (90%)
  starting transfers between devices  10 us (5%)
  local copies, waits for them, and re-layouts  9.26 us (4%)
    pallas_call x1, Pallas kernels, mlp(): pl.pallas_call(functools.partial(mlp_kernel, sorted_out, blocks, rows, sl...  53.5 us
    pallas_call x1, Pallas kernels, attend_backward(): pl.pallas_call(functools.partial(attend_bwd_kernel, fills, steps, BQ, BK)...  48.2 us
    pallas_call x1, Pallas kernels, finish(): pl.pallas_call(finish_kernel, out_shape=(shape((rows, width), f32), shape...  47.7 us
    pallas_call x1, Pallas kernels, attend_forward(): pl.pallas_call(functools.partial(attend_fwd_kernel, fills, BQ, BK), out_s...  34.9 us
    pallas_call x1, Pallas kernels, project_qkv(): pl.pallas_call(functools.partial(qkv_kernel, steps), out_shape=(low,) * 6...  11 us
    ppermute x5, starting transfers between devices, local(): lax.ppermute(a, 'dp', turn)  10 us
    unnamed x21, local copies, waits for them, and re-layouts  6.65 us
  transfers between devices with their start and end apart: 5, of which 0 were waited for; matrix products, arithmetic and copies ran while one was open for 0% of the time, Pallas kernels for 22%

profile of v5, /device:TPU:0, one launch (start us, length us, event | category | flops | bytes accessed | tf_op | source)
XLA Modules:
  0.0 215.4 jit_solution(7902969151540178271)
XLA Ops:
  0.6 11.0 %project_qkv.1 = (bf16[1024,768]{1,0:T(8,128)(2,1)}, bf16[1024,768]{1,0:T(8,128)(2,1)}, bf16[1024,768]{1,0:T(8,128)(2,1)}, bf16[1024,768]{1,0:T(8,128)(2,1)}, bf...) custom-call(f32[1024,768]{1,0:T(8,128)} %bitcast.25, s32[1,1024]{1,0:T(1,128)} %seg_own.3, ...), custom_call_target="tpu_custom_call" | custom-call | flops 4000000000 | bytes 13000000 | tf_op jit(solution)/shard_map/project_qkv/pallas_call | solution.py:642
  11.6 34.9 %attend_forward.1 = (bf16[1024,768]{1,0:T(8,128)(2,1)}, bf16[12,1024,128]{2,1,0:T(8,128)(2,1)}) custom-call(s32[1]{0:T(128)} %bitcast.band_ref, bf16[1024,768]{1,0:T(8,128)(2,1)} %get-tuple-element.48.q_ref, bf16[1024,768]{1,0:T(8,128)(2,1)} %get-tuple-element.49.k_own, bf16[1024,768]{1,0:T(8,128)(2,1)} %get-tuple-element.50.k_far, ...), custom_call_target="tpu_custom_call" | custom-call | flops 30000001024 | bytes 10000000 | tf_op jit(solution)/shard_map/attend_forward/pallas_call | solution.py:164
  46.5 53.5 %mlp.1 = (f32[1024,768]{1,0:T(8,128)}, f32[1024,768]{1,0:T(8,128)}, bf16[1024,768]{1,0:T(8,128)(2,1)}, f32[8,768]{1,0:T(8,128)}, f32[8,3072]{1,0:T(8,128)}, /*in...) custom-call(f32[1024,768]{1,0:T(8,128)} %bitcast.26, ...), custom_call_target="tpu_custom_call" | custom-call | flops 40000000000 | bytes 40000000 | tf_op jit(solution)/shard_map/mlp/pallas_call | solution.py:548
  100.1 2.5 %collective-permute-start.1 = (bf16[4,2,96,384]{3,2,1,0:T(8,128)(2,1)}, bf16[4,2,96,384]{3,2,1,0:T(8,128)(2,1)S(1)}, u32[]{:S(2)}, u32[]{:S(2)}) collective-permute-start(bf16[4,2,96,384]{3,2,1,0:T(8,128)(2,1)} %get-tuple-element.70), channel_id=1, source_target_pairs={{0,4},{2,6},{4,0},{6,2},{8,12},{10,14},{12,8},{14,10},{16,20},{18,... | collective-permute-start | bytes 1769480 | tf_op jit(solution)/shard_map/ppermute | solution.py:1182
  102.6 2.1 collective-permute-start.2
  104.7 2.6 %collective-permute-start.3 = (bf16[2,2,192,384]{3,2,1,0:T(8,128)(2,1)}, bf16[2,2,192,384]{3,2,1,0:T(8,128)(2,1)S(1)}, u32[]{:S(2)}, u32[]{:S(2)}) collective-permute-start(bf16[2,2,192,384]{3,2,1,0:T(8,128)(2,1)} %get-tuple-element.72), channel_id=1, source_target_pairs={{0,16},{2,18},{4,20},{6,22},{8,24},{10,26},{12,28},{14,30},{16,0},... | collective-permute-start | bytes 1769480 | tf_op jit(solution)/shard_map/ppermute | solution.py:1182
  107.3 1.3 collective-permute-start.4
  108.6 1.5 collective-permute-start
  110.1 0.0 copy-start
  110.1 0.0 copy-start.1
  110.1 0.0 copy-start.2
  110.1 0.0 copy-start.3
  110.1 48.2 %attend_backward.1 = (bf16[1024,768]{1,0:T(8,128)(2,1)}, bf16[768,1024]{1,0:T(8,128)(2,1)}, bf16[768,1024]{1,0:T(8,128)(2,1)}, bf16[768,1024]{1,0:T(8,128)(2,1)}...) custom-call(s32[1]{0:T(128)} %bitcast.band_ref, bf16[12,1024,128]{2,1,0:T(8,128)(2,1)} %get-tuple-element.54.qm, ...), custom_call_target="tpu_custom_call" | custom-call | flops 44999999488 | bytes 20000000 | tf_op jit(solution)/shard_map/attend_backward/pallas_call | solution.py:285
  158.3 0.0 collective-permute-done.1.br_hbm
  158.3 0.0 copy-start.5
  158.3 0.0 collective-permute-done.2.c1_hbm
  158.4 0.0 copy-start.6
  158.4 0.0 collective-permute-done.3.c2_hbm
  158.4 0.0 copy-start.7
  158.4 0.0 collective-permute-done.4.c3_hbm
  158.4 0.0 copy-start.8
  158.4 0.0 collective-permute-done.ar_hbm
  158.4 0.0 copy-start.4
  158.4 0.7 copy-done.5
  159.2 0.2 copy-done.6
  159.4 0.2 copy-done.7
  159.5 0.2 copy-done.8
  159.7 0.3 copy-done.4
  160.0 0.0 copy-done
  160.0 0.0 copy-done.1
  160.0 0.0 copy-done.2
  160.0 0.0 copy-done.3
  160.0 47.7 %finish.1 = (f32[1024,768]{1,0:T(8,128)}, f32[192,384]{1,0:T(8,128)S(1)}, f32[48,3072]{1,0:T(8,128)S(1)}, f32[8,48]{1,0:T(8,128)S(1)}, f32[1,192]{1,0:T(1,128)S(1)}) custom-call(bf16[1024,768]{1,0:T(8,128)(2,1)} %get-tuple-element.59.dq_hbm, bf16[768,1024]{1,0:T(8,128)(2,1)} %get-tuple-element.60.dko_hbm, bf16[768,1024]{1,0:T(8,128)(2,1)} %get-tuple-element.61.dkf_hbm, ...), custom_call_target="tpu_custom_call" | custom-call | flops 20000000000 | bytes 40000000 | tf_op jit(solution)/shard_map/finish/pallas_call | solution.py:1009
  207.7 0.6 slice.38
  208.4 0.7 slice.35
  209.1 0.7 slice.42
  209.8 0.5 slice_bitcast_fusion
  210.3 3.8 %copy.34 = f32[1,1024,768]{2,1,0:T(8,128)} copy(f32[1,1024,768]{2,1,0:T(8,128)} %bitcast.23) | data formatting | bytes 6291456
  214.1 0.6 copy.35
  214.7 0.7 copy.36
Async XLA Ops:
  100.1 58.2 %collective-permute-start.1 = (bf16[4,2,96,384]{3,2,1,0:T(8,128)(2,1)}, bf16[4,2,96,384]{3,2,1,0:T(8,128)(2,1)S(1)}, u32[]{:S(2)}, u32[]{:S(2)}) collective-permute-start(bf16[4,2,96,384]{3,2,1,0:T(8,128)(2,1)} %get-tuple-element.70), channel_id=1, source_target_pairs={{0,4},{2,6},{4,0},{6,2},{8,12},{10,14},{12,8},{14,10},{16,20},{18,... | collective-permute-start | bytes 1769480 | tf_op jit(solution)/shard_map/ppermute | solution.py:1182
  102.6 55.7 %collective-permute-start.2 = (bf16[2,2,192,384]{3,2,1,0:T(8,128)(2,1)}, bf16[2,2,192,384]{3,2,1,0:T(8,128)(2,1)S(1)}, u32[]{:S(2)}, u32[]{:S(2)}) collective-permute-start(bf16[2,2,192,384]{3,2,1,0:T(8,128)(2,1)} %get-tuple-element.71), channel_id=1, source_target_pairs={{0,8},{2,10},{4,12},{6,14},{8,16},{10,18},{12,20},{14,22},{16,24},... | collective-permute-start | bytes 1769480 | tf_op jit(solution)/shard_map/ppermute | solution.py:1182
  104.7 53.7 %collective-permute-start.3 = (bf16[2,2,192,384]{3,2,1,0:T(8,128)(2,1)}, bf16[2,2,192,384]{3,2,1,0:T(8,128)(2,1)S(1)}, u32[]{:S(2)}, u32[]{:S(2)}) collective-permute-start(bf16[2,2,192,384]{3,2,1,0:T(8,128)(2,1)} %get-tuple-element.72), channel_id=1, source_target_pairs={{0,16},{2,18},{4,20},{6,22},{8,24},{10,26},{12,28},{14,30},{16,0},... | collective-permute-start | bytes 1769480 | tf_op jit(solution)/shard_map/ppermute | solution.py:1182
  107.3 51.1 %collective-permute-start.4 = (bf16[2,2,192,384]{3,2,1,0:T(8,128)(2,1)}, bf16[2,2,192,384]{3,2,1,0:T(8,128)(2,1)S(1)}, u32[]{:S(2)}, u32[]{:S(2)}) collective-permute-start(bf16[2,2,192,384]{3,2,1,0:T(8,128)(2,1)} %get-tuple-element.73), channel_id=1, source_target_pairs={{0,24},{2,26},{4,28},{6,30},{8,0},{10,2},{12,4},{14,6},{16,8},{18,... | collective-permute-start | bytes 1769480 | tf_op jit(solution)/shard_map/ppermute | solution.py:1182
  108.6 49.8 %collective-permute-start = (bf16[4,2,144,384]{3,2,1,0:T(8,128)(2,1)}, bf16[4,2,144,384]{3,2,1,0:T(8,128)(2,1)S(1)}, u32[]{:S(2)}, u32[]{:S(2)}) collective-permute-start(bf16[4,2,144,384]{3,2,1,0:T(8,128)(2,1)} %get-tuple-element.69), channel_id=1, source_target_pairs={{0,2},{2,0},{4,6},{6,4},{8,10},{10,8},{12,14},{14,12},{16,18},{18,... | collective-permute-start | bytes 2654216 | tf_op jit(solution)/shard_map/ppermute | solution.py:1182
  110.1 49.9 %copy-start = (f32[768]{0:T(1024)S(1)}, f32[768]{0:T(1024)}, u32[]{:S(2)}) copy-start(f32[768]{0:T(1024)} %gain.5) | copy-start | bytes 9220
  110.1 49.9 %copy-start.1 = (bf16[4,2,96,384]{3,2,1,0:T(8,128)(2,1)S(1)}, bf16[4,2,96,384]{3,2,1,0:T(8,128)(2,1)}, u32[]{:S(2)}) copy-start(bf16[4,2,96,384]{3,2,1,0:T(8,128)(2,1)} %get-tuple-element.67.bk_hbm) | copy-start | bytes 1769476
  110.1 49.9 %copy-start.2 = (f32[8,3072]{1,0:T(8,128)S(1)}, f32[8,3072]{1,0:T(8,128)}, u32[]{:S(2)}) copy-start(f32[8,3072]{1,0:T(8,128)} %get-tuple-element.75.usums) | copy-start | bytes 294916
  110.1 49.9 %copy-start.3 = (f32[8,768]{1,0:T(8,128)S(1)}, f32[8,768]{1,0:T(8,128)}, u32[]{:S(2)}) copy-start(f32[8,768]{1,0:T(8,128)} %get-tuple-element.74.msums) | copy-start | bytes 73732
  158.3 0.8 copy-start.5
  158.4 1.0 copy-start.6
  158.4 1.2 copy-start.7
  158.4 1.4 copy-start.8
  158.4 1.6 copy-start.4

commit v6 on v5

--- a/solution.py
+++ b/solution.py
@@ -425,26 +425,22 @@
     z = me >> 2
     shard = width // 16
 
+    corners = [(y ^ (q >> 1)) * 2 + (x ^ (q & 1)) for q in range(4)]
+
     def down_arrived(j):
         d_copy(j).wait_recv()
         if not sorted_out:
             at = pl.ds(pl.multiple_of(j * SLICE, SLICE), SLICE)
             add_low(outs[0].at[at, :], d_own.at[at, :], d_in.at[at, :])
             return
-        for t in range(2):
-            for out, x_bit, y_bit, first in (
-                (outs[0], 1 - x, t, 0),
-                (outs[1], x, t, 0),
-                (outs[2], t, 1 - y, shard),
-                (outs[3], t, y, shard),
-            ):
-                at = pl.ds(pl.multiple_of(j * SLICE + (y_bit * 2 + x_bit) * 4 * shard + first, shard), shard)
-                add_low(out.at[j, t, 0:shard], d_own.at[at, :], d_in.at[at, :])
+        for q in range(4):
+            at = pl.ds(pl.multiple_of(j * SLICE + corners[q] * 4 * shard, shard), 2 * shard)
+            add_low(outs[q].at[j, 0 : 2 * shard], d_own.at[at, :], d_in.at[at, :])
 
     def down_along_z(d):
         if sorted_out:
             for t in range(4):
-                at = pl.ds(pl.multiple_of(((z + d) & 3) * SLICE + t * 4 * shard + 2 * shard, shard), 2 * shard)
+                at = pl.ds(pl.multiple_of((z ^ d) * SLICE + t * 4 * shard + 2 * shard, shard), 2 * shard)
                 add_low(outs[4 + d].at[t // 2, t % 2, 0 : 2 * shard], d_own.at[at, :], d_in.at[at, :])
 
     def up_arrived(c):
@@ -457,23 +453,21 @@
         def fold(dst, s, part):
             at = pl.ds(pl.multiple_of(s * shard, shard), shard)
             cols = slice(part * half, (part + 1) * half)
-            add_low(dst, own.at[at, cols], u_in.at[c, at, cols])
-
-        def near(s, carry):
-            zz, t = s >> 1, s & 1
-            for sends in range(2):
-                fold(outs[1 - sends].at[zz, t, shard : 2 * shard], zz * 4 + t * 2 + (x ^ sends), 0)
-                fold(outs[3 - sends].at[zz, t, shard : 2 * shard], zz * 4 + (y ^ sends) * 2 + t, 1)
+            add_low(dst.at[(2 + part) * shard : (3 + part) * shard], own.at[at, cols], u_in.at[c, at, cols])
+
+        def near(zz, carry):
+            for q in range(4):
+                for part in range(2):
+                    fold(outs[q].at[zz], zz * 4 + corners[q], part)
             return carry
 
         def along(s, carry):
             for d in range(4):
                 for part in range(2):
-                    to = slice((2 + part) * shard, (3 + part) * shard)
-                    fold(outs[4 + d].at[s >> 1, s & 1, to], ((z + d) & 3) * 4 + s, part)
+                    fold(outs[4 + d].at[s >> 1, s & 1], (z ^ d) * 4 + s, part)
             return carry
 
-        lax.fori_loop(0, 8 if c == 0 else 4, near if c == 0 else along, 0, unroll=2)
+        lax.fori_loop(0, 4, near if c == 0 else along, 0, unroll=2)
 
     def proj_arrived():
         p_copy().wait_recv()
@@ -481,14 +475,13 @@
             add_low(outs[2], p_own, p_in)
             return
 
-        def one(s, carry):
-            zz, t = s >> 1, s & 1
-            for sends in range(2):
-                at = pl.ds(pl.multiple_of((zz * 4 + t * 2 + (x ^ sends)) * shard, shard), shard)
-                add_low(outs[1 - sends].at[zz, t, 2 * shard : 3 * shard], p_own.at[at, :], p_in.at[at, :])
+        def one(zz, carry):
+            for q in range(4):
+                at = pl.ds(pl.multiple_of((zz * 4 + corners[q]) * shard, shard), shard)
+                add_low(outs[q].at[zz, 4 * shard : 5 * shard], p_own.at[at, :], p_in.at[at, :])
             return carry
 
-        lax.fori_loop(0, 8, one, 0, unroll=4)
+        lax.fori_loop(0, 4, one, 0, unroll=2)
 
     middle = blocks + slices
     for c in range(per_half):
@@ -538,7 +531,7 @@
     shape = jax.ShapeDtypeStruct
     if sorted_out:
         sixteenth = width // 16
-        pieces = [shape((4, 2, n * sixteenth, half), bf16) for n in (3, 3, 2, 2)]
+        pieces = [shape((4, 5 * sixteenth, half), bf16)] * 4
         pieces += [shape((2, 2, 4 * sixteenth, half), bf16)] * 4
     else:
         pieces = [shape((ff, half), bf16), shape((width, ff // 2), bf16), shape((width, half), bf16)]
@@ -760,11 +753,11 @@
 
 
 def finish_kernel(
-    dq_hbm, dko_hbm, dkf_hbm, dvo_hbm, dvf_hbm, n_hbm, tok_hbm, rgrad_hbm, w_hbm, ak_hbm, bk_hbm, ck_hbm, ar_hbm, br_hbm, c1_hbm, c2_hbm, c3_hbm, gain, msums, usums,
-    out, down_out, wide_out, vec_out, usum_out,
-    packed, dko, dko_in, dvo, dvo_in, n1, tok, wq, ak, bk, ck, cols, far_in, tail,
-    a_one, b_one, c_one, a_two, b_two, c_two, a_thr, b_thr, c_thr, ta_one, tb_one, ta_two, tb_two, ta_thr, tb_thr, vec, vec_band, vec_x, vec_y, vec_z,
-    load_sem, swap_send, swap_recv, send, recv, vsend, vrecv,
+    dq_hbm, dko_hbm, dkf_hbm, dvo_hbm, dvf_hbm, n_hbm, tok_hbm, rgrad_hbm, w_hbm, pk_hbm, ck_hbm, c1_hbm, px_hbm, py_hbm, pd_hbm, c2_hbm, c3_hbm, gain, msums, usums,
+    out_hbm, down_out, wide_out, vec_out, usum_out,
+    packed, dko, dko_in, dvo, dvo_in, n1, tok, out, wq, pk, p_one, ck, cols, far_in, tail,
+    c_one, c_two, p_thr, c_thr, ta_one, tb_one, ta_two, tb_two, ta_thr, tb_thr, vec, vec_band, vec_x, vec_y, vec_z,
+    load_sem, store_sem, swap_send, swap_recv, send, recv, vsend, vrecv,
 ):
     me = lax.axis_index("dp")
     band = lax.axis_index("band")
@@ -777,23 +770,26 @@
     peers_z = [(((z + d) & 3) * 4 + (me & 3), band) for d in (1, 2, 3)]
 
     def load(t, src, dst):
-        copy = pltpu.make_async_copy(src, dst, load_sem.at[t])
-        copy.start()
-        return copy
+        return pltpu.make_async_copy(src, dst, load_sem.at[t])
 
     loads = {
-        "early": (load(0, ak_hbm, ak), load(1, ar_hbm, a_one), load(2, bk_hbm, bk), load(3, br_hbm, b_one)),
-        "along": (load(8, ck_hbm, ck), load(13, c1_hbm, c_one.at[0]), load(14, c2_hbm, c_one.at[1]), load(15, c3_hbm, c_one.at[2])),
-        "queries": (load(6, dq_hbm, packed.at[:, 0:width]),),
-        "normed": (load(7, n_hbm, n1),),
+        "queries": (load(6, dq_hbm, packed.at[:, 0:width]), load(7, n_hbm, n1)),
         "keys": (load(4, dko_hbm, dko), load(5, dvo_hbm, dvo)),
-        "weight": (load(10, w_hbm, wq),),
-        "rows": (load(11, tok_hbm, tok), load(12, rgrad_hbm, out)),
+        "early": (load(0, pk_hbm, pk), load(1, px_hbm, p_one.at[0]), load(2, py_hbm, p_one.at[1]), load(3, pd_hbm, p_one.at[2])),
+        "along": (load(8, ck_hbm, ck), load(13, c2_hbm, c_one.at[1]), load(14, c3_hbm, c_one.at[2])),
+        "rows": (load(10, w_hbm, wq), load(11, tok_hbm, tok), load(12, rgrad_hbm, out)),
     }
+
+    def fetch(name):
+        for copy in loads[name]:
+            copy.start()
 
     def ready(name):
         for copy in loads[name]:
             copy.wait()
+
+    for name in ("queries", "keys", "early"):
+        fetch(name)
 
     barrier = pltpu.get_barrier_semaphore()
     for peer in (peer_band, peer_x, peer_y, *peers_z):
@@ -810,6 +806,7 @@
 
     swap_k = push(dkf_hbm, dko_in, peer_band, swap_send.at[0], swap_recv.at[0])
     swap_v = push(dvf_hbm, dvo_in, peer_band, swap_send.at[1], swap_recv.at[1])
+    c_near = push(c1_hbm, c_one.at[0], (me ^ 4, band), send.at[2, 2], recv.at[2, 2])
 
     def put(dst, src):
         dst[...] = src[...]
@@ -846,22 +843,6 @@
         for d in range(3):
             total = total + three[d].astype(f32)
         return total
-
-    ready("early")
-    a_copy = second_stage(0, lambda i, j: ak.at[i, j], a_one, a_two, y, peer_y)
-    b_copy = second_stage(1, lambda i, j: bk.at[i, j], b_one, b_two, x, peer_x)
-    ready("along")
-
-    def along(s, c):
-        i, j = s >> 1, s & 1
-        total = ck[i, j].astype(f32)
-        for d in range(3):
-            total = total + c_one[d, i, j].astype(f32)
-        ck[i, j] = total.astype(bf16)
-        return c
-
-    lax.fori_loop(0, 4, along, 0, unroll=True)
-    c_copy = push(ck.at[:, 1 - x], c_two, peer_x, send.at[2, 0], recv.at[2, 0])
 
     def columns(t):
         cols[:, :, :, :, t * width : (t + 1) * width] = (
@@ -877,7 +858,7 @@
                 packed[here, t * width + p * 128 : t * width + (p + 1) * 128] = turned
             return c
 
-        lax.fori_loop(0, rows // 256, step, 0)
+        lax.fori_loop(0, rows // 256, step, 0, unroll=2)
 
     def swap(t, start, size, to):
         return pltpu.make_async_remote_copy(
@@ -893,13 +874,25 @@
     swap_near = swap(2, (3 - band) * third, third, band * width)
     swap_wide = swap(3, (1 - band) * 2 * width, width, (1 - band) * third)
     ready("queries")
-    ready("normed")
     columns(0)
+    fetch("along")
+    fetch("rows")
 
     @pl.when(band == 1)
     def _():
         swap_wide.start()
 
+    ready("early")
+
+    def plane(zz, c):
+        total = pk[zz].astype(f32)
+        for t in range(3):
+            total = total + p_one[t, zz].astype(f32)
+        pk[zz] = total.astype(bf16)
+        return c
+
+    lax.fori_loop(0, 4, plane, 0)
+    p_copies = [push(pk.at[(z + d) & 3], p_thr.at[d - 1], peers_z[d - 1], send.at[0, d], recv.at[0, d]) for d in (1, 2, 3)]
     ready("keys")
     swap_k.wait_recv()
     turn(1, dko, dko_in)
@@ -913,8 +906,6 @@
     def _():
         swap_wide.start()
 
-    a_copies = third_stage(0, a_one, a_two, a_thr, y, a_copy)
-    b_copies = third_stage(1, b_one, b_two, b_thr, x, b_copy)
     swap_near.wait()
     swap_wide.wait()
     mine = pl.ds(pl.multiple_of(band * half, 128), half)
@@ -922,12 +913,7 @@
     cut = ta_one.shape[-1]
     ta_first = push(tail.at[:, :, 1 - x, :, 0:cut], ta_one, peer_x, send.at[3, 4], recv.at[3, 4])
     tb_first = push(tail.at[:, 1 - y, :, :, cut:half], tb_one, peer_y, send.at[4, 4], recv.at[4, 4])
-    c_copy.wait_recv()
-    add_low(c_two.at[0], c_two.at[0], ck.at[0, x])
-    add_low(c_two.at[1], c_two.at[1], ck.at[1, x])
-    c_last = push(c_two.at[1 - y], c_thr, peer_y, send.at[2, 1], recv.at[2, 1])
-
-    ready("weight")
+
     ready("rows")
     vec[...] = jnp.zeros(vec.shape, f32)
 
@@ -945,28 +931,48 @@
         return c
 
     lax.fori_loop(0, rows // 256, rows_back, 0)
+    store = pltpu.make_async_copy(out, out_hbm, store_sem)
+    store.start()
     vec[4:8, :] = msums[0:4, :]
     for t in range(usums.shape[1] // width):
         vec[8 + t : 9 + t, :] = usums[0:1, t * width : (t + 1) * width]
     v_band = push(vec, vec_band, peer_band, vsend.at[0], vrecv.at[0])
+    v_band.wait()
+    vec_band[...] = vec[...] + vec_band[...]
+    v_z = [push(vec_band, vec_z.at[d], peers_z[d], vsend.at[3 + d], vrecv.at[3 + d]) for d in range(3)]
     ta_first.wait_recv()
     ta_copy = second_stage(3, lambda i, j: tail.at[i, j, x, :, 0:cut], ta_one, ta_two, y, peer_y)
     tb_first.wait_recv()
     tb_copy = second_stage(4, lambda i, j: tail.at[i, y, j, :, cut:half], tb_one, tb_two, x, peer_x)
-    v_band.wait()
-    vec_band[...] = vec[...] + vec_band[...]
-    v_x = push(vec_band, vec_x, peer_x, vsend.at[1], vrecv.at[1])
+    for copy in v_z:
+        copy.wait()
+    vec_z[0] = vec_band[...] + vec_z[0] + vec_z[1] + vec_z[2]
+    v_x = push(vec_z.at[0], vec_x, peer_x, vsend.at[1], vrecv.at[1])
+    c_near.wait_recv()
+    ready("along")
+
+    def along(s, c):
+        i, j = s >> 1, s & 1
+        total = ck[i, j].astype(f32)
+        for d in range(3):
+            total = total + c_one[d, i, j].astype(f32)
+        ck[i, j] = total.astype(bf16)
+        return c
+
+    lax.fori_loop(0, 4, along, 0, unroll=True)
+    c_copy = push(ck.at[:, 1 - x], c_two, peer_x, send.at[2, 0], recv.at[2, 0])
+
     ta_copies = third_stage(3, ta_one, ta_two, ta_thr, y, ta_copy)
     tb_copies = third_stage(4, tb_one, tb_two, tb_thr, x, tb_copy)
     v_x.wait()
-    vec_x[...] = vec_band[...] + vec_x[...]
+    vec_x[...] = vec_z[0] + vec_x[...]
     v_y = push(vec_x, vec_y, peer_y, vsend.at[2], vrecv.at[2])
+    c_copy.wait_recv()
+    add_low(c_two.at[0], c_two.at[0], ck.at[0, x])
+    add_low(c_two.at[1], c_two.at[1], ck.at[1, x])
+    c_last = push(c_two.at[1 - y], c_thr, peer_y, send.at[2, 1], recv.at[2, 1])
     v_y.wait()
-    vec_y[...] = vec_x[...] + vec_y[...]
-    v_z = [push(vec_y, vec_z.at[d], peers_z[d], vsend.at[3 + d], vrecv.at[3 + d]) for d in range(3)]
-    for copy in v_z:
-        copy.wait_recv()
-    vec[...] = vec_y[...] + vec_z[0] + vec_z[1] + vec_z[2]
+    vec[...] = vec_x[...] + vec_y[...]
     shard = vec_out.shape[1]
     vec_out[...] = pltpu.roll(vec[0:8, :], width - me * shard, 1)[:, 0:shard]
     wide = usum_out.shape[1]
@@ -974,22 +980,22 @@
     row = vec[pl.ds(8 + me // per_row, 1), :]
     usum_out[...] = pltpu.roll(jnp.broadcast_to(row, (8, width)), width - (me % per_row) * wide, 1)[0:1, 0:wide]
     shard = width // 16
-    a_sum, b_sum = last(a_two, a_thr, a_copies), last(b_two, b_thr, b_copies)
+    p_sum = last(pk, p_thr, p_copies)
     c_last.wait_recv()
     c_sum = c_two[y].astype(f32) + c_thr[...].astype(f32)
-    down_out[0:shard, :] = a_sum[0:shard]
-    down_out[shard : 2 * shard, :] = b_sum[0:shard]
+    down_out[0 : 2 * shard, :] = p_sum[0 : 2 * shard]
     down_out[2 * shard : 4 * shard, :] = c_sum[0 : 2 * shard]
-    ups = (a_sum[shard : 2 * shard], b_sum[shard : 2 * shard], c_sum[2 * shard : 3 * shard], c_sum[3 * shard : 4 * shard])
+    ups = [part[t * shard : (t + 1) * shard] for part in (p_sum, c_sum) for t in (2, 3)]
     for t, part in enumerate(ups):
         wide_out[:, half + t * third : half + (t + 1) * third] = part
-    wide_out[:, half + 4 * third :] = a_sum[2 * shard : 3 * shard]
+    wide_out[:, half + 4 * third :] = p_sum[4 * shard : 5 * shard]
     wide_out[:, 0:cut] = last(ta_two, ta_thr, ta_copies)
     wide_out[:, cut:half] = last(tb_two, tb_thr, tb_copies)
-    done = {id(c) for c in (v_band, v_x, v_y)}
+    done = {id(c) for c in (v_band, v_x, v_y, *v_z)}
     for copy in pending:
         if id(copy) not in done:
             copy.wait_send()
+    store.wait()
 
 
 def finish(dq, dk_own, dk_far, dv_own, dv_far, normed, tokens, rgrad, w_qkv, pieces, gain, msums, usums):
@@ -999,7 +1005,7 @@
     shards = (4, 2, 2)
     third, shard = width // 2, width // 16
     q_shape = shards + (shard, half)
-    a_piece, b_piece, c_piece = (3 * shard, third), (2 * shard, third), (4 * shard, third)
+    p_piece, c_piece = (5 * shard, third), (4 * shard, third)
     cut = half // 256 * 128 + 128
     ta_piece, tb_piece = (shard, cut), (shard, half - cut)
     hbm, vmem = pl.BlockSpec(memory_space=pl.ANY), pl.BlockSpec(memory_space=pltpu.VMEM)
@@ -1016,27 +1022,23 @@
             shape((1, ff // 16), f32),
         ),
         in_specs=[hbm] * 17 + [vmem] * 3,
-        out_specs=[vmem] * 5,
+        out_specs=[hbm] + [vmem] * 4,
         scratch_shapes=[
             low(rows, 3 * width),
             *([low(width, rows)] * 4),
             low(rows, width),
             pltpu.VMEM((rows, width), f32),
+            pltpu.VMEM((rows, width), f32),
             low(width, 3 * width),
-            low(4, 2, *a_piece),
-            low(4, 2, *b_piece),
+            low(4, *p_piece),
+            low(3, 4, *p_piece),
             low(2, 2, *c_piece),
             low(*shards, shard, 3 * width),
             low(*q_shape),
             low(*q_shape),
-            low(4, 2, *a_piece),
-            low(4, 2, *b_piece),
             low(3, 2, 2, *c_piece),
-            low(4, *a_piece),
-            low(4, *b_piece),
             low(2, *c_piece),
-            low(3, *a_piece),
-            low(3, *b_piece),
+            low(3, *p_piece),
             low(*c_piece),
             low(4, 2, *ta_piece),
             low(4, 2, *tb_piece),
@@ -1050,6 +1052,7 @@
             pltpu.VMEM((16, width), f32),
             pltpu.VMEM((3, 16, width), f32),
             dma((16,)),
+            dma,
             dma((4,)),
             dma((4,)),
             dma((5, 5)),
@@ -1176,10 +1179,9 @@
         down_bias,
     )
     if size == 16:
-        turns = [[(i, i ^ bit) for i in range(size)] for bit in (1, 2)]
-        turns += [[(i, (i + 4 * d) % size) for i in range(size)] for d in (1, 2, 3)]
-        sent = (pieces[0], pieces[2], *pieces[5:8])
-        pieces = [pieces[1], pieces[3], pieces[4]] + [lax.ppermute(a, "dp", turn) for a, turn in zip(sent, turns)]
+        turns = [[(i, i ^ bits) for i in range(size)] for bits in (1, 2, 3, 8, 12)]
+        sent = (*pieces[1:4], *pieces[6:8])
+        pieces = [pieces[0], *pieces[4:6]] + [lax.ppermute(a, "dp", turn) for a, turn in zip(sent, turns)]
     query_grad, dk_own, dk_far, dv_own, dv_far, output = attend_backward(
         band_at, output, query_lanes, attended_grad, attended, *keys
     )

time: 216 us -> 212 us (0.981)
  Pallas kernels: 195 us -> 192 us
    pallas_call x1, Pallas kernels: 47.7 us -> 44.5 us  [finish(): pl.pallas_call(finish_kernel, out_shape=(shape((rows, width), f32), shape...]
  transfers between devices with their start and end apart: 5 -> 5, of which waited for: 0 -> 0; matrix products, arithmetic and copies ran while one was open for 0% -> 0% of each run, Pallas kernels for 22% -> 23%
where the time goes in v6:
time: 212 us; the launch traced here: 211 us
  Pallas kernels  192 us (91%)
  local copies, waits for them, and re-layouts  9.33 us (4%)
  starting transfers between devices  8.94 us (4%)
    pallas_call x1, Pallas kernels, mlp(): pl.pallas_call(functools.partial(mlp_kernel, sorted_out, blocks, rows, sl...  53.4 us
    pallas_call x1, Pallas kernels, attend_backward(): pl.pallas_call(functools.partial(attend_bwd_kernel, fills, steps, BQ, BK)...  48.2 us
    pallas_call x1, Pallas kernels, finish(): pl.pallas_call(finish_kernel, out_shape=(shape((rows, width), f32), shape...  44.5 us
    pallas_call x1, Pallas kernels, attend_forward(): pl.pallas_call(functools.partial(attend_fwd_kernel, fills, BQ, BK), out_s...  34.9 us
    pallas_call x1, Pallas kernels, project_qkv(): pl.pallas_call(functools.partial(qkv_kernel, steps), out_shape=(low,) * 6...  11 us
    ppermute x5, starting transfers between devices, local(): lax.ppermute(a, 'dp', turn)  8.94 us
    unnamed x21, local copies, waits for them, and re-layouts  6.71 us
  transfers between devices with their start and end apart: 5, of which 0 were waited for; matrix products, arithmetic and copies ran while one was open for 0% of the time, Pallas kernels for 23%

profile of v6, /device:TPU:0, one launch (start us, length us, event | category | flops | bytes accessed | tf_op | source)
XLA Modules:
  0.0 211.1 jit_solution(5599758468786309391)
XLA Ops:
  0.6 11.0 %project_qkv.1 = (bf16[1024,768]{1,0:T(8,128)(2,1)}, bf16[1024,768]{1,0:T(8,128)(2,1)}, bf16[1024,768]{1,0:T(8,128)(2,1)}, bf16[1024,768]{1,0:T(8,128)(2,1)}, bf...) custom-call(f32[1024,768]{1,0:T(8,128)} %bitcast.25, s32[1,1024]{1,0:T(1,128)} %seg_own.3, ...), custom_call_target="tpu_custom_call" | custom-call | flops 4000000000 | bytes 13000000 | tf_op jit(solution)/shard_map/project_qkv/pallas_call | solution.py:635
  11.6 34.9 %attend_forward.1 = (bf16[1024,768]{1,0:T(8,128)(2,1)}, bf16[12,1024,128]{2,1,0:T(8,128)(2,1)}) custom-call(s32[1]{0:T(128)} %bitcast.band_ref, bf16[1024,768]{1,0:T(8,128)(2,1)} %get-tuple-element.48.q_ref, bf16[1024,768]{1,0:T(8,128)(2,1)} %get-tuple-element.49.k_own, bf16[1024,768]{1,0:T(8,128)(2,1)} %get-tuple-element.50.k_far, ...), custom_call_target="tpu_custom_call" | custom-call | flops 30000001024 | bytes 10000000 | tf_op jit(solution)/shard_map/attend_forward/pallas_call | solution.py:164
  46.5 53.4 %mlp.1 = (f32[1024,768]{1,0:T(8,128)}, f32[1024,768]{1,0:T(8,128)}, bf16[1024,768]{1,0:T(8,128)(2,1)}, f32[8,768]{1,0:T(8,128)}, f32[8,3072]{1,0:T(8,128)}, /*in...) custom-call(f32[1024,768]{1,0:T(8,128)} %bitcast.26, ...), custom_call_target="tpu_custom_call" | custom-call | flops 40000000000 | bytes 40000000 | tf_op jit(solution)/shard_map/mlp/pallas_call | solution.py:541
  100.0 3.6 %collective-permute-start.3 = (bf16[2,2,192,384]{3,2,1,0:T(8,128)(2,1)}, bf16[2,2,192,384]{3,2,1,0:T(8,128)(2,1)S(1)}, u32[]{:S(2)}, u32[]{:S(2)}) collective-permute-start(bf16[2,2,192,384]{3,2,1,0:T(8,128)(2,1)} %get-tuple-element.72), channel_id=1, source_target_pairs={{0,16},{2,18},{4,20},{6,22},{8,24},{10,26},{12,28},{14,30},{16,0},... | collective-permute-start | bytes 1769480 | tf_op jit(solution)/shard_map/ppermute | solution.py:1184
  103.5 1.9 collective-permute-start.4
  105.4 1.5 collective-permute-start
  106.9 1.5 collective-permute-start.1
  108.4 0.5 collective-permute-start.2
  108.9 0.0 copy-start
  108.9 0.0 copy-start.1
  108.9 0.0 copy-start.2
  108.9 0.0 copy-start.3
  108.9 48.2 %attend_backward.1 = (bf16[1024,768]{1,0:T(8,128)(2,1)}, bf16[768,1024]{1,0:T(8,128)(2,1)}, bf16[768,1024]{1,0:T(8,128)(2,1)}, bf16[768,1024]{1,0:T(8,128)(2,1)}...) custom-call(s32[1]{0:T(128)} %bitcast.band_ref, bf16[12,1024,128]{2,1,0:T(8,128)(2,1)} %get-tuple-element.54.qm, ...), custom_call_target="tpu_custom_call" | custom-call | flops 44999999488 | bytes 20000000 | tf_op jit(solution)/shard_map/attend_backward/pallas_call | solution.py:285
  157.1 0.0 collective-permute-done.3.c2_hbm
  157.1 0.0 copy-start.7
  157.1 0.0 collective-permute-done.4.c3_hbm
  157.2 0.0 copy-start.8
  157.2 0.0 collective-permute-done.px_hbm
  157.2 0.0 copy-start.4
  157.2 0.0 collective-permute-done.1.py_hbm
  157.2 0.0 copy-start.5
  157.2 0.0 collective-permute-done.2.pd_hbm
  157.2 0.0 copy-start.6
  157.2 0.7 copy-done.7
  158.0 0.2 copy-done.8
  158.2 0.2 copy-done.4
  158.4 0.3 copy-done.5
  158.7 0.2 copy-done.6
  158.9 0.0 copy-done
  158.9 0.0 copy-done.1
  158.9 0.0 copy-done.2
  158.9 0.0 copy-done.3
  158.9 44.5 %finish.1 = (f32[1024,768]{1,0:T(8,128)}, f32[192,384]{1,0:T(8,128)S(1)}, f32[48,3072]{1,0:T(8,128)S(1)}, f32[8,48]{1,0:T(8,128)S(1)}, f32[1,192]{1,0:T(1,128)S(1)}) custom-call(bf16[1024,768]{1,0:T(8,128)(2,1)} %get-tuple-element.59.dq_hbm, bf16[768,1024]{1,0:T(8,128)(2,1)} %get-tuple-element.60.dko_hbm, bf16[768,1024]{1,0:T(8,128)(2,1)} %get-tuple-element.61.dkf_hbm, ...), custom_call_target="tpu_custom_call" | custom-call | flops 20000000000 | bytes 40000000 | tf_op jit(solution)/shard_map/finish/pallas_call | solution.py:1015
  203.4 0.6 slice.38
  204.0 0.7 slice.35
  204.7 0.7 slice.42
  205.5 0.5 slice_bitcast_fusion
  206.0 3.8 %copy.34 = f32[1,1024,768]{2,1,0:T(8,128)} copy(f32[1,1024,768]{2,1,0:T(8,128)} %bitcast.23) | data formatting | bytes 6291456
  209.8 0.6 copy.35
  210.3 0.7 copy.36
Async XLA Ops:
  100.0 57.2 %collective-permute-start.3 = (bf16[2,2,192,384]{3,2,1,0:T(8,128)(2,1)}, bf16[2,2,192,384]{3,2,1,0:T(8,128)(2,1)S(1)}, u32[]{:S(2)}, u32[]{:S(2)}) collective-permute-start(bf16[2,2,192,384]{3,2,1,0:T(8,128)(2,1)} %get-tuple-element.72), channel_id=1, source_target_pairs={{0,16},{2,18},{4,20},{6,22},{8,24},{10,26},{12,28},{14,30},{16,0},... | collective-permute-start | bytes 1769480 | tf_op jit(solution)/shard_map/ppermute | solution.py:1184
  103.5 53.6 %collective-permute-start.4 = (bf16[2,2,192,384]{3,2,1,0:T(8,128)(2,1)}, bf16[2,2,192,384]{3,2,1,0:T(8,128)(2,1)S(1)}, u32[]{:S(2)}, u32[]{:S(2)}) collective-permute-start(bf16[2,2,192,384]{3,2,1,0:T(8,128)(2,1)} %get-tuple-element.73), channel_id=1, source_target_pairs={{0,24},{2,26},{4,28},{6,30},{8,16},{10,18},{12,20},{14,22},{16,8},... | collective-permute-start | bytes 1769480 | tf_op jit(solution)/shard_map/ppermute | solution.py:1184
  105.4 51.7 %collective-permute-start = (bf16[4,240,384]{2,1,0:T(8,128)(2,1)}, bf16[4,240,384]{2,1,0:T(8,128)(2,1)S(1)}, u32[]{:S(2)}, u32[]{:S(2)}) collective-permute-start(bf16[4,240,384]{2,1,0:T(8,128)(2,1)} %get-tuple-element.69), channel_id=1, source_target_pairs={{0,2},{2,0},{4,6},{6,4},{8,10},{10,8},{12,14},{14,12},{16,18},{18,... | collective-permute-start | bytes 2211848 | tf_op jit(solution)/shard_map/ppermute | solution.py:1184
  106.9 50.3 %collective-permute-start.1 = (bf16[4,240,384]{2,1,0:T(8,128)(2,1)}, bf16[4,240,384]{2,1,0:T(8,128)(2,1)S(1)}, u32[]{:S(2)}, u32[]{:S(2)}) collective-permute-start(bf16[4,240,384]{2,1,0:T(8,128)(2,1)} %get-tuple-element.70), channel_id=1, source_target_pairs={{0,4},{2,6},{4,0},{6,2},{8,12},{10,14},{12,8},{14,10},{16,20},{18,... | collective-permute-start | bytes 2211848 | tf_op jit(solution)/shard_map/ppermute | solution.py:1184
  108.4 48.8 %collective-permute-start.2 = (bf16[4,240,384]{2,1,0:T(8,128)(2,1)}, bf16[4,240,384]{2,1,0:T(8,128)(2,1)S(1)}, u32[]{:S(2)}, u32[]{:S(2)}) collective-permute-start(bf16[4,240,384]{2,1,0:T(8,128)(2,1)} %get-tuple-element.71), channel_id=1, source_target_pairs={{0,6},{2,4},{4,2},{6,0},{8,14},{10,12},{12,10},{14,8},{16,22},{18,... | collective-permute-start | bytes 2211848 | tf_op jit(solution)/shard_map/ppermute | solution.py:1184
  108.9 50.0 %copy-start = (f32[768]{0:T(1024)S(1)}, f32[768]{0:T(1024)}, u32[]{:S(2)}) copy-start(f32[768]{0:T(1024)} %gain.5) | copy-start | bytes 9220
  108.9 50.0 %copy-start.1 = (bf16[2,2,192,384]{3,2,1,0:T(8,128)(2,1)S(1)}, bf16[2,2,192,384]{3,2,1,0:T(8,128)(2,1)}, u32[]{:S(2)}) copy-start(bf16[2,2,192,384]{3,2,1,0:T(8,128)(2,1)} %get-tuple-element.67.ck_hbm) | copy-start | bytes 1769476
  108.9 50.0 %copy-start.2 = (f32[8,3072]{1,0:T(8,128)S(1)}, f32[8,3072]{1,0:T(8,128)}, u32[]{:S(2)}) copy-start(f32[8,3072]{1,0:T(8,128)} %get-tuple-element.75.usums) | copy-start | bytes 294916
  108.9 50.0 %copy-start.3 = (f32[8,768]{1,0:T(8,128)S(1)}, f32[8,768]{1,0:T(8,128)}, u32[]{:S(2)}) copy-start(f32[8,768]{1,0:T(8,128)} %get-tuple-element.74.msums) | copy-start | bytes 73732
  157.1 0.8 copy-start.7
  157.2 1.0 copy-start.8
  157.2 1.2 copy-start.4
  157.2 1.4 copy-start.5
  157.2 1.7 copy-start.6

commit v7 on v6

--- a/solution.py
+++ b/solution.py
@@ -66,7 +66,7 @@
     return start, blocks, early, late
 
 
-def over_blocks(count, early, late, rows, body):
+def over_blocks(count, early, late, rows, body, paired=False):
     for first, end, part in (
         (0, early, slice(0, EDGE)),
         (early, count - late, slice(0, rows)),
@@ -77,6 +77,16 @@
             body(j, part)
             return c
 
+        if paired and part == slice(0, rows):
+
+            def two(j, c, first=first, part=part):
+                body(first + 2 * j, part)
+                body(first + 2 * j + 1, part)
+                return c
+
+            pairs = (end - first) // 2
+            lax.fori_loop(0, pairs, two, 0)
+            first = first + 2 * pairs
         lax.fori_loop(first, end, step, 0)
 
 
@@ -131,7 +141,7 @@
                     m = jnp.maximum(m, s[:, t * 128 : (t + 1) * 128])
                 mx[h, part, :] = m
 
-        over_blocks(count, early, late, BQ, first)
+        over_blocks(count, early, late, BQ, first, True)
         for h in range(HEADS):
             mx[h] = jnp.broadcast_to(jnp.max(mx[h], axis=1, keepdims=True), (BQ, 128))
 
@@ -484,29 +494,34 @@
         lax.fori_loop(0, 4, one, 0, unroll=2)
 
     middle = blocks + slices
+    @pl.when(i == middle)
+    def _():
+        columns(mm(ats[...], ags[...], TN), p_own, p_far, slice(None))
+        p_copy().start()
+
     for c in range(per_half):
         at = slice(c * SLICE, (c + 1) * SLICE)
 
-        @pl.when(i == middle + c)
+        @pl.when(i == middle + 1 + c)
         def _(c=c, at=at):
             hid[0:width, at] = up_slice((1 - band) * per_half + c)
             u_copy(c).start()
             for j in range(2 * c, 2 * c + 2):
                 down_arrived(j)
 
-        @pl.when(i == middle + per_half + c)
+        @pl.when(i == middle + 1 + per_half + c)
         def _(c=c):
             hid[0:width, (per_half + c) * SLICE : (per_half + c + 1) * SLICE] = up_slice(band * per_half + c)
             for d in range(2 * c, 2 * c + 2):
                 down_along_z(d)
+            if c == 0:
+                proj_arrived()
+            else:
+                up_arrived(c - 1)
 
     @pl.when(i == middle + slices)
     def _():
-        columns(mm(ats[...], ags[...], TN), p_own, p_far, slice(None))
-        p_copy().start()
-        for c in range(per_half):
-            up_arrived(c)
-        proj_arrived()
+        up_arrived(per_half - 1)
         for j in range(slices):
             d_copy(j).wait_send()
         for c in range(per_half):
@@ -891,7 +906,7 @@
         pk[zz] = total.astype(bf16)
         return c
 
-    lax.fori_loop(0, 4, plane, 0)
+    lax.fori_loop(0, 4, plane, 0, unroll=True)
     p_copies = [push(pk.at[(z + d) & 3], p_thr.at[d - 1], peers_z[d - 1], send.at[0, d], recv.at[0, d]) for d in (1, 2, 3)]
     ready("keys")
     swap_k.wait_recv()

time: 212 us -> 210 us (level)
  no operation moved by 1% of the time
where the time goes in v7:
time: 210 us; the launch traced here: 209 us
  Pallas kernels  191 us (91%)
  local copies, waits for them, and re-layouts  9.33 us (4%)
  starting transfers between devices  8.44 us (4%)
    pallas_call x1, Pallas kernels, mlp(): pl.pallas_call(functools.partial(mlp_kernel, sorted_out, blocks, rows, sl...  52.6 us
    pallas_call x1, Pallas kernels, attend_backward(): pl.pallas_call(functools.partial(attend_bwd_kernel, fills, steps, BQ, BK)...  48.2 us
    pallas_call x1, Pallas kernels, finish(): pl.pallas_call(finish_kernel, out_shape=(shape((rows, width), f32), shape...  45.1 us
    pallas_call x1, Pallas kernels, attend_forward(): pl.pallas_call(functools.partial(attend_fwd_kernel, fills, BQ, BK), out_s...  34.1 us
    pallas_call x1, Pallas kernels, project_qkv(): pl.pallas_call(functools.partial(qkv_kernel, steps), out_shape=(low,) * 6...  11 us
    ppermute x5, starting transfers between devices, local(): lax.ppermute(a, 'dp', turn)  8.44 us
    unnamed x21, local copies, waits for them, and re-layouts  6.71 us
  transfers between devices with their start and end apart: 5, of which 0 were waited for; matrix products, arithmetic and copies ran while one was open for 0% of the time, Pallas kernels for 23%

profile of v7, /device:TPU:0, one launch (start us, length us, event | category | flops | bytes accessed | tf_op | source)
XLA Modules:
  0.0 209.5 jit_solution(13768427502173132730)
XLA Ops:
  0.6 11.0 %project_qkv.1 = (bf16[1024,768]{1,0:T(8,128)(2,1)}, bf16[1024,768]{1,0:T(8,128)(2,1)}, bf16[1024,768]{1,0:T(8,128)(2,1)}, bf16[1024,768]{1,0:T(8,128)(2,1)}, bf...) custom-call(f32[1024,768]{1,0:T(8,128)} %bitcast.25, s32[1,1024]{1,0:T(1,128)} %seg_own.3, ...), custom_call_target="tpu_custom_call" | custom-call | flops 4000000000 | bytes 13000000 | tf_op jit(solution)/shard_map/project_qkv/pallas_call | solution.py:650
  11.6 34.1 %attend_forward.1 = (bf16[1024,768]{1,0:T(8,128)(2,1)}, bf16[12,1024,128]{2,1,0:T(8,128)(2,1)}) custom-call(s32[1]{0:T(128)} %bitcast.band_ref, bf16[1024,768]{1,0:T(8,128)(2,1)} %get-tuple-element.48.q_ref, bf16[1024,768]{1,0:T(8,128)(2,1)} %get-tuple-element.49.k_own, bf16[1024,768]{1,0:T(8,128)(2,1)} %get-tuple-element.50.k_far, ...), custom_call_target="tpu_custom_call" | custom-call | flops 30000001024 | bytes 10000000 | tf_op jit(solution)/shard_map/attend_forward/pallas_call | solution.py:174
  45.8 52.6 %mlp.1 = (f32[1024,768]{1,0:T(8,128)}, f32[1024,768]{1,0:T(8,128)}, bf16[1024,768]{1,0:T(8,128)(2,1)}, f32[8,768]{1,0:T(8,128)}, f32[8,3072]{1,0:T(8,128)}, /*in...) custom-call(f32[1024,768]{1,0:T(8,128)} %bitcast.26, ...), custom_call_target="tpu_custom_call" | custom-call | flops 40000000000 | bytes 40000000 | tf_op jit(solution)/shard_map/mlp/pallas_call | solution.py:556
  98.3 3.6 %collective-permute-start.3 = (bf16[2,2,192,384]{3,2,1,0:T(8,128)(2,1)}, bf16[2,2,192,384]{3,2,1,0:T(8,128)(2,1)S(1)}, u32[]{:S(2)}, u32[]{:S(2)}) collective-permute-start(bf16[2,2,192,384]{3,2,1,0:T(8,128)(2,1)} %get-tuple-element.72), channel_id=1, source_target_pairs={{0,16},{2,18},{4,20},{6,22},{8,24},{10,26},{12,28},{14,30},{16,0},... | collective-permute-start | bytes 1769480 | tf_op jit(solution)/shard_map/ppermute | solution.py:1199
  101.9 1.4 collective-permute-start.4
  103.3 1.2 collective-permute-start
  104.5 0.4 collective-permute-start.1
  104.9 1.8 collective-permute-start.2
  106.8 0.0 copy-start
  106.8 0.0 copy-start.1
  106.8 0.0 copy-start.2
  106.8 0.0 copy-start.3
  106.8 48.2 %attend_backward.1 = (bf16[1024,768]{1,0:T(8,128)(2,1)}, bf16[768,1024]{1,0:T(8,128)(2,1)}, bf16[768,1024]{1,0:T(8,128)(2,1)}, bf16[768,1024]{1,0:T(8,128)(2,1)}...) custom-call(s32[1]{0:T(128)} %bitcast.band_ref, bf16[12,1024,128]{2,1,0:T(8,128)(2,1)} %get-tuple-element.54.qm, ...), custom_call_target="tpu_custom_call" | custom-call | flops 44999999488 | bytes 20000000 | tf_op jit(solution)/shard_map/attend_backward/pallas_call | solution.py:295
  155.0 0.0 collective-permute-done.3.c2_hbm
  155.0 0.0 copy-start.7
  155.0 0.0 collective-permute-done.4.c3_hbm
  155.0 0.0 copy-start.8
  155.0 0.0 collective-permute-done.px_hbm
  155.0 0.0 copy-start.4
  155.0 0.0 collective-permute-done.1.py_hbm
  155.0 0.0 copy-start.5
  155.1 0.0 collective-permute-done.2.pd_hbm
  155.1 0.0 copy-start.6
  155.1 0.7 copy-done.7
  155.8 0.2 copy-done.8
  156.0 0.2 copy-done.4
  156.2 0.3 copy-done.5
  156.5 0.2 copy-done.6
  156.7 0.0 copy-done
  156.7 0.0 copy-done.1
  156.7 0.0 copy-done.2
  156.7 0.0 copy-done.3
  156.7 45.1 %finish.1 = (f32[1024,768]{1,0:T(8,128)}, f32[192,384]{1,0:T(8,128)S(1)}, f32[48,3072]{1,0:T(8,128)S(1)}, f32[8,48]{1,0:T(8,128)S(1)}, f32[1,192]{1,0:T(1,128)S(1)}) custom-call(bf16[1024,768]{1,0:T(8,128)(2,1)} %get-tuple-element.59.dq_hbm, bf16[768,1024]{1,0:T(8,128)(2,1)} %get-tuple-element.60.dko_hbm, bf16[768,1024]{1,0:T(8,128)(2,1)} %get-tuple-element.61.dkf_hbm, ...), custom_call_target="tpu_custom_call" | custom-call | flops 20000000000 | bytes 40000000 | tf_op jit(solution)/shard_map/finish/pallas_call | solution.py:1030
  201.8 0.6 slice.38
  202.5 0.7 slice.35
  203.2 0.7 slice.42
  203.9 0.5 slice_bitcast_fusion
  204.4 3.8 %copy.34 = f32[1,1024,768]{2,1,0:T(8,128)} copy(f32[1,1024,768]{2,1,0:T(8,128)} %bitcast.23) | data formatting | bytes 6291456
  208.2 0.6 copy.35
  208.7 0.7 copy.36
Async XLA Ops:
  98.3 56.7 %collective-permute-start.3 = (bf16[2,2,192,384]{3,2,1,0:T(8,128)(2,1)}, bf16[2,2,192,384]{3,2,1,0:T(8,128)(2,1)S(1)}, u32[]{:S(2)}, u32[]{:S(2)}) collective-permute-start(bf16[2,2,192,384]{3,2,1,0:T(8,128)(2,1)} %get-tuple-element.72), channel_id=1, source_target_pairs={{0,16},{2,18},{4,20},{6,22},{8,24},{10,26},{12,28},{14,30},{16,0},... | collective-permute-start | bytes 1769480 | tf_op jit(solution)/shard_map/ppermute | solution.py:1199
  101.9 53.1 %collective-permute-start.4 = (bf16[2,2,192,384]{3,2,1,0:T(8,128)(2,1)}, bf16[2,2,192,384]{3,2,1,0:T(8,128)(2,1)S(1)}, u32[]{:S(2)}, u32[]{:S(2)}) collective-permute-start(bf16[2,2,192,384]{3,2,1,0:T(8,128)(2,1)} %get-tuple-element.73), channel_id=1, source_target_pairs={{0,24},{2,26},{4,28},{6,30},{8,16},{10,18},{12,20},{14,22},{16,8},... | collective-permute-start | bytes 1769480 | tf_op jit(solution)/shard_map/ppermute | solution.py:1199
  103.3 51.7 %collective-permute-start = (bf16[4,240,384]{2,1,0:T(8,128)(2,1)}, bf16[4,240,384]{2,1,0:T(8,128)(2,1)S(1)}, u32[]{:S(2)}, u32[]{:S(2)}) collective-permute-start(bf16[4,240,384]{2,1,0:T(8,128)(2,1)} %get-tuple-element.69), channel_id=1, source_target_pairs={{0,2},{2,0},{4,6},{6,4},{8,10},{10,8},{12,14},{14,12},{16,18},{18,... | collective-permute-start | bytes 2211848 | tf_op jit(solution)/shard_map/ppermute | solution.py:1199
  104.5 50.6 %collective-permute-start.1 = (bf16[4,240,384]{2,1,0:T(8,128)(2,1)}, bf16[4,240,384]{2,1,0:T(8,128)(2,1)S(1)}, u32[]{:S(2)}, u32[]{:S(2)}) collective-permute-start(bf16[4,240,384]{2,1,0:T(8,128)(2,1)} %get-tuple-element.70), channel_id=1, source_target_pairs={{0,4},{2,6},{4,0},{6,2},{8,12},{10,14},{12,8},{14,10},{16,20},{18,... | collective-permute-start | bytes 2211848 | tf_op jit(solution)/shard_map/ppermute | solution.py:1199
  104.9 50.2 %collective-permute-start.2 = (bf16[4,240,384]{2,1,0:T(8,128)(2,1)}, bf16[4,240,384]{2,1,0:T(8,128)(2,1)S(1)}, u32[]{:S(2)}, u32[]{:S(2)}) collective-permute-start(bf16[4,240,384]{2,1,0:T(8,128)(2,1)} %get-tuple-element.71), channel_id=1, source_target_pairs={{0,6},{2,4},{4,2},{6,0},{8,14},{10,12},{12,10},{14,8},{16,22},{18,... | collective-permute-start | bytes 2211848 | tf_op jit(solution)/shard_map/ppermute | solution.py:1199
  106.8 50.0 %copy-start = (f32[768]{0:T(1024)S(1)}, f32[768]{0:T(1024)}, u32[]{:S(2)}) copy-start(f32[768]{0:T(1024)} %gain.5) | copy-start | bytes 9220
  106.8 50.0 %copy-start.1 = (bf16[2,2,192,384]{3,2,1,0:T(8,128)(2,1)S(1)}, bf16[2,2,192,384]{3,2,1,0:T(8,128)(2,1)}, u32[]{:S(2)}) copy-start(bf16[2,2,192,384]{3,2,1,0:T(8,128)(2,1)} %get-tuple-element.67.ck_hbm) | copy-start | bytes 1769476
  106.8 50.0 %copy-start.2 = (f32[8,3072]{1,0:T(8,128)S(1)}, f32[8,3072]{1,0:T(8,128)}, u32[]{:S(2)}) copy-start(f32[8,3072]{1,0:T(8,128)} %get-tuple-element.75.usums) | copy-start | bytes 294916
  106.8 50.0 %copy-start.3 = (f32[8,768]{1,0:T(8,128)S(1)}, f32[8,768]{1,0:T(8,128)}, u32[]{:S(2)}) copy-start(f32[8,768]{1,0:T(8,128)} %get-tuple-element.74.msums) | copy-start | bytes 73732
  155.0 0.8 copy-start.7
  155.0 1.0 copy-start.8
  155.0 1.2 copy-start.4
  155.0 1.4 copy-start.5
  155.1 1.7 copy-start.6

commit v8 on v7

--- a/solution.py
+++ b/solution.py
@@ -352,7 +352,12 @@
 def mlp_kernel(sorted_out, blocks, rows, slices, tok_ref, att_ref, cot_ref, wproj, wup, wdown, pbias, gain, shift, ubias, dbias,
                out_ref, rgrad_ref, agrad_ref, sums_ref, usums_ref, *rest):
     outs, scratch = rest[: 8 if sorted_out else 3], rest[8 if sorted_out else 3 :]
-    hid, ugr, n2s, bgs, ags, ats, d_own, d_far, d_in, u_in, p_own, p_far, p_in, send_sem, recv_sem = scratch
+    hid, ugr, n2s, bgs, ags, ats, d_own, d_far, d_in, u_in, p_own, p_far, p_in, send_sem, recv_sem, *held = scratch
+    stores = []
+    if sorted_out:
+        store_sem = held.pop()
+        stores = [pltpu.make_async_copy(held[q], outs[q], store_sem.at[q]) for q in range(4)]
+        outs = (*held, *outs[4:])
     i = pl.program_id(0)
     me, band = lax.axis_index("dp"), lax.axis_index("band")
     other = (me, 1 - band)
@@ -378,7 +383,10 @@
     def _():
         barrier = pltpu.get_barrier_semaphore()
         pl.semaphore_signal(barrier, inc=1, device_id=other, device_id_type=MESH)
-        pl.semaphore_wait(barrier, 1)
+
+    @pl.when(i == blocks)
+    def _():
+        pl.semaphore_wait(pltpu.get_barrier_semaphore(), 1)
 
     @pl.when(i < blocks)
     def _():
@@ -521,12 +529,16 @@
 
     @pl.when(i == middle + slices)
     def _():
+        for store in stores:
+            store.start()
         up_arrived(per_half - 1)
         for j in range(slices):
             d_copy(j).wait_send()
         for c in range(per_half):
             u_copy(c).wait_send()
         p_copy().wait_send()
+        for store in stores:
+            store.wait()
 
 
 def mlp(size, tokens, attended, cotangent, w_proj, w_up, w_down, proj_bias, gain, shift, up_bias, down_bias, rows=256):
@@ -552,13 +564,15 @@
         pieces = [shape((ff, half), bf16), shape((width, ff // 2), bf16), shape((width, half), bf16)]
     kept = [shape((8, width), f32), shape((8, ff), f32)] + pieces
     low = lambda *s: pltpu.VMEM(s, bf16)
+    direct = pieces[:4] if sorted_out else []
+    held = [low(*a.shape) for a in direct] + [pltpu.SemaphoreType.DMA((4,))] * sorted_out
     copies = slices + per_half + 1
     return pl.pallas_call(
         functools.partial(mlp_kernel, sorted_out, blocks, rows, slices),
         out_shape=[shape((count, width), f32), shape((count, width), f32), shape((count, width), bf16)] + kept,
         grid=(blocks + 2 * slices + 1,),
         in_specs=[block, block, block] + [full(a) for a in (w_proj, w_up, w_down, *vectors)],
-        out_specs=[block, block, block] + [full(a) for a in kept],
+        out_specs=[block, block, block] + [pl.BlockSpec(memory_space=pl.ANY) if a in direct else full(a) for a in kept],
         scratch_shapes=[
             low(count, ff),
             low(count, ff),
@@ -568,6 +582,7 @@
             *([low(width, half)] * 3),
             pltpu.SemaphoreType.DMA((copies,)),
             pltpu.SemaphoreType.DMA((copies,)),
+            *held,
         ],
         compiler_params=pltpu.CompilerParams(vmem_limit_bytes=62 * MIB, collective_id=1, has_side_effects=True),
         cost_estimate=pl.CostEstimate(flops=40 * 10**9, bytes_accessed=40 * 10**6, transcendentals=0),

time: 210 us -> 209 us (level)
  no operation moved by 1% of the time
where the time goes in v8:
time: 209 us
  Pallas kernels  190 us (91%)
  local copies, waits for them, and re-layouts  9.33 us (4%)
  starting transfers between devices  8.94 us (4%)
    pallas_call x1, Pallas kernels, mlp(): pl.pallas_call(functools.partial(mlp_kernel, sorted_out, blocks, rows, sl...  52.5 us
    pallas_call x1, Pallas kernels, attend_backward(): pl.pallas_call(functools.partial(attend_bwd_kernel, fills, steps, BQ, BK)...  48.2 us
    pallas_call x1, Pallas kernels, finish(): pl.pallas_call(finish_kernel, out_shape=(shape((rows, width), f32), shape...  44.3 us
    pallas_call x1, Pallas kernels, attend_forward(): pl.pallas_call(functools.partial(attend_fwd_kernel, fills, BQ, BK), out_s...  34.1 us
    pallas_call x1, Pallas kernels, project_qkv(): pl.pallas_call(functools.partial(qkv_kernel, steps), out_shape=(low,) * 6...  11 us
    ppermute x5, starting transfers between devices, local(): lax.ppermute(a, 'dp', turn)  8.94 us
    unnamed x21, local copies, waits for them, and re-layouts  6.71 us
  transfers between devices with their start and end apart: 5, of which 0 were waited for; matrix products, arithmetic and copies ran while one was open for 0% of the time, Pallas kernels for 23%

profile of v8, /device:TPU:0, one launch (start us, length us, event | category | flops | bytes accessed | tf_op | source)
XLA Modules:
  0.0 209.2 jit_solution(16933783118442196276)
XLA Ops:
  0.6 11.0 %project_qkv.1 = (bf16[1024,768]{1,0:T(8,128)(2,1)}, bf16[1024,768]{1,0:T(8,128)(2,1)}, bf16[1024,768]{1,0:T(8,128)(2,1)}, bf16[1024,768]{1,0:T(8,128)(2,1)}, bf...) custom-call(f32[1024,768]{1,0:T(8,128)} %bitcast.25, s32[1,1024]{1,0:T(1,128)} %seg_own.3, ...), custom_call_target="tpu_custom_call" | custom-call | flops 4000000000 | bytes 13000000 | tf_op jit(solution)/shard_map/project_qkv/pallas_call | solution.py:665
  11.6 34.1 %attend_forward.1 = (bf16[1024,768]{1,0:T(8,128)(2,1)}, bf16[12,1024,128]{2,1,0:T(8,128)(2,1)}) custom-call(s32[1]{0:T(128)} %bitcast.band_ref, bf16[1024,768]{1,0:T(8,128)(2,1)} %get-tuple-element.48.q_ref, bf16[1024,768]{1,0:T(8,128)(2,1)} %get-tuple-element.49.k_own, bf16[1024,768]{1,0:T(8,128)(2,1)} %get-tuple-element.50.k_far, ...), custom_call_target="tpu_custom_call" | custom-call | flops 30000001024 | bytes 10000000 | tf_op jit(solution)/shard_map/attend_forward/pallas_call | solution.py:174
  45.8 52.5 %mlp.1 = (f32[1024,768]{1,0:T(8,128)}, f32[1024,768]{1,0:T(8,128)}, bf16[1024,768]{1,0:T(8,128)(2,1)}, f32[8,768]{1,0:T(8,128)}, f32[8,3072]{1,0:T(8,128)}, /*in...) custom-call(f32[1024,768]{1,0:T(8,128)} %bitcast.26, ...), custom_call_target="tpu_custom_call" | custom-call | flops 40000000000 | bytes 40000000 | tf_op jit(solution)/shard_map/mlp/pallas_call | solution.py:570
  98.3 4.1 %collective-permute-start.3 = (bf16[2,2,192,384]{3,2,1,0:T(8,128)(2,1)}, bf16[2,2,192,384]{3,2,1,0:T(8,128)(2,1)S(1)}, u32[]{:S(2)}, u32[]{:S(2)}) collective-permute-start(bf16[2,2,192,384]{3,2,1,0:T(8,128)(2,1)} %get-tuple-element.72), channel_id=1, source_target_pairs={{0,16},{2,18},{4,20},{6,22},{8,24},{10,26},{12,28},{14,30},{16,0},... | collective-permute-start | bytes 1769480 | tf_op jit(solution)/shard_map/ppermute | solution.py:1214
  102.4 1.4 collective-permute-start.4
  103.7 1.5 collective-permute-start
  105.2 1.5 collective-permute-start.1
  106.7 0.5 collective-permute-start.2
  107.2 0.0 copy-start
  107.2 0.0 copy-start.1
  107.2 0.0 copy-start.2
  107.2 0.0 copy-start.3
  107.2 48.2 %attend_backward.1 = (bf16[1024,768]{1,0:T(8,128)(2,1)}, bf16[768,1024]{1,0:T(8,128)(2,1)}, bf16[768,1024]{1,0:T(8,128)(2,1)}, bf16[768,1024]{1,0:T(8,128)(2,1)}...) custom-call(s32[1]{0:T(128)} %bitcast.band_ref, bf16[12,1024,128]{2,1,0:T(8,128)(2,1)} %get-tuple-element.54.qm, ...), custom_call_target="tpu_custom_call" | custom-call | flops 44999999488 | bytes 20000000 | tf_op jit(solution)/shard_map/attend_backward/pallas_call | solution.py:295
  155.4 0.0 collective-permute-done.3.c2_hbm
  155.5 0.0 copy-start.7
  155.5 0.0 collective-permute-done.4.c3_hbm
  155.5 0.0 copy-start.8
  155.5 0.0 collective-permute-done.px_hbm
  155.5 0.0 copy-start.4
  155.5 0.0 collective-permute-done.1.py_hbm
  155.5 0.0 copy-start.5
  155.5 0.0 collective-permute-done.2.pd_hbm
  155.5 0.0 copy-start.6
  155.5 0.7 copy-done.7
  156.3 0.2 copy-done.8
  156.5 0.2 copy-done.4
  156.7 0.3 copy-done.5
  157.0 0.2 copy-done.6
  157.2 0.0 copy-done
  157.2 0.0 copy-done.1
  157.2 0.0 copy-done.2
  157.2 0.0 copy-done.3
  157.2 44.3 %finish.1 = (f32[1024,768]{1,0:T(8,128)}, f32[192,384]{1,0:T(8,128)S(1)}, f32[48,3072]{1,0:T(8,128)S(1)}, f32[8,48]{1,0:T(8,128)S(1)}, f32[1,192]{1,0:T(1,128)S(1)}) custom-call(bf16[1024,768]{1,0:T(8,128)(2,1)} %get-tuple-element.59.dq_hbm, bf16[768,1024]{1,0:T(8,128)(2,1)} %get-tuple-element.60.dko_hbm, bf16[768,1024]{1,0:T(8,128)(2,1)} %get-tuple-element.61.dkf_hbm, ...), custom_call_target="tpu_custom_call" | custom-call | flops 20000000000 | bytes 40000000 | tf_op jit(solution)/shard_map/finish/pallas_call | solution.py:1045
  201.6 0.6 slice.38
  202.2 0.7 slice.35
  202.9 0.7 slice.42
  203.6 0.5 slice_bitcast_fusion
  204.2 3.8 %copy.34 = f32[1,1024,768]{2,1,0:T(8,128)} copy(f32[1,1024,768]{2,1,0:T(8,128)} %bitcast.23) | data formatting | bytes 6291456
  207.9 0.6 copy.35
  208.5 0.7 copy.36
Async XLA Ops:
  98.3 57.2 %collective-permute-start.3 = (bf16[2,2,192,384]{3,2,1,0:T(8,128)(2,1)}, bf16[2,2,192,384]{3,2,1,0:T(8,128)(2,1)S(1)}, u32[]{:S(2)}, u32[]{:S(2)}) collective-permute-start(bf16[2,2,192,384]{3,2,1,0:T(8,128)(2,1)} %get-tuple-element.72), channel_id=1, source_target_pairs={{0,16},{2,18},{4,20},{6,22},{8,24},{10,26},{12,28},{14,30},{16,0},... | collective-permute-start | bytes 1769480 | tf_op jit(solution)/shard_map/ppermute | solution.py:1214
  102.4 53.1 %collective-permute-start.4 = (bf16[2,2,192,384]{3,2,1,0:T(8,128)(2,1)}, bf16[2,2,192,384]{3,2,1,0:T(8,128)(2,1)S(1)}, u32[]{:S(2)}, u32[]{:S(2)}) collective-permute-start(bf16[2,2,192,384]{3,2,1,0:T(8,128)(2,1)} %get-tuple-element.73), channel_id=1, source_target_pairs={{0,24},{2,26},{4,28},{6,30},{8,16},{10,18},{12,20},{14,22},{16,8},... | collective-permute-start | bytes 1769480 | tf_op jit(solution)/shard_map/ppermute | solution.py:1214
  103.7 51.8 %collective-permute-start = (bf16[4,240,384]{2,1,0:T(8,128)(2,1)}, bf16[4,240,384]{2,1,0:T(8,128)(2,1)S(1)}, u32[]{:S(2)}, u32[]{:S(2)}) collective-permute-start(bf16[4,240,384]{2,1,0:T(8,128)(2,1)} %get-tuple-element.69), channel_id=1, source_target_pairs={{0,2},{2,0},{4,6},{6,4},{8,10},{10,8},{12,14},{14,12},{16,18},{18,... | collective-permute-start | bytes 2211848 | tf_op jit(solution)/shard_map/ppermute | solution.py:1214
  105.2 50.3 %collective-permute-start.1 = (bf16[4,240,384]{2,1,0:T(8,128)(2,1)}, bf16[4,240,384]{2,1,0:T(8,128)(2,1)S(1)}, u32[]{:S(2)}, u32[]{:S(2)}) collective-permute-start(bf16[4,240,384]{2,1,0:T(8,128)(2,1)} %get-tuple-element.70), channel_id=1, source_target_pairs={{0,4},{2,6},{4,0},{6,2},{8,12},{10,14},{12,8},{14,10},{16,20},{18,... | collective-permute-start | bytes 2211848 | tf_op jit(solution)/shard_map/ppermute | solution.py:1214
  106.7 48.8 %collective-permute-start.2 = (bf16[4,240,384]{2,1,0:T(8,128)(2,1)}, bf16[4,240,384]{2,1,0:T(8,128)(2,1)S(1)}, u32[]{:S(2)}, u32[]{:S(2)}) collective-permute-start(bf16[4,240,384]{2,1,0:T(8,128)(2,1)} %get-tuple-element.71), channel_id=1, source_target_pairs={{0,6},{2,4},{4,2},{6,0},{8,14},{10,12},{12,10},{14,8},{16,22},{18,... | collective-permute-start | bytes 2211848 | tf_op jit(solution)/shard_map/ppermute | solution.py:1214
  107.2 50.0 %copy-start = (f32[768]{0:T(1024)S(1)}, f32[768]{0:T(1024)}, u32[]{:S(2)}) copy-start(f32[768]{0:T(1024)} %gain.5) | copy-start | bytes 9220
  107.2 50.0 %copy-start.1 = (bf16[2,2,192,384]{3,2,1,0:T(8,128)(2,1)S(1)}, bf16[2,2,192,384]{3,2,1,0:T(8,128)(2,1)}, u32[]{:S(2)}) copy-start(bf16[2,2,192,384]{3,2,1,0:T(8,128)(2,1)} %get-tuple-element.67.ck_hbm) | copy-start | bytes 1769476
  107.2 50.0 %copy-start.2 = (f32[8,3072]{1,0:T(8,128)S(1)}, f32[8,3072]{1,0:T(8,128)}, u32[]{:S(2)}) copy-start(f32[8,3072]{1,0:T(8,128)} %get-tuple-element.75.usums) | copy-start | bytes 294916
  107.2 50.0 %copy-start.3 = (f32[8,768]{1,0:T(8,128)S(1)}, f32[8,768]{1,0:T(8,128)}, u32[]{:S(2)}) copy-start(f32[8,768]{1,0:T(8,128)} %get-tuple-element.74.msums) | copy-start | bytes 73732
  155.5 0.8 copy-start.7
  155.5 1.0 copy-start.8
  155.5 1.2 copy-start.4
  155.5 1.4 copy-start.5
  155.5 1.7 copy-start.6
